TPU v7x, 32 devices: a whole 2x2x4 slice. The times are simulated.
32 devices in a mesh: rows: 16 (over z, x, core), seq: 2 (over y).
Axes of the slice: x: 2, y: 2, z: 4, core: 2. Of those that a mesh axis runs over, the one named last changes fastest.
Arguments:
- inputs: bfloat16 [64, 1024, 768], P('rows', 'seq'), may hold values from -6 to 6
- split_point: int32 [64], P('rows'), may hold values from 256 to 767
- keep_mask: int32 [64, 1024], P('rows', 'seq'), may hold values from 0 to 1, as said below
- norm_gain: float32 [768], replicated, may hold values from 0.5 to 1.5
- proj_in: bfloat16 [768, 2304], replicated, may hold values from -0.21875 to 0.21875
- short_filter: float32 [3, 1536], replicated, may hold values from -3 to 3
- cond_filter: float32 [3, 768], replicated, may hold values from -0.109375 to 0.109375
- spec_slope: float32 [768], replicated, may hold values from -2 to 2
- spec_shift: float32 [768], replicated, may hold values from -3 to 3
- skip_gain: float32 [768], replicated, may hold values from -2.5 to 2.5
- proj_out: bfloat16 [768, 768], replicated, may hold values from -0.21875 to 0.21875
- ffn_gain: float32 [768], replicated, may hold values from 0.5 to 1.5
- ffn_in: bfloat16 [768, 6144], replicated, may hold values from -0.21875 to 0.21875
- ffn_out: bfloat16 [3072, 768], replicated, may hold values from -0.109375 to 0.109375
- out_grad: bfloat16 [64, 1024, 768], P('rows', 'seq'), may hold values from -6 to 6
Outputs:
- output: bfloat16 [64, 1024, 768], P('rows', 'seq')
- input_grad: float32 [64, 1024, 768], P('rows', 'seq')
- norm_gain_grad: float32 [768], replicated
- proj_in_grad: float32 [768, 2304], P('rows')
- short_filter_grad: float32 [3, 1536], replicated
- cond_filter_grad: float32 [3, 768], replicated
- spec_slope_grad: float32 [768], replicated
- spec_shift_grad: float32 [768], replicated
- skip_gain_grad: float32 [768], replicated
- proj_out_grad: float32 [768, 768], P('rows')
- ffn_gain_grad: float32 [768], replicated
- ffn_in_grad: float32 [768, 6144], P('rows')
- ffn_out_grad: float32 [3072, 768], P(None, 'rows')
Inputs may be any that keep to these rules, and one draw needn't show every extreme that they name: `keep_mask`: each row keeps its first positions, at least 768 and at most 1023 of them, and masks the rest.
All inputs are finite; a program needn't handle non-finite values.
Results may differ from a plain program's by a relative error of at most 0.019.
Values may be sent and summed in bfloat16 or wider, within the bound.
A program may use at most 512 MiB of HBM per device.

v0:
```python
import math

import jax
import jax.numpy as jnp
from jax import lax
from jax.sharding import PartitionSpec as P

EPSILON = 1e-05
PRECISE = lax.Precision.HIGH


def passed_along(value, axis, steps):
    count = lax.axis_size(axis)
    leading, last = (max(0, -steps), min(count, count - steps))
    return lax.ppermute(value, axis, [(source, source + steps) for source in range(leading, last)])


def layer_norm(values, scaling):
    center = values - jnp.mean(values, axis=-1, keepdims=True)
    spread = jnp.mean(center * center, axis=-1, keepdims=True)
    return center * lax.rsqrt(spread + EPSILON) * scaling


def conv_three(extended, weights, same_one, same_two):
    length = extended.shape[1] - 2
    return (
        weights[0] * extended[:, 2:]
        + weights[1] * extended[:, 1 : length + 1] * same_one
        + weights[2] * extended[:, :length] * same_two
    )


def dft_tables(seq_length):
    table_shape = (seq_length + 1, seq_length)
    product = lax.broadcasted_iota(jnp.int32, table_shape, 0) * lax.broadcasted_iota(
        jnp.int32, table_shape, 1
    )
    angles = (product % (2 * seq_length)).astype(jnp.float32) * (math.pi / seq_length)
    freq = lax.broadcasted_iota(jnp.int32, (seq_length + 1, 1), 0)
    edge = jnp.logical_or(freq == 0, freq == seq_length)
    weights = jnp.where(edge, 1.0, 2.0).astype(jnp.float32) / (2.0 * seq_length)
    return (jnp.cos(angles), jnp.sin(angles), weights)


def analyze(values, conds, cos_table, sin_table):
    value_real = jnp.einsum("ft,ktd->kfd", cos_table, values, precision=PRECISE)
    value_imag = -jnp.einsum("ft,ktd->kfd", sin_table, values, precision=PRECISE)
    cond_real = jnp.einsum("ft,ktd->kfd", cos_table, conds, precision=PRECISE)
    cond_imag = -jnp.einsum("ft,ktd->kfd", sin_table, conds, precision=PRECISE)
    return (value_real, value_imag, cond_real, cond_imag)


def synth(
    value_real,
    value_imag,
    cond_real,
    cond_imag,
    values,
    slopes,
    shifts,
    skip_gains,
    cos_table,
    sin_table,
    freq_weights,
):
    factor = jax.nn.sigmoid(slopes * (cond_real * cond_real + cond_imag * cond_imag) + shifts)
    filter_real = cond_real * factor
    filter_imag = cond_imag * factor
    prod_real = (value_real * filter_real - value_imag * filter_imag) * freq_weights
    prod_imag = (value_real * filter_imag + value_imag * filter_real) * freq_weights
    mixed_out = jnp.einsum("ft,kfd->ktd", cos_table, prod_real, precision=PRECISE) - jnp.einsum(
        "ft,kfd->ktd", sin_table, prod_imag, precision=PRECISE
    )
    return mixed_out + skip_gains * values


def times_transpose(left, right):
    return lax.dot_general(
        left, right, (((1,), (1,)), ((), ())), preferred_element_type=jnp.float32
    )


def transpose_times(left, right):
    return lax.dot_general(
        left, right, (((0,), (0,)), ((), ())), preferred_element_type=jnp.float32
    )


def per_device(
    inputs,
    split_point,
    keep_mask,
    norm_gain,
    proj_in,
    short_filter,
    cond_filter,
    spec_slope,
    spec_shift,
    skip_gain,
    proj_out,
    ffn_gain,
    ffn_in,
    ffn_out,
    out_grad,
):
    local_rows, local_len, model_width = inputs.shape
    hidden_width = ffn_out.shape[0]
    seq_count = lax.axis_size("seq")
    seq_index = lax.axis_index("seq")
    full_len = local_len * seq_count
    chan_width = model_width // seq_count
    token_count = local_rows * local_len
    positions = seq_index * local_len + lax.broadcasted_iota(jnp.int32, (local_rows, local_len), 1)
    splits = split_point[:, None]
    segment = positions >= splits
    same_one = (segment == (positions - 1 >= splits)).astype(jnp.float32)[:, :, None]
    same_two = (segment == (positions - 2 >= splits)).astype(jnp.float32)[:, :, None]
    keep_float = keep_mask.astype(jnp.float32)[:, :, None]
    flat_in = inputs.reshape(token_count, model_width).astype(jnp.float32)
    normed_one, norm_one_back = jax.vjp(layer_norm, flat_in, norm_gain)
    first_act = normed_one.astype(jnp.bfloat16)
    projected = jnp.dot(first_act, proj_in, preferred_element_type=jnp.float32).astype(jnp.bfloat16)
    proj_rows = projected.reshape(local_rows, local_len, 3 * model_width)
    edge_values = passed_along(proj_rows[:, local_len - 2 :, :], "seq", 1)
    extended = jnp.concatenate([edge_values, proj_rows], axis=1).astype(jnp.float32)

    def mixer_local(ext_values, short_weights, cond_weights):
        query_value = jnp.concatenate(
            [ext_values[:, :, :model_width], ext_values[:, :, 2 * model_width :]], axis=2
        )
        conv_both = conv_three(query_value, short_weights, same_one, same_two)
        cond_conv = conv_three(
            ext_values[:, :, model_width : 2 * model_width], cond_weights, same_one, same_two
        )
        return (
            conv_both[:, :, :model_width],
            conv_both[:, :, model_width:] * keep_float,
            cond_conv * keep_float,
        )

    (query_conv, value_masked, cond_masked), mixer_back = jax.vjp(
        mixer_local, extended, short_filter, cond_filter
    )
    value_low = value_masked.astype(jnp.bfloat16)
    cond_low = cond_masked.astype(jnp.bfloat16)
    slope_part = lax.dynamic_slice_in_dim(spec_slope, seq_index * chan_width, chan_width)
    shift_part = lax.dynamic_slice_in_dim(spec_shift, seq_index * chan_width, chan_width)
    skip_part = lax.dynamic_slice_in_dim(skip_gain, seq_index * chan_width, chan_width)
    cos_table, sin_table, freq_weights = dft_tables(full_len)

    def synth_local(
        value_real, value_imag, cond_real, cond_imag, values, slopes, shifts, skip_gains
    ):
        return synth(
            value_real,
            value_imag,
            cond_real,
            cond_imag,
            values,
            slopes,
            shifts,
            skip_gains,
            cos_table,
            sin_table,
            freq_weights,
        )

    value_chan = lax.all_to_all(value_low, "seq", split_axis=2, concat_axis=1, tiled=True)
    cond_chan = lax.all_to_all(cond_low, "seq", split_axis=2, concat_axis=1, tiled=True)
    value_float = value_chan.astype(jnp.float32)
    spectra = analyze(value_float, cond_chan.astype(jnp.float32), cos_table, sin_table)
    mixed_chan = synth_local(
        spectra[0],
        spectra[1],
        spectra[2],
        spectra[3],
        value_float,
        slope_part,
        shift_part,
        skip_part,
    ).astype(jnp.bfloat16)
    mixed_home = lax.all_to_all(mixed_chan, "seq", split_axis=1, concat_axis=2, tiled=True)
    mixed_float = mixed_home.astype(jnp.float32)
    gated = (query_conv * mixed_float).astype(jnp.bfloat16).reshape(token_count, model_width)
    branch = jnp.dot(gated, proj_out, preferred_element_type=jnp.float32)
    resid = flat_in + branch
    normed_two, norm_two_back = jax.vjp(layer_norm, resid, ffn_gain)
    second_act = normed_two.astype(jnp.bfloat16)
    gate_up = jnp.dot(second_act, ffn_in, preferred_element_type=jnp.float32)

    def glu_local(both_parts):
        return (
            jax.nn.gelu(both_parts[:, :hidden_width], approximate=False)
            * both_parts[:, hidden_width:]
        )

    hidden, glu_back = jax.vjp(glu_local, gate_up)
    hidden_low = hidden.astype(jnp.bfloat16)
    result = resid + jnp.dot(hidden_low, ffn_out, preferred_element_type=jnp.float32)
    output = result.astype(jnp.bfloat16).reshape(local_rows, local_len, model_width)
    flat_grad = out_grad.reshape(token_count, model_width)
    hidden_grad = times_transpose(flat_grad, ffn_out)
    (gate_up_grad,) = glu_back(hidden_grad)
    gate_up_low = gate_up_grad.astype(jnp.bfloat16)
    second_grad = times_transpose(gate_up_low, ffn_in)
    resid_part, ffn_gain_part = norm_two_back(second_grad)
    resid_grad = flat_grad.astype(jnp.float32) + resid_part
    branch_low = resid_grad.astype(jnp.bfloat16)
    gated_grad = times_transpose(branch_low, proj_out).reshape(local_rows, local_len, model_width)
    query_grad = gated_grad * mixed_float
    mixed_grad = (gated_grad * query_conv).astype(jnp.bfloat16)
    grad_chan = lax.all_to_all(mixed_grad, "seq", split_axis=2, concat_axis=1, tiled=True)
    grad_float = grad_chan.astype(jnp.float32)
    item_count = grad_chan.shape[0]
    slope_items = jnp.broadcast_to(slope_part, (item_count, 1, chan_width))
    shift_items = jnp.broadcast_to(shift_part, (item_count, 1, chan_width))
    skip_items = jnp.broadcast_to(skip_part, (item_count, 1, chan_width))
    value_float = value_chan.astype(jnp.float32)

    def spectral(values, conds, slopes, shifts, skip_gains):
        spectra = analyze(values, conds, cos_table, sin_table)
        return synth_local(
            spectra[0], spectra[1], spectra[2], spectra[3], values, slopes, shifts, skip_gains
        )

    unused, pull = jax.vjp(
        spectral, value_float, cond_chan.astype(jnp.float32), slope_items, shift_items, skip_items
    )
    value_back, cond_back, slope_rows, shift_rows, skip_rows = pull(grad_float)
    value_grad, cond_grad = (
        lax.all_to_all(
            value_back.astype(jnp.bfloat16), "seq", split_axis=1, concat_axis=2, tiled=True
        ),
        lax.all_to_all(
            cond_back.astype(jnp.bfloat16), "seq", split_axis=1, concat_axis=2, tiled=True
        ),
    )
    start_chan = (seq_index * chan_width,)
    empty_width = jnp.zeros((model_width,), jnp.float32)
    slope_full = lax.dynamic_update_slice(empty_width, jnp.sum(slope_rows, axis=(0, 1)), start_chan)
    shift_full = lax.dynamic_update_slice(empty_width, jnp.sum(shift_rows, axis=(0, 1)), start_chan)
    skip_full = lax.dynamic_update_slice(empty_width, jnp.sum(skip_rows, axis=(0, 1)), start_chan)
    ext_grad, short_grad, cond_weight_grad = mixer_back(
        (query_grad, value_grad.astype(jnp.float32), cond_grad.astype(jnp.float32))
    )
    incoming = passed_along(ext_grad[:, :2, :].astype(jnp.bfloat16), "seq", -1).astype(jnp.float32)
    proj_grad = ext_grad[:, 2:, :] + jnp.pad(incoming, ((0, 0), (local_len - 2, 0), (0, 0)))
    proj_low = proj_grad.astype(jnp.bfloat16).reshape(token_count, 3 * model_width)
    first_grad = times_transpose(proj_low, proj_in)
    input_part, norm_gain_part = norm_one_back(first_grad)
    input_grad = (resid_grad + input_part).reshape(local_rows, local_len, model_width)
    share = lax.psum_scatter(
        jnp.concatenate(
            [
                transpose_times(first_act, proj_low),
                transpose_times(gated, branch_low),
                transpose_times(second_act, gate_up_low),
                transpose_times(flat_grad, hidden_low),
            ],
            axis=1,
        ).astype(jnp.bfloat16),
        "rows",
        scatter_dimension=0,
        tiled=True,
    )
    summed = lax.psum(share, "seq").astype(jnp.float32)
    small_sums = lax.psum(
        (
            norm_gain_part,
            short_grad,
            cond_weight_grad,
            slope_full,
            shift_full,
            skip_full,
            ffn_gain_part,
        ),
        ("rows", "seq"),
    )
    proj_in_grad = summed[:, : 3 * model_width]
    proj_out_grad = summed[:, 3 * model_width : 4 * model_width]
    ffn_in_grad = summed[:, 4 * model_width : 4 * model_width + 2 * hidden_width]
    ffn_out_grad = jnp.transpose(summed[:, 4 * model_width + 2 * hidden_width :])
    return (
        output,
        input_grad,
        small_sums[0],
        proj_in_grad,
        small_sums[1],
        small_sums[2],
        small_sums[3],
        small_sums[4],
        small_sums[5],
        proj_out_grad,
        small_sums[6],
        ffn_in_grad,
        ffn_out_grad,
    )


def solution(mesh):
    in_specs = (
        P("rows", "seq", None),
        P("rows"),
        P("rows", "seq"),
        P(),
        P(),
        P(),
        P(),
        P(),
        P(),
        P(),
        P(),
        P(),
        P(),
        P(),
        P("rows", "seq", None),
    )
    out_specs = (
        P("rows", "seq", None),
        P("rows", "seq", None),
        P(),
        P("rows", None),
        P(),
        P(),
        P(),
        P(),
        P(),
        P("rows", None),
        P(),
        P("rows", None),
        P(None, "rows"),
    )
    return jax.shard_map(
        per_device, mesh=mesh, in_specs=in_specs, out_specs=out_specs, check_vma=False
    )
```

profile of v0, /device:TPU:0, one launch (start us, length us, event | category | flops | bytes accessed | tf_op | source)
XLA Modules:
  0.0 1535.2 jit_solution(1265153593060463719)
XLA Ops:
  82.0 51.7 %multiply_add_fusion.1 = f32[4,512,1536]{1,0,2:T(4,128)} fusion(f32[4,514,768]{1,0,2:T(4,128)} %get-tuple-element.47, f32[4,514,768]{1,0,2:T(4,128)} %get-tuple-element.46, f32[4,512]{1,0:T(4,128)S(1)} %get-tuple-element.66, f32[1536]{0:T(1024)S(1)} %copy-done.39, f32[4,512]{1,0:T(4,128)S(1)} %get-tuple-element.65, f32[1536]{0:T(1024)S(1)} %copy-done.41, ...), kind=kLoop, calls=%fused_computation.36 | loop fusion | flops 31457280 | bytes 25249792 | tf_op jit(solution)/shard_map/jvp()/add | solution.py:27
  133.8 16.6 %multiply_convert_fusion.3 = (bf16[4,512,768]{1,0,2:T(4,128)(2,1)}, bf16[4,512,768]{1,0,2:T(4,128)(2,1)}) fusion(f32[4,514,2304]{1,0,2:T(4,128)} %copy-done.1, f32[4,512]{1,0:T(4,128)S(1)} %get-tuple-element.66, f32[768]{0:T(1024)S(1)} %copy-done.48, f32[4,512]{1,0:T(4,128)S(1)} %get-tuple-element.65, f32[768]{0:T(1024)S(1)} %copy-done.49, ...), kind=kLoop, calls=%fused_computation.151 | loop fusion | flops 17301504 | bytes 31491072 | tf_op jit(solution)/shard_map/convert_element_type | solution.py:145
  157.2 34.6 %all-to-all-done.1 = bf16[4,512,768]{1,0,2:T(4,128)(2,1)} async-done(((bf16[4,512,768]{1,0,2:T(4,128)(2,1)}), bf16[4,512,768]{1,0,2:T(4,128)(2,1)}, u32[]{:S(2)}, u32[]{:S(2)}) %all-to-all-start.1) | async-done | bytes 3145760 | tf_op jit(solution)/shard_map/all_to_all | solution.py:169
  203.5 25.3 %fusion.89 = f32[4,384,1025]{1,2,0:T(8,128)} fusion(bf16[4,1024,384]{2,1,0:T(8,128)(2,1)} %bitcast.349), kind=kOutput, calls=%fused_computation.171 | convolution fusion | flops 9687808000 | bytes 9443328 | tf_op jit(solution)/shard_map/ft,ktd->kfd/dot_general | solution.py:49
  228.9 23.1 %fusion.95 = f32[4,384,1025]{1,2,0:T(8,128)} fusion(bf16[4,1024,384]{2,1,0:T(8,128)(2,1)S(1)} %bitcast.350), kind=kOutput, calls=%fused_computation.177 | convolution fusion | flops 9687808000 | bytes 9443328 | tf_op jit(solution)/shard_map/ft,ktd->kfd/dot_general | solution.py:48
  258.2 25.6 %fusion.87 = f32[4,384,1025]{1,2,0:T(8,128)} fusion(bf16[4,1024,384]{2,1,0:T(8,128)(2,1)} %bitcast.337), kind=kOutput, calls=%fused_computation.169 | convolution fusion | flops 9687808000 | bytes 9443328 | tf_op jit(solution)/shard_map/ft,ktd->kfd/dot_general | solution.py:47
  283.8 23.0 %fusion.97 = f32[4,384,1025]{1,2,0:T(8,128)} fusion(bf16[4,1024,384]{2,1,0:T(8,128)(2,1)S(1)} %bitcast.338), kind=kOutput, calls=%fused_computation.179 | convolution fusion | flops 9687808000 | bytes 9443328 | tf_op jit(solution)/shard_map/ft,ktd->kfd/dot_general | solution.py:46
  315.5 43.5 %fusion.29 = f32[4,384,1024]{1,2,0:T(8,128)} fusion(f32[4,384,1025]{1,2,0:T(8,128)} %fusion.87, f32[4,384,1025]{1,2,0:T(8,128)} %fusion.97, f32[1025]{0:T(1024)S(1)} %select_multiply_fusion, f32[4,384,1025]{1,2,0:T(8,128)} %fusion.95, f32[384]{0:T(512)S(1)} %dynamic_slice.10, f32[4,384,1025]{1,2,0:T(8,128)S(1)} %bitcast.325, f32[384]{0:T(512)S(1)} %dynamic_slice.9), kind=kOutput, calls=%fused_computation.76 | convolution fusion | flops 9712998400 | bytes 31489028 | tf_op jit(solution)/shard_map/ft,kfd->ktd/dot_general | solution.py:71
  359.0 32.5 %fusion.57 = bf16[4,1024,384]{2,1,0:T(8,128)(2,1)S(1)} fusion(bf16[4,1024,384]{2,1,0:T(8,128)(2,1)S(1)} %bitcast.339, f32[4,384,1024]{1,2,0:T(8,128)} %fusion.29, f32[384]{0:T(512)S(1)} %copy-done.67, f32[4,1025,384]{2,1,0:T(8,128)} %fusion.250), kind=kOutput, calls=%fused_computation.120 | convolution fusion | flops 9695672320 | bytes 18882048 | tf_op jit(solution)/shard_map/ft,kfd->ktd/dot_general | solution.py:71
  394.0 38.8 %all_to_all.81 = bf16[4,1024,384]{2,0,1:T(4,128)(2,1)} all-to-all(bf16[4,1024,384]{2,0,1:T(4,128)(2,1)S(1)} %copy.73), channel_id=1, replica_groups=mesh['rows'=16,'seq'=2] {'seq'}, dimensions={1} | all-to-all | bytes 6291456 | tf_op jit(solution)/shard_map/all_to_all | solution.py:182
  456.4 30.5 %fusion.205 = f32[2048,6144]{1,0:T(8,128)} fusion(bf16[768,6144]{1,0:T(8,128)(2,1)} %param.27, f32[2048,768]{1,0:T(8,128)} %copy-done.11, f32[768]{0:T(1024)S(1)} %copy-done.66, f32[2048]{0:T(1024)S(1)} %fusion.144, f32[2048]{0:T(1024)S(1)} %broadcast_multiply_fusion.2), kind=kOutput, calls=%fused_computation.289 | convolution fusion | flops 19333644288 | bytes 66079744 | tf_op jit(solution)/shard_map/dot_general | solution.py:189
  486.9 65.6 %fusion.12 = (f32[2048,3072]{1,0:T(8,128)}, f32[2048,3072]{1,0:T(8,128)}, f32[2048,3072]{1,0:T(8,128)}) fusion(f32[2048,6144]{1,0:T(8,128)} %fusion.205, bf16[2048,768]{1,0:T(8,128)(2,1)} %bitcast.335, bf16[3072,768]{1,0:T(8,128)(2,1)} %param.28), kind=kOutput, calls=%fused_computation.50 | convolution fusion | flops 10072621056 | bytes 108527616 | tf_op jit(solution)/shard_map/dot_general | solution.py:78
  552.5 46.8 %multiply_add_fusion = (f32[2048,3072]{1,0:T(8,128)}, bf16[2048,3072]{1,0:T(8,128)(2,1)}) fusion(f32[2048,3072]{1,0:T(8,128)} %get-tuple-element.41, f32[2048,3072]{1,0:T(8,128)} %get-tuple-element.69, f32[2048,6144]{1,0:T(8,128)} %fusion.205), kind=kLoop, calls=%fused_computation.3 | loop fusion | flops 106954752 | bytes 138412032 | tf_op jit(solution)/shard_map/transpose(jvp())/add_any | solution.py:193
  599.3 31.1 %multiply_reduce_fusion.4 = (f32[768]{0:T(1024)}, f32[2048]{0:T(1024)}, f32[2048,768]{1,0:T(8,128)}) fusion(f32[2048,768]{1,0:T(8,128)} %copy-done.11, f32[2048]{0:T(1024)} %copy-done.63, f32[2048]{0:T(1024)S(1)} %copy-done.35, f32[768]{0:T(1024)} %param.26, bf16[768,6144]{1,0:T(8,128)(2,1)} %param.27, f32[2048,3072]{1,0:T(8,128)} %get-tuple-element.42, ...), kind=kOutput, calls=%fused_computation.138 | convolution fusion | flops 19363526656 | bytes 72382464 | tf_op jit(solution)/shard_map/dot_general | solution.py:78
  684.4 19.1 %all-to-all-done.3 = bf16[4,512,768]{1,0,2:T(4,128)(2,1)} async-done(((bf16[4,512,768]{1,0,2:T(4,128)(2,1)}), bf16[4,512,768]{1,0,2:T(4,128)(2,1)}, u32[]{:S(2)}, u32[]{:S(2)}) %all-to-all-start.3) | async-done | bytes 3145760 | tf_op jit(solution)/shard_map/all_to_all | solution.py:212
  709.7 30.3 %fusion.71 = f32[4,384,1025]{1,2,0:T(8,128)} fusion(bf16[4,1024,384]{2,1,0:T(8,128)(2,1)} %bitcast.333, f32[1025]{0:T(1024)S(1)} %copy-done.22), kind=kOutput, calls=%fused_computation.153 | convolution fusion | flops 9692528640 | bytes 9447428 | tf_op jit(solution)/shard_map/transpose(jvp(ft,kfd->ktd))/dot_general | solution.py:71
  740.0 27.0 %multiply_add_fusion.2 = (f32[4,384,1025]{1,2,0:T(8,128)}, f32[4,384,1025]{1,2,0:T(8,128)}, f32[4,384,1025]{1,2,0:T(8,128)}) fusion(f32[4,384,1025]{1,2,0:T(8,128)} %fusion.97, f32[4,384,1025]{1,2,0:T(8,128)} %fusion.71, f32[4,384,1025]{1,2,0:T(8,128)} %fusion.87, f32[1025]{0:T(1024)S(1)} %copy-done.22, bf16[4,384,1024]{1,2,0:T(8,128)(2,1)S(1)} %bitcast.334), kind=kOutput, calls=%fused_computation.99 | convolution fusion | flops 9700403200 | bytes 40935428 | tf_op jit(solution)/shard_map/transpose(jvp(ft,kfd->ktd))/dot_general | solution.py:71
  775.2 41.5 %fusion.35 = f32[4,384,1024]{1,2,0:T(8,128)} fusion(f32[4,384,1025]{1,2,0:T(8,128)} %get-tuple-element.71, f32[4,384,1025]{1,2,0:T(8,128)} %fusion.71, f32[4,384,1025]{1,2,0:T(8,128)} %fusion.95, f32[4,384,1025]{1,2,0:T(8,128)S(1)} %bitcast.327, f32[384]{0:T(512)S(1)} %copy-done.54, f32[384]{0:T(512)S(1)} %copy-done.57), kind=kOutput, calls=%fused_computation.86 | convolution fusion | flops 9709849600 | bytes 31484928 | tf_op jit(solution)/shard_map/transpose(jvp(ft,ktd->kfd))/dot_general | solution.py:46
  816.7 32.6 %fusion.54 = bf16[4,1024,384]{2,1,0:T(8,128)(2,1)S(1)} fusion(f32[4,384,1024]{1,2,0:T(8,128)} %fusion.35, bf16[4,512,2,384]{3,1,2,0:T(8,128)(2,1)S(1)} %copy-done.8, f32[384]{0:T(512)S(1)} %copy-done.68, f32[4,384,1025]{1,2,0:T(8,128)} %fusion.248), kind=kOutput, calls=%fused_computation.111 | convolution fusion | flops 9695672320 | bytes 18882048 | tf_op jit(solution)/shard_map/transpose(jvp(ft,ktd->kfd))/dot_general | solution.py:47
  858.7 38.3 %fusion.16 = f32[4,384,1024]{2,1,0:T(8,128)} fusion(f32[4,384,1025]{1,2,0:T(8,128)} %get-tuple-element.45, f32[4,384,1025]{1,2,0:T(8,128)} %fusion.89, f32[4,384,1025]{1,2,0:T(8,128)} %fusion.95, f32[4,384,1025]{1,2,0:T(8,128)} %get-tuple-element.44, f32[384]{0:T(512)S(1)} %copy-done.57, f32[384]{0:T(512)S(1)} %copy-done.54), kind=kOutput, calls=%fused_computation.58 | convolution fusion | flops 9720870912 | bytes 31484928 | tf_op jit(solution)/shard_map/transpose(jvp(ft,ktd->kfd))/dot_general | solution.py:49
  897.0 39.7 %fusion.110 = bf16[4,1024,384]{1,2,0:T(8,128)(2,1)} fusion(f32[4,384,1024]{2,1,0:T(8,128)} %fusion.16, f32[4,384,1025]{1,2,0:T(8,128)} %fusion.95, f32[4,384,1025]{1,2,0:T(8,128)} %get-tuple-element.44, f32[4,384,1025]{1,2,0:T(8,128)} %get-tuple-element.45, f32[4,384,1025]{1,2,0:T(8,128)} %fusion.89, f32[384]{0:T(512)S(1)} %copy-done.57, f32[384]{0:T(512)S(1)} %copy-done.54), kind=kOutput, calls=%fused_computation.192 | convolution fusion | flops 9722441728 | bytes 34630656 | tf_op jit(solution)/shard_map/transpose(jvp(ft,ktd->kfd))/dot_general | solution.py:48
  948.0 42.5 %convolution_convert_fusion.1 = bf16[768,6144]{1,0:T(8,128)(2,1)} fusion(f32[2048,3072]{1,0:T(8,128)} %get-tuple-element.42, f32[2048,3072]{1,0:T(8,128)} %get-tuple-element.40, f32[2048,768]{1,0:T(8,128)} %copy-done.11, f32[768]{0:T(1024)} %param.26, f32[2048]{0:T(1024)S(1)} %copy-done.64, f32[2048]{0:T(1024)S(1)} %copy-done.36), kind=kOutput, calls=%fused_computation.41 | convolution fusion | flops 19363528704 | bytes 66079744 | tf_op jit(solution)/shard_map/dot_general | solution.py:84
  1006.0 40.5 %multiply_reduce_fusion.8 = (f32[768]{0:T(1024)}, f32[768]{0:T(1024)}, f32[768]{0:T(1024)}, f32[4,512,768]{1,0,2:T(4,128)}, f32[4,512,768]{1,0,2:T(4,128)}, /*index=5*/f32[4,512,768]{1,0,2:T(4,128)}, f32[4,512,768]{1,0,2:T(4,128)}) fusion(f32[4,514,2304]{1,0,2:T(4,128)} %copy-done.1, f32[4,512]{1,0:T(4,128)S(1)} %copy-done.26, ...), kind=kLoop, calls=%fused_computation.142 | loop fusion | flops 20444928 | bytes 56666112 | tf_op jit(solution)/shard_map/transpose(jvp())/reduce_sum | solution.py:29
  1046.5 78.6 %multiply_reduce_fusion.2 = (f32[1536]{0:T(1024)}, f32[1536]{0:T(1024)}, f32[1536]{0:T(1024)}, f32[4,512,1536]{1,0,2:T(4,128)S(1)}, f32[4,512,1536]{1,0,2:T(4,128)}, /*index=5*/f32[4,512,1536]{1,0,2:T(4,128)}) fusion(f32[4,514,768]{1,0,2:T(4,128)} %get-tuple-element.47, f32[4,514,768]{1,0,2:T(4,128)} %get-tuple-element.46, f32[4,512]{1,0:T(4,128)S(1)} %copy-done.26, ...), kind=kLoop, calls=%fused_computation.34 | loop fusion | flops 47181312 | bytes 63016960 | tf_op jit(solution)/shard_map/transpose(jvp())/reduce_sum | solution.py:29
  1125.1 18.9 %pad_add_fusion.1 = f32[4,514,1536]{1,0,2:T(4,128)S(1)} fusion(f32[4,512,1536]{1,0,2:T(4,128)} %get-tuple-element.52, f32[4,512,1536]{1,0,2:T(4,128)S(1)} %get-tuple-element.50, f32[4,512,1536]{1,0,2:T(4,128)} %get-tuple-element.51), kind=kLoop, calls=%fused_computation.28 | loop fusion | flops 6316032 | bytes 50380800 | tf_op jit(solution)/shard_map/transpose(jvp())/add_any | solution.py:27
  1165.2 35.2 %pad_add_fusion = f32[4,514,2304]{1,0,2:T(4,128)} fusion(f32[4,514,768]{1,0,2:T(4,128)} %get-tuple-element.49, f32[4,514,768]{1,0,2:T(4,128)} %get-tuple-element.48, f32[4,514,768]{1,0,2:T(4,128)} %pad_add_fusion.3), kind=kLoop, calls=%fused_computation.19 | loop fusion | flops 9474048 | bytes 37896192 | tf_op jit(solution)/shard_map/transpose(jvp())/add_any | solution.py:129
  1223.7 17.3 %fusion.7 = bf16[4,512,2304]{1,0,2:T(4,128)(2,1)S(1)} fusion(f32[4,514,2304]{1,0,2:T(4,128)} %pad_add_fusion, bf16[4,2,2304]{1,0,2:T(4,128)(2,1)} %copy.87), kind=kLoop, calls=%fused_computation.22 | loop fusion | flops 14155776 | bytes 28348416 | tf_op jit(solution)/shard_map/convert_element_type | solution.py:248
  1255.1 16.9 %pad_maximum_fusion = bf16[768,12288]{1,0:T(8,128)(2,1)} fusion(bf16[768,3072]{1,0:T(8,128)(2,1)} %fusion.79, bf16[768,6144]{1,0:T(8,128)(2,1)} %convolution_convert_fusion.1, bf16[768,768]{1,0:T(8,128)(2,1)S(1)} %copy-done.17, bf16[768,2304]{1,0:T(8,128)(2,1)} %bitcast_convert_fusion), kind=kLoop, calls=%fused_computation.23 | loop fusion | flops 75497472 | bytes 37748736 | tf_op jit(solution)/shard_map/concatenate | solution.py:253
  1272.0 16.7 %add_convert_fusion.2 = bf16[2048,768]{1,0:T(8,128)(2,1)} fusion(f32[2048,768]{1,0:T(8,128)} %copy-done.11, bf16[2048,3072]{1,0:T(8,128)(2,1)} %get-tuple-element.43, bf16[3072,768]{1,0:T(8,128)(2,1)} %param.28), kind=kOutput, calls=%fused_computation.148 | convolution fusion | flops 9666822144 | bytes 26738688 | tf_op jit(solution)/shard_map/dot_general | solution.py:199
  1288.7 21.2 %fusion.206 = (f32[384]{0:T(512)}, f32[384]{0:T(512)}) fusion(f32[4,384,1025]{1,2,0:T(8,128)} %fusion.89, f32[4,384,1025]{1,2,0:T(8,128)} %fusion.95, f32[384]{0:T(512)S(1)} %copy-done.55, f32[384]{0:T(512)S(1)} %copy-done.58, f32[4,384,1025]{1,2,0:T(8,128)} %get-tuple-element.71, f32[4,384,1025]{1,2,0:T(8,128)} %fusion.87, f32[4,384,1025]{1,2,0:T(8,128)} %fusion.71, ...), kind=kLoop, calls=%fused_computation.290 | loop fusion | flops 39359232 | bytes 37791744 | tf_op jit(solution)/shard_map/reduce_sum | solution.py:241
  1355.8 113.3 %reduce-scatter.2.cloned.1.call-done = bf16[48,12288]{1,0:T(8,128)(2,1)} async-done(((bf16[768,12288]{1,0:T(8,128)(2,1)}), bf16[48,12288]{1,0:T(8,128)(2,1)}) %reduce-scatter.2.cloned.1.call-update) | async-done | bytes 1179664 | tf_op jit(solution)/shard_map/reduce_scatter | solution.py:252
  1470.4 42.2 %all-reduce.20 = (f32[768]{0:T(1024)}, f32[3,1536]{1,0:T(4,128)}, f32[3,768]{1,0:T(4,128)}, f32[768]{0:T(1024)}, f32[768]{0:T(1024)}, /*index=5*/f32[768]{0:T(1024)}, f32[768]{0:T(1024)}) all-reduce(f32[768]{0:T(1024)} %get-tuple-element.21, f32[3,1536]{1,0:T(4,128)} %pad_add_fusion.4, ...), channel_id=1, replica_groups=mesh['rows'=16,'seq'=2] {'rows','seq'}, use_global_device_ids=true, to_apply=%region_9.10 | all-reduce | flops 10752 | bytes 86016 | tf_op jit(solution)/shard_map/psum | solution.py:267
  (267 shorter events, 359.5 us)
Async XLA Ops:
  28.1 26.9 %collective-permute-start = (bf16[4,2,2304]{2,0,1:T(4,128)(2,1)}, bf16[4,2,2304]{2,0,1:T(4,128)(2,1)}, u32[]{:S(2)}, u32[]{:S(2)}) collective-permute-start(bf16[4,2,2304]{2,0,1:T(4,128)(2,1)} %copy.100), channel_id=1, source_target_pairs={{0,1},{2,3},{4,5},{6,7},{8,9},{10,11},{12,13},{14,15},{16,17},{18,... | collective-permute-start | bytes 110600 | tf_op jit(solution)/shard_map/ppermute | solution.py:15
  36.1 97.7 %copy-start.23 = (f32[4,512]{1,0:T(4,128)}, f32[4,512]{1,0:T(4,128)S(1)}, u32[]{:S(2)}) copy-start(f32[4,512]{1,0:T(4,128)S(1)} %get-tuple-element.65) | copy-start | bytes 24580
  36.1 97.7 %copy-start.25 = (f32[4,512]{1,0:T(4,128)}, f32[4,512]{1,0:T(4,128)S(1)}, u32[]{:S(2)}) copy-start(f32[4,512]{1,0:T(4,128)S(1)} %get-tuple-element.66) | copy-start | bytes 24580
  82.0 51.8 %copy-start.33 = (f32[4,512]{1,0:T(4,128)S(1)}, f32[4,512]{1,0:T(4,128)}, u32[]{:S(2)}) copy-start(f32[4,512]{1,0:T(4,128)} %convert_element_type.177) | copy-start | bytes 24580
  82.0 51.8 %copy-start.47 = (f32[768]{0:T(1024)S(1)}, f32[768]{0:T(1024)}, u32[]{:S(2)}) copy-start(f32[768]{0:T(1024)} %get-tuple-element.28) | copy-start | bytes 9220
  82.0 51.8 %copy-start.48 = (f32[768]{0:T(1024)S(1)}, f32[768]{0:T(1024)}, u32[]{:S(2)}) copy-start(f32[768]{0:T(1024)} %get-tuple-element.29) | copy-start | bytes 9220
  82.0 51.8 %copy-start.49 = (f32[768]{0:T(1024)S(1)}, f32[768]{0:T(1024)}, u32[]{:S(2)}) copy-start(f32[768]{0:T(1024)} %get-tuple-element.30) | copy-start | bytes 9220
  150.4 41.5 %all-to-all-start.1 = ((bf16[4,512,768]{1,0,2:T(4,128)(2,1)}), bf16[4,512,768]{1,0,2:T(4,128)(2,1)}, u32[]{:S(2)}, u32[]{:S(2)}) async-start(bf16[4,512,768]{1,0,2:T(4,128)(2,1)} %get-tuple-element.61), calls=%async_computation.1 | async-start | bytes 6291456 | tf_op jit(solution)/shard_map/all_to_all | solution.py:169
  155.8 159.7 %copy-start.53 = (f32[384]{0:T(512)}, f32[384]{0:T(512)S(1)}, u32[]{:S(2)}) copy-start(f32[384]{0:T(512)S(1)} %dynamic_slice.10) | copy-start | bytes 4612
  155.9 159.6 %copy-start.56 = (f32[384]{0:T(512)}, f32[384]{0:T(512)S(1)}, u32[]{:S(2)}) copy-start(f32[384]{0:T(512)S(1)} %dynamic_slice.9) | copy-start | bytes 4612
  157.2 158.3 %copy-start.21 = (f32[1025]{0:T(1024)}, f32[1025]{0:T(1024)S(1)}, u32[]{:S(2)}) copy-start(f32[1025]{0:T(1024)S(1)} %select_multiply_fusion) | copy-start | bytes 12304
  191.8 60.1 %all-to-all-start = ((bf16[4,512,768]{1,0,2:T(4,128)(2,1)}), bf16[4,512,768]{1,0,2:T(4,128)(2,1)}, u32[]{:S(2)}, u32[]{:S(2)}) async-start(bf16[4,512,768]{1,0,2:T(4,128)(2,1)} %get-tuple-element.62), calls=%async_computation | async-start | bytes 6291456 | tf_op jit(solution)/shard_map/all_to_all | solution.py:168
  258.2 48.5 %slice-start = ((s8[6340608]{0:T(1024)(128)(4,1)}), s8[4194304]{0:T(1024)(128)(4,1)S(1)}, s32[]{:S(2)}) async-start(s8[6340608]{0:T(1024)(128)(4,1)} %bitcast.324), calls=%async_computation.9 | async-start | bytes 8388608
  258.2 48.5 %slice-start.4 = ((s8[6340608]{0:T(1024)(128)(4,1)}), s8[4194304]{0:T(1024)(128)(4,1)S(1)}, s32[]{:S(2)}) async-start(s8[6340608]{0:T(1024)(128)(4,1)} %bitcast.328), calls=%async_computation.13 | async-start | bytes 8388608
  315.5 43.5 %copy-start.67 = (f32[384]{0:T(512)S(1)}, f32[384]{0:T(512)}, u32[]{:S(2)}) copy-start(f32[384]{0:T(512)} %dynamic_slice.11) | copy-start | bytes 4612
  452.5 34.5 %copy-start.34 = (f32[2048]{0:T(1024)}, f32[2048]{0:T(1024)S(1)}, u32[]{:S(2)}) copy-start(f32[2048]{0:T(1024)S(1)} %broadcast_multiply_fusion.2) | copy-start | bytes 24580
  456.4 30.5 %copy-start.63 = (f32[2048]{0:T(1024)}, f32[2048]{0:T(1024)S(1)}, u32[]{:S(2)}) copy-start(f32[2048]{0:T(1024)S(1)} %fusion.144) | copy-start | bytes 24580
  552.5 46.8 %copy-start.35 = (f32[2048]{0:T(1024)S(1)}, f32[2048]{0:T(1024)}, u32[]{:S(2)}) copy-start(f32[2048]{0:T(1024)} %copy-done.34) | copy-start | bytes 24580
  599.3 31.1 %copy-start.44 = (f32[2048]{0:T(1024)S(1)}, f32[2048]{0:T(1024)}, u32[]{:S(2)}) copy-start(f32[2048]{0:T(1024)} %copy-done.43) | copy-start | bytes 24580
  663.8 39.7 %all-to-all-start.3 = ((bf16[4,512,768]{1,0,2:T(4,128)(2,1)}), bf16[4,512,768]{1,0,2:T(4,128)(2,1)}, u32[]{:S(2)}, u32[]{:S(2)}) async-start(bf16[4,512,768]{1,0,2:T(4,128)(2,1)} %get-tuple-element.56), calls=%async_computation.3 | async-start | bytes 6291456 | tf_op jit(solution)/shard_map/all_to_all | solution.py:212
  709.7 30.3 %copy-start.8 = (bf16[4,512,2,384]{3,1,2,0:T(8,128)(2,1)S(1)}, bf16[4,512,2,384]{3,1,2,0:T(8,128)(2,1)}, u32[]{:S(2)}) copy-start(bf16[4,512,2,384]{3,1,2,0:T(8,128)(2,1)} %copy.76) | copy-start | bytes 9437188
  709.7 57.4 %slice-start.2 = ((s8[6340608]{0:T(1024)(128)(4,1)}), s8[4194304]{0:T(1024)(128)(4,1)S(1)}, s32[]{:S(2)}) async-start(s8[6340608]{0:T(1024)(128)(4,1)} %bitcast.326), calls=%async_computation.11 | async-start | bytes 8388608
  709.7 57.4 %slice-start.6 = ((s8[6340608]{0:T(1024)(128)(4,1)}), s8[4194304]{0:T(1024)(128)(4,1)S(1)}, s32[]{:S(2)}) async-start(s8[6340608]{0:T(1024)(128)(4,1)} %bitcast.330), calls=%async_computation.15 | async-start | bytes 8388608
  775.2 41.5 %copy-start.68 = (f32[384]{0:T(512)S(1)}, f32[384]{0:T(512)}, u32[]{:S(2)}) copy-start(f32[384]{0:T(512)} %dynamic_slice.11) | copy-start | bytes 4612
  853.5 89.2 %all-to-all-start.5 = ((bf16[4,1024,384]{2,0,1:T(4,128)(2,1)}), bf16[4,1024,384]{2,0,1:T(4,128)(2,1)}, u32[]{:S(2)}, u32[]{:S(2)}) async-start(bf16[4,1024,384]{2,0,1:T(4,128)(2,1)} %copy.83), calls=%async_computation.5 | async-start | bytes 6291456 | tf_op jit(solution)/shard_map/all_to_all | solution.py:231
  942.7 55.6 %all-to-all-start.4 = ((bf16[4,1024,384]{2,0,1:T(4,128)(2,1)}), bf16[4,1024,384]{2,0,1:T(4,128)(2,1)}, u32[]{:S(2)}, u32[]{:S(2)}) async-start(bf16[4,1024,384]{2,0,1:T(4,128)(2,1)} %copy.79), calls=%async_computation.4 | async-start | bytes 6291456 | tf_op jit(solution)/shard_map/all_to_all | solution.py:234
  947.9 521.2 %reduce-scatter.2.cloned.1.call-start = ((), (), s32[]{:S(2)}) async-start(), calls=%async_computation.7 | async-start | bytes 20054016 | tf_op jit(solution)/shard_map/reduce_scatter | solution.py:252
  1005.9 40.6 %copy-start.38 = (f32[1536]{0:T(1024)S(1)}, f32[1536]{0:T(1024)}, u32[]{:S(2)}) copy-start(f32[1536]{0:T(1024)} %get-tuple-element.25) | copy-start | bytes 18436
  1005.9 40.6 %copy-start.40 = (f32[1536]{0:T(1024)S(1)}, f32[1536]{0:T(1024)}, u32[]{:S(2)}) copy-start(f32[1536]{0:T(1024)} %get-tuple-element.26) | copy-start | bytes 18436
  1006.0 40.6 %copy-start.42 = (f32[1536]{0:T(1024)S(1)}, f32[1536]{0:T(1024)}, u32[]{:S(2)}) copy-start(f32[1536]{0:T(1024)} %get-tuple-element.27) | copy-start | bytes 18436
  1209.5 10.4 collective-permute-start.1
  1272.0 250.1 %all-reduce.23.cloned.1.call-start = ((), (), s32[]{:S(2)}) async-start(), calls=%async_computation.8 | async-start | bytes 2359296 | tf_op jit(solution)/shard_map/psum | solution.py:266
  (58 other events, 657.5 us)
Sparse Core Ops, SparseCore 0:
  1272.1 196.9 reduce-scatter.1
  1471.4 42.9 all-reduce.22
where the time goes:
time: 1540 us
  matrix products  630 us (41%)
  other arithmetic  440 us (29%)
  local copies, waits for them, and re-layouts  169 us (11%)
  waiting for transfers between devices  167 us (11%)
  blocking collectives  81 us (5%)
  starting transfers between devices  33.5 us (2%)
    reduce_sum x2, other arithmetic, conv_three(): weights[2] * extended[:, :length] * same_two  119 us
    dot_general x4, matrix products, times_transpose(): lax.dot_general(left, right, (((1,), (1,)), ((), ())), preferred_element_...  115 us
    reduce_scatter x1, waiting for transfers between devices, per_device(): lax.psum_scatter(jnp.concatenate([transpose_times(first_act, proj_low), t...  113 us
    dot_general x4, matrix products, transpose_times(): lax.dot_general(left, right, (((0,), (0,)), ((), ())), preferred_element_...  74.7 us
    dot_general x2, matrix products, synth(): jnp.einsum('ft,kfd->ktd', cos_table, prod_real, precision=PRECISE)  70.5 us
    dot_general x2, matrix products, analyze(): value_real = jnp.einsum('ft,ktd->kfd', cos_table, values, precision=PRECISE)  64.5 us
    dot_general x2, matrix products, analyze(): cond_imag = -jnp.einsum('ft,ktd->kfd', sin_table, conds, precision=PRECISE)  63.7 us
    dot_general x2, matrix products, analyze(): cond_real = jnp.einsum('ft,ktd->kfd', cos_table, conds, precision=PRECISE)  62.8 us
  transfers between devices with their start and end apart: 9, of which 3 were waited for; matrix products, arithmetic and copies ran while one was open for 21% of the time, Pallas kernels for 0%

commit v1 on v0

--- a/solution.py
+++ b/solution.py
@@ -1,11 +1,651 @@
+import functools
 import math
 
 import jax
 import jax.numpy as jnp
 from jax import lax
+from jax.experimental import pallas as pl
+from jax.experimental.pallas import tpu as pltpu
 from jax.sharding import PartitionSpec as P
 
 EPSILON = 1e-05
+BF = jnp.bfloat16
+F32 = jnp.float32
+ROOT_HALF = math.sqrt(0.5)
+LIMIT = 67043328
+
+
+def mm(a, b):
+    return lax.dot_general(a, b, (((1,), (0,)), ((), ())), preferred_element_type=F32)
+
+
+def mm_t(a, b):
+    return lax.dot_general(a, b, (((1,), (1,)), ((), ())), preferred_element_type=F32)
+
+
+def spectral_tables(length, offset):
+    quarter = length // 4
+    two_n = 2 * length
+    m = lax.broadcasted_iota(jnp.int32, (quarter, quarter), 0)
+    s = lax.broadcasted_iota(jnp.int32, (quarter, quarter), 1)
+
+    def cos_sin(freq):
+        angle = ((freq * s + offset) % two_n).astype(F32) * (2.0 * math.pi / two_n)
+        return jnp.cos(angle), jnp.sin(angle)
+
+    half = quarter // 2
+    forward, inverse = [], []
+    for r in (1, 2, 3):
+        c, sn = cos_sin(8 * m + r)
+        forward.append(jnp.concatenate([jnp.concatenate([c, sn], 1), jnp.concatenate([-sn, c], 1)], 0))
+        inverse.append(forward[-1].T * (2.0 / two_n))
+    row = m % half
+    low = m < half
+    c, sn = cos_sin(8 * jnp.where(m == half, half, row))
+    zero = jnp.where(low | (m == half), c, -sn)
+    c4, sn4 = cos_sin(8 * row + 4)
+    four = jnp.where(low, c4, -sn4)
+    edge = jnp.where((m == 0) | (m == half), 1.0, 2.0) / two_n
+    fwd_real = jnp.concatenate([zero, four], 0)
+    inv_real = jnp.concatenate([(zero * edge).T, four.T * (2.0 / two_n)], 0)
+    return (
+        fwd_real.astype(BF),
+        jnp.concatenate(forward, 0).astype(BF),
+        inv_real.astype(BF),
+        jnp.concatenate(inverse, 0).astype(BF),
+    )
+
+
+def loop(count, body):
+    lax.fori_loop(0, count, lambda i, c: (body(i), c)[1], 0)
+
+
+def rows_of(i, size):
+    return pl.ds(pl.multiple_of(i * size, size), size)
+
+
+def norm_stats(v):
+    center = v - jnp.mean(v, axis=-1, keepdims=True)
+    scale = lax.rsqrt(jnp.mean(center * center, axis=-1, keepdims=True) + EPSILON)
+    return center * scale, scale
+
+
+def same_masks(position, split):
+    same_one = position != split
+    return same_one, same_one & (position != split + 1)
+
+
+def butterfly(x_ref, y_ref, lane, width, quarter):
+    tile = 32
+    lanes = slice(lane, lane + width)
+
+    def body(i):
+        x0, x1, x2, x3 = [
+            x_ref[pl.ds(pl.multiple_of(q * quarter + i * tile, tile), tile), :].astype(F32) for q in range(4)
+        ]
+        a, b, c, d = x0 + x2, x1 + x3, x0 - x2, x1 - x3
+        sd, sb = d * ROOT_HALF, b * ROOT_HALF
+        out = (a + b, a - b, x0 + sd, -x2 - sb, c, -d, x0 - sd, x2 - sb)
+        for k, value in enumerate(out):
+            y_ref[pl.ds(pl.multiple_of(k * quarter + i * tile, tile), tile), lanes] = value.astype(BF)
+
+    loop(quarter // tile, body)
+
+
+def blockwise(y_ref, spec_ref, fwd_real_ref, fwd_ref, quarter):
+    q = quarter
+    for k in range(2):
+        spec_ref[k * q : (k + 1) * q, :] = mm(fwd_real_ref[k * q : (k + 1) * q, :], y_ref[k * q : (k + 1) * q, :])
+    for k in range(3):
+        spec_ref[2 * q + 2 * k * q : 2 * q + 2 * (k + 1) * q, :] = mm(
+            fwd_ref[2 * k * q : 2 * (k + 1) * q, :], y_ref[2 * q + 2 * k * q : 2 * q + 2 * (k + 1) * q, :]
+        )
+
+
+def resynth(u_ref, out_ref, inv_real_ref, inv_ref, quarter):
+    blockwise(u_ref, out_ref, inv_real_ref, inv_ref, quarter)
+
+
+def each_bin(quarter, body, tile=16):
+    half = quarter // 2
+    body(0, half, True)
+
+    def run(base, span, skip):
+        def step(i):
+            start = base + (i + skip) * tile
+            body(start, start + span, False)
+
+        loop(span // tile - skip, step)
+
+    run(0, half, 1)
+    run(quarter, half, 0)
+    for k in range(3):
+        run(2 * quarter + 2 * k * quarter, quarter, 0)
+
+
+def recombine(o_ref, lanes, i, tile, quarter):
+    def part(k):
+        return o_ref[pl.ds(pl.multiple_of(k * quarter + i * tile, tile), tile), lanes]
+
+    u0, u4, a1, b1, a2, b2, a3, b3 = [part(k) for k in range(8)]
+    even, odd = u0 + u4, u0 - u4
+    return (
+        even + a1 + a2 + a3,
+        odd + (a1 - b1 - a3 - b3) * ROOT_HALF - b2,
+        even - b1 - a2 + b3,
+        odd + (a3 - b3 - a1 - b1) * ROOT_HALF + b2,
+    )
+
+
+def conv_back(ref, t, tile, weights, split):
+    block = ref[pl.ds(pl.multiple_of(t, tile), tile + 8), :]
+    width = block.shape[1]
+    position = t + lax.broadcasted_iota(jnp.int32, (tile, width), 0)
+    one, two = same_masks(position, split)
+    return (
+        weights[0:1, :] * block[8 : tile + 8]
+        + jnp.where(one, weights[1:2, :] * block[7 : tile + 7], 0.0)
+        + jnp.where(two, weights[2:3, :] * block[6 : tile + 6], 0.0)
+    )
+
+
+def mixer_forward_kernel(
+    split_ref, keep_ref, x_ref, norm_gain_ref, wq_ref, wk_ref, wv_ref, fq_ref, fv_ref, fk_ref, slope_ref, shift_ref,
+    skip_ref, wo_ref, ffn_gain_ref, fwd_real_ref, fwd_ref, inv_real_ref, inv_ref,
+    first_ref, q_ref, k_ref, v_ref, mixed_ref, gated_ref, resid_ref, second_ref,
+    qs, ks, vs, xv, xc, y_s, spec_s, u_s, o_s, qc,
+):
+    r, j = pl.program_id(0), pl.program_id(1)
+    length, width = q_ref.shape
+    quarter = length // 4
+    split, keep = split_ref[r], keep_ref[r]
+    tile = 64
+
+    @pl.when(j == 0)
+    def _():
+        def body(i):
+            rows = rows_of(i, tile)
+            v = x_ref[rows, :].astype(F32)
+            n, _ = norm_stats(v)
+            first_ref[rows, :] = (n * norm_gain_ref[...]).astype(BF)
+            resid_ref[rows, :] = v
+
+        loop(length // tile, body)
+        for ref in (qs, ks, vs):
+            ref[0:8, :] = jnp.zeros((8, width), F32)
+
+    for w_ref, out_ref, ref in ((wq_ref, q_ref, qs), (wk_ref, k_ref, ks), (wv_ref, v_ref, vs)):
+        value = mm(first_ref[...], w_ref[...]).astype(BF)
+        out_ref[...] = value
+        ref[8 : 8 + length, :] = value.astype(F32)
+
+    def conv(i):
+        t = i * tile
+        rows = rows_of(i, tile)
+        kept = t + lax.broadcasted_iota(jnp.int32, (tile, width), 0) < keep
+        qc[rows, :] = conv_back(qs, t, tile, fq_ref, split)
+        xv[rows, :] = jnp.where(kept, conv_back(vs, t, tile, fv_ref, split), 0.0).astype(BF)
+        xc[rows, :] = jnp.where(kept, conv_back(ks, t, tile, fk_ref, split), 0.0).astype(BF)
+
+    loop(length // tile, conv)
+    butterfly(xv, y_s, 0, width, quarter)
+    butterfly(xc, y_s, width, width, quarter)
+    blockwise(y_s, spec_s, fwd_real_ref, fwd_ref, quarter)
+
+    def bins(re, im, first):
+        n = 16
+        re, im = pl.ds(pl.multiple_of(re, n), n), pl.ds(pl.multiple_of(im, n), n)
+        vr, vi = spec_s[re, 0:width], spec_s[im, 0:width]
+        cr, ci = spec_s[re, width : 2 * width], spec_s[im, width : 2 * width]
+        slope, shift = slope_ref[...], shift_ref[...]
+        rr, ii = cr * cr, ci * ci
+        if first:
+            edge = lax.broadcasted_iota(jnp.int32, (n, width), 0) == 0
+            hr = cr * jax.nn.sigmoid(slope * jnp.where(edge, rr, rr + ii) + shift)
+            hi = ci * jax.nn.sigmoid(slope * jnp.where(edge, ii, rr + ii) + shift)
+            ur = vr * hr - jnp.where(edge, 0.0, vi * hi)
+            ui = jnp.where(edge, vi * hi, vr * hi + vi * hr)
+        else:
+            gain = jax.nn.sigmoid(slope * (rr + ii) + shift)
+            hr, hi = cr * gain, ci * gain
+            ur, ui = vr * hr - vi * hi, vr * hi + vi * hr
+        u_s[re, :] = ur.astype(BF)
+        u_s[im, :] = ui.astype(BF)
+
+    each_bin(quarter, bins)
+    resynth(u_s, o_s, inv_real_ref, inv_ref, quarter)
+
+    def finish(i):
+        n = 32
+        parts = recombine(o_s, slice(0, width), i, n, quarter)
+        for k, part in enumerate(parts):
+            rows = pl.ds(pl.multiple_of(k * quarter + i * n, n), n)
+            mixed = (part + skip_ref[...] * xv[rows, :].astype(F32)).astype(BF)
+            mixed_ref[rows, :] = mixed
+            gated_ref[rows, :] = (qc[rows, :] * mixed.astype(F32)).astype(BF)
+
+    loop(quarter // 32, finish)
+    resid_ref[...] += mm(gated_ref[...], wo_ref[...])
+
+    @pl.when(j == pl.num_programs(1) - 1)
+    def _():
+        def body(i):
+            rows = rows_of(i, tile)
+            n, _ = norm_stats(resid_ref[rows, :])
+            second_ref[rows, :] = (n * ffn_gain_ref[...]).astype(BF)
+
+        loop(length // tile, body)
+
+
+def once(shape, index):
+    return pl.BlockSpec(shape, index, pipeline_mode=pl.Buffered(1))
+
+
+def mixer_specs(length, model, width):
+    blocks = model // width
+    row = pl.BlockSpec((None, length, model), lambda r, j, *_: (r, 0, 0))
+    part = pl.BlockSpec((None, length, width), lambda r, j, *_: (r, 0, j))
+
+    def columns(rows, offset):
+        return pl.BlockSpec((rows, width), lambda r, j, *_: (0, j + offset * blocks))
+
+    out_rows = pl.BlockSpec((width, model), lambda r, j, *_: (j, 0))
+    gain = once((1, model), lambda r, j, *_: (0, 0))
+    q = length // 4
+    tables = [once((2 * q, q), lambda r, j, *_: (0, 0)), once((6 * q, 2 * q), lambda r, j, *_: (0, 0))]
+    return blocks, row, part, columns, out_rows, gain, tables + tables
+
+
+def mixer_forward(x, split, keep, norm_gain, proj_in, short_filter, cond_filter, slope, shift, skip, proj_out, ffn_gain, tables, width=256):
+    rows, length, model = x.shape
+    blocks, row, part, columns, out_rows, gain, table_specs = mixer_specs(length, model, width)
+    one = columns(1, 0)
+    shape = jax.ShapeDtypeStruct
+    low, full = shape((rows, length, model), BF), shape((rows, length, model), F32)
+    pad = pltpu.VMEM((length + 8, width), F32)
+    flops = rows * (2 * length * model * (3 * model + model) + 2 * 3 * model * (2 * length) * length // 2)
+    return pl.pallas_call(
+        mixer_forward_kernel,
+        out_shape=[low, low, low, low, low, low, full, low],
+        grid_spec=pltpu.PrefetchScalarGridSpec(
+            num_scalar_prefetch=2,
+            grid=(rows, blocks),
+            in_specs=[row, gain, columns(model, 0), columns(model, 1), columns(model, 2), columns(3, 0), columns(3, 1), columns(3, 0), one, one, one, out_rows, gain] + table_specs,
+            out_specs=[row, part, part, part, part, part, row, row],
+            scratch_shapes=[pad, pad, pad] + [pltpu.VMEM((length, width), BF)] * 2 + [
+                pltpu.VMEM((2 * length, 2 * width), BF),
+                pltpu.VMEM((2 * length, 2 * width), F32),
+                pltpu.VMEM((2 * length, width), BF),
+                pltpu.VMEM((2 * length, width), F32),
+                pltpu.VMEM((length, width), F32),
+            ],
+        ),
+        compiler_params=pltpu.CompilerParams(dimension_semantics=("arbitrary", "arbitrary"), vmem_limit_bytes=LIMIT),
+        cost_estimate=pl.CostEstimate(flops=flops, bytes_accessed=rows * length * model * 20, transcendentals=rows * length * model),
+        name="mixer_forward",
+    )(split, keep, x, norm_gain, proj_in, proj_in, proj_in, short_filter, short_filter, cond_filter, slope, shift, skip, proj_out, ffn_gain, *tables)
+
+
+def normal_cdf_pdf(x):
+    z = jnp.abs(x) * ROOT_HALF
+    t = 1.0 / (1.0 + 0.3275911 * z)
+    e = jnp.exp(-z * z)
+    poly = t * (0.127414796 + t * (-0.142248368 + t * (0.7107068705 + t * (-0.7265760135 + t * 0.5307027145))))
+    tail = poly * e
+    return jnp.where(x >= 0, 1.0 - tail, tail), x * e * (1.0 / math.sqrt(2.0 * math.pi))
+
+
+def ffn_kernel(
+    sa_ref, og_ref, sat_ref, ogt_ref, wg_ref, wu_ref, wo_ref, out_ref, back_ref, grads_ref, gs, us, ds, hid, gg, ug
+):
+    j = pl.program_id(0)
+    tokens, model = sa_ref.shape
+    tile = gs.shape[0]
+    chunk = 32
+
+    @pl.when(j == 0)
+    def _():
+        def body(i):
+            out_ref[rows_of(i, tile), :] = jnp.zeros((tile, model), F32)
+            back_ref[rows_of(i, tile), :] = jnp.zeros((tile, model), F32)
+
+        loop(tokens // tile, body)
+
+    def body(i):
+        rows = rows_of(i, tile)
+        sa = sa_ref[rows, :]
+        gs[...] = mm(sa, wg_ref[...])
+        us[...] = mm(sa, wu_ref[...])
+        ds[...] = mm_t(og_ref[rows, :], wo_ref[...])
+        for c in range(tile // chunk):
+            part = slice(c * chunk, (c + 1) * chunk)
+            gate, up, dh = gs[part, :], us[part, :], ds[part, :]
+            cdf, xpdf = normal_cdf_pdf(gate)
+            act = gate * cdf
+            target = pl.ds(pl.multiple_of(i * tile + c * chunk, chunk), chunk)
+            hid[target, :] = (act * up).astype(BF)
+            gg[target, :] = (dh * up * (cdf + xpdf)).astype(BF)
+            ug[target, :] = (dh * act).astype(BF)
+        out_ref[rows, :] += mm(hid[rows, :], wo_ref[...])
+        back_ref[rows, :] += mm_t(gg[rows, :], wg_ref[...]) + mm_t(ug[rows, :], wu_ref[...])
+
+    loop(tokens // tile, body)
+    grads_ref[0] = mm(sat_ref[...], gg[...]).astype(BF)
+    grads_ref[1] = mm(sat_ref[...], ug[...]).astype(BF)
+    grads_ref[2] = mm(ogt_ref[...], hid[...]).astype(BF)
+
+
+def ffn_both(second_act, out_grad, ffn_in, ffn_out, width=512, tile=256):
+    tokens, model = second_act.shape
+    hidden = ffn_out.shape[0]
+    blocks = hidden // width
+    shape = jax.ShapeDtypeStruct
+    whole = once((tokens, model), lambda j: (0, 0))
+    turned = once((model, tokens), lambda j: (0, 0))
+    return pl.pallas_call(
+        ffn_kernel,
+        out_shape=[shape((tokens, model), F32), shape((tokens, model), F32), shape((3, model, hidden), BF)],
+        grid=(blocks,),
+        in_specs=[
+            whole, whole, turned, turned,
+            pl.BlockSpec((model, width), lambda j: (0, j)),
+            pl.BlockSpec((model, width), lambda j: (0, j + blocks)),
+            pl.BlockSpec((width, model), lambda j: (j, 0)),
+        ],
+        out_specs=[whole, whole, pl.BlockSpec((3, model, width), lambda j: (0, 0, j))],
+        scratch_shapes=[pltpu.VMEM((tile, width), F32)] * 3 + [pltpu.VMEM((tokens, width), BF)] * 3,
+        compiler_params=pltpu.CompilerParams(dimension_semantics=("arbitrary",), vmem_limit_bytes=LIMIT),
+        cost_estimate=pl.CostEstimate(flops=18 * tokens * model * hidden, bytes_accessed=tokens * model * 24 + model * hidden * 12, transcendentals=tokens * hidden),
+        name="ffn_both",
+    )(second_act, out_grad, second_act.T, out_grad.T, ffn_in, ffn_in, ffn_out)
+
+
+def norm_back_kernel(resid_ref, sum_ref, back_ref, og_ref, gain_ref, out_ref, grad_ref, low_ref, gain_grad_ref):
+    @pl.when(pl.program_id(0) == 0)
+    def _():
+        gain_grad_ref[...] = jnp.zeros_like(gain_grad_ref)
+
+    tile = 64
+
+    def body(i):
+        rows = rows_of(i, tile)
+        resid = resid_ref[rows, :]
+        n, scale = norm_stats(resid)
+        u = back_ref[rows, :]
+        ug = u * gain_ref[...]
+        un = u * n
+        part = ug - jnp.mean(ug, axis=-1, keepdims=True) - n * jnp.mean(ug * n, axis=-1, keepdims=True)
+        grad = og_ref[rows, :].astype(F32) + scale * part
+        out_ref[rows, :] = (resid + sum_ref[rows, :]).astype(BF)
+        grad_ref[rows, :] = grad
+        low_ref[rows, :] = grad.astype(BF)
+        gain_grad_ref[...] += jnp.sum(un.reshape(tile // 8, 8, un.shape[1]), axis=0)
+
+    loop(resid_ref.shape[0] // tile, body)
+
+
+def norm_back(resid, total, back, out_grad, gain, tile=512):
+    tokens, model = resid.shape
+    shape = jax.ShapeDtypeStruct
+    block = pl.BlockSpec((tile, model), lambda i: (i, 0))
+    fixed = pl.BlockSpec((8, model), lambda i: (0, 0))
+    return pl.pallas_call(
+        norm_back_kernel,
+        out_shape=[shape((tokens, model), BF), shape((tokens, model), F32), shape((tokens, model), BF), shape((8, model), F32)],
+        grid=(tokens // tile,),
+        in_specs=[block, block, block, block, pl.BlockSpec((1, model), lambda i: (0, 0))],
+        out_specs=[block, block, block, fixed],
+        compiler_params=pltpu.CompilerParams(dimension_semantics=("arbitrary",), vmem_limit_bytes=LIMIT),
+        cost_estimate=pl.CostEstimate(flops=20 * tokens * model, bytes_accessed=tokens * model * 22, transcendentals=tokens),
+        name="norm_back",
+    )(resid, total, back, out_grad, gain)
+
+
+def eight_sum(v):
+    return jnp.sum(v.reshape(v.shape[0] // 8, 8, v.shape[1]), axis=0)
+
+
+def mixer_backward_kernel(
+    split_ref, keep_ref, x_ref, grad_ref, low_ref, norm_gain_ref, q_ref, k_ref, v_ref, mixed_ref, wo_ref, wq_ref, wk_ref, wv_ref,
+    fq_ref, fv_ref, fk_ref, slope_ref, shift_ref, skip_ref, fwd_real_ref, fwd_ref, inv_real_ref, inv_ref,
+    in_grad_ref, pq_ref, pk_ref, pv_ref, gain_grad_ref, chan_ref,
+    qs, ks, vs, xv, xc, xy, y_s, spec_s, u_s, o_s, acc,
+):
+    r, j = pl.program_id(0), pl.program_id(1)
+    length, width = q_ref.shape
+    quarter = length // 4
+    split, keep = split_ref[r], keep_ref[r]
+    tile = 64
+    lanes = pl.ds(pl.multiple_of(j * width, width), width)
+
+    @pl.when((r == 0) & (j == 0))
+    def _():
+        gain_grad_ref[...] = jnp.zeros_like(gain_grad_ref)
+        chan_ref[...] = jnp.zeros_like(chan_ref)
+
+    @pl.when(j == 0)
+    def _():
+        acc[...] = jnp.zeros_like(acc)
+
+    for ref, source in ((qs, q_ref), (ks, k_ref), (vs, v_ref)):
+        ref[0:8, :] = jnp.zeros((8, width), F32)
+
+        def widen(i, ref=ref, source=source):
+            ref[pl.ds(pl.multiple_of(8 + i * tile, 8), tile), :] = source[rows_of(i, tile), :].astype(F32)
+
+        loop(length // tile, widen)
+
+    o_s[0:length, 0:width] = mm_t(low_ref[...], wo_ref[...])
+
+    def conv(i):
+        t = i * tile
+        rows = rows_of(i, tile)
+        kept = t + lax.broadcasted_iota(jnp.int32, (tile, width), 0) < keep
+        gated_grad = o_s[rows, 0:width]
+        low = (gated_grad * conv_back(qs, t, tile, fq_ref, split)).astype(BF)
+        xy[rows, :] = low
+        value = jnp.where(kept, conv_back(vs, t, tile, fv_ref, split), 0.0).astype(BF)
+        xv[rows, :] = value
+        xc[rows, :] = jnp.where(kept, conv_back(ks, t, tile, fk_ref, split), 0.0).astype(BF)
+        chan_ref[2, :, lanes] += eight_sum(low.astype(F32) * value.astype(F32))
+
+    loop(length // tile, conv)
+    butterfly(xv, y_s, 0, width, quarter)
+    butterfly(xc, y_s, width, width, quarter)
+    butterfly(xy, y_s, 2 * width, width, quarter)
+
+    def query(i):
+        rows = rows_of(i, tile)
+        qs[rows, :] = o_s[rows, 0:width] * mixed_ref[rows, :].astype(F32)
+
+    loop(length // tile, query)
+    blockwise(y_s, spec_s, fwd_real_ref, fwd_ref, quarter)
+
+    def bins(re, im, first):
+        n = 16
+        re, im = pl.ds(pl.multiple_of(re, n), n), pl.ds(pl.multiple_of(im, n), n)
+        vr, vi = spec_s[re, 0:width], spec_s[im, 0:width]
+        cr, ci = spec_s[re, width : 2 * width], spec_s[im, width : 2 * width]
+        yr, yi = spec_s[re, 2 * width : 3 * width], spec_s[im, 2 * width : 3 * width]
+        slope, shift = slope_ref[...], shift_ref[...]
+        rr, ii = cr * cr, ci * ci
+        if first:
+            edge = lax.broadcasted_iota(jnp.int32, (n, width), 0) == 0
+            pr, pi = jnp.where(edge, rr, rr + ii), jnp.where(edge, ii, rr + ii)
+            gr, gi = jax.nn.sigmoid(slope * pr + shift), jax.nn.sigmoid(slope * pi + shift)
+            ar = vr * yr + jnp.where(edge, 0.0, vi * yi)
+            ai = jnp.where(edge, -vi * yi, vi * yr - vr * yi)
+            br = ar * cr - jnp.where(edge, 0.0, ai * ci)
+            bi = jnp.where(edge, -ai * ci, br)
+            wr, wi = br * gr * (1.0 - gr), bi * gi * (1.0 - gi)
+            ws = jnp.where(edge, 0.5 * (wr + wi), wr)
+            wp = jnp.where(edge, 0.5 * (wr * pr + wi * pi), wr * pr)
+            hr, hi = gr * cr, gi * ci
+            er = hr * yr + jnp.where(edge, 0.0, hi * yi)
+            ei = jnp.where(edge, hi * yi, hr * yi - hi * yr)
+            dr = gr * ar + 2.0 * slope * wr * cr
+            di = 2.0 * slope * wi * ci - gi * ai
+        else:
+            p = rr + ii
+            g = jax.nn.sigmoid(slope * p + shift)
+            ar, ai = vr * yr + vi * yi, vi * yr - vr * yi
+            ws = (ar * cr - ai * ci) * (g * (1.0 - g))
+            wp = ws * p
+            hr, hi = g * cr, g * ci
+            er, ei = hr * yr + hi * yi, hr * yi - hi * yr
+            k = 2.0 * slope * ws
+            dr, di = g * ar + k * cr, k * ci - g * ai
+        chan_ref[0, :, lanes] += eight_sum(wp)
+        chan_ref[1, :, lanes] += eight_sum(ws)
+        u_s[re, 0:width] = er.astype(BF)
+        u_s[im, 0:width] = ei.astype(BF)
+        u_s[re, width : 2 * width] = dr.astype(BF)
+        u_s[im, width : 2 * width] = di.astype(BF)
+
+    each_bin(quarter, bins)
+    resynth(u_s, o_s, inv_real_ref, inv_ref, quarter)
+
+    def finish(i):
+        n = 32
+        value = recombine(o_s, slice(0, width), i, n, quarter)
+        cond = recombine(o_s, slice(width, 2 * width), i, n, quarter)
+        for k in range(4):
+            rows = pl.ds(pl.multiple_of(k * quarter + i * n, n), n)
+            kept = k * quarter + i * n + lax.broadcasted_iota(jnp.int32, (n, width), 0) < keep
+            grad = (value[k] + skip_ref[...] * xy[rows, :].astype(F32)).astype(BF).astype(F32)
+            vs[rows, :] = jnp.where(kept, grad, 0.0)
+            ks[rows, :] = jnp.where(kept, cond[k].astype(BF).astype(F32), 0.0)
+
+    loop(quarter // 32, finish)
+    for ref in (qs, ks, vs):
+        ref[length : length + 8, :] = jnp.zeros((8, width), F32)
+
+    for slot, (ref, source, f_ref, out_ref) in enumerate(((qs, q_ref, fq_ref, pq_ref), (vs, v_ref, fv_ref, pv_ref), (ks, k_ref, fk_ref, pk_ref))):
+
+        def adjoint(i, slot=slot, ref=ref, source=source, f_ref=f_ref, out_ref=out_ref):
+            t = i * tile
+            rows = rows_of(i, tile)
+            block = ref[pl.ds(pl.multiple_of(t, tile), tile + 8), :]
+            position = t + lax.broadcasted_iota(jnp.int32, (tile, width), 0)
+            g0 = block[0:tile]
+            g1 = jnp.where(position + 1 != split, block[1 : tile + 1], 0.0)
+            g2 = jnp.where((position + 2 != split) & (position + 1 != split), block[2 : tile + 2], 0.0)
+            s = source[rows, :].astype(F32)
+            out_ref[rows, :] = (f_ref[0:1, :] * g0 + f_ref[1:2, :] * g1 + f_ref[2:3, :] * g2).astype(BF)
+            for k, g in enumerate((g0, g1, g2)):
+                chan_ref[3 + 3 * slot + k, :, lanes] += eight_sum(g * s)
+
+        loop(length // tile, adjoint)
+
+    acc[...] += mm_t(pq_ref[...], wq_ref[...]) + mm_t(pk_ref[...], wk_ref[...]) + mm_t(pv_ref[...], wv_ref[...])
+
+    @pl.when(j == pl.num_programs(1) - 1)
+    def _():
+        def body(i):
+            rows = rows_of(i, tile)
+            n, scale = norm_stats(x_ref[rows, :].astype(F32))
+            u = acc[rows, :]
+            ug = u * norm_gain_ref[...]
+            part = ug - jnp.mean(ug, axis=-1, keepdims=True) - n * jnp.mean(ug * n, axis=-1, keepdims=True)
+            in_grad_ref[rows, :] = (grad_ref[rows, :] + scale * part).astype(in_grad_ref.dtype)
+            gain_grad_ref[...] += eight_sum(u * n)
+
+        loop(length // tile, body)
+
+
+def mixer_backward(x, resid_grad, branch_low, split, keep, norm_gain, q, k, v, mixed, proj_out, proj_in, short_filter, cond_filter, slope, shift, skip, tables, width=256):
+    rows, length, model = x.shape
+    blocks, row, part, columns, out_rows, gain, table_specs = mixer_specs(length, model, width)
+    one = columns(1, 0)
+    shape = jax.ShapeDtypeStruct
+    low = shape((rows, length, model), BF)
+    pad = pltpu.VMEM((length + 8, width), F32)
+    single = once((None, length, model), lambda r, j, *_: (r, 0, 0))
+    flops = rows * (2 * length * model * (3 * model + model) + 2 * 5 * model * (2 * length) * length // 2)
+    return pl.pallas_call(
+        mixer_backward_kernel,
+        out_shape=[low, low, low, low, shape((8, model), F32), shape((12, 8, model), F32)],
+        grid_spec=pltpu.PrefetchScalarGridSpec(
+            num_scalar_prefetch=2,
+            grid=(rows, blocks),
+            in_specs=[row, single, row, gain, part, part, part, part, out_rows, columns(model, 0), columns(model, 1), columns(model, 2), columns(3, 0), columns(3, 1), columns(3, 0), one, one, one] + table_specs,
+            out_specs=[row, part, part, part, once((8, model), lambda r, j, *_: (0, 0)), once((12, 8, model), lambda r, j, *_: (0, 0, 0))],
+            scratch_shapes=[pad, pad, pad] + [pltpu.VMEM((length, width), BF)] * 3 + [
+                pltpu.VMEM((2 * length, 3 * width), BF),
+                pltpu.VMEM((2 * length, 3 * width), F32),
+                pltpu.VMEM((2 * length, 2 * width), BF),
+                pltpu.VMEM((2 * length, 2 * width), F32),
+                pltpu.VMEM((length, model), F32),
+            ],
+        ),
+        compiler_params=pltpu.CompilerParams(dimension_semantics=("arbitrary", "arbitrary"), vmem_limit_bytes=LIMIT),
+        cost_estimate=pl.CostEstimate(flops=flops, bytes_accessed=rows * length * model * 26, transcendentals=rows * length * model),
+        name="mixer_backward",
+    )(split, keep, x, resid_grad, branch_low, norm_gain, q, k, v, mixed, proj_out, proj_in, proj_in, proj_in, short_filter, short_filter, cond_filter, slope, shift, skip, *tables)
+
+
+def layer_rows(x, split, keep, out_grad, p, tables):
+    rows, length, model = x.shape
+    norm_gain, proj_in, short_filter, cond_filter, slope, shift, skip, proj_out, ffn_gain, ffn_in, ffn_out = p
+    lift = lambda a: a.reshape(1, -1)
+    first, q, k, v, mixed, gated, resid, second = mixer_forward(
+        x, split, keep, lift(norm_gain), proj_in, short_filter, cond_filter, lift(slope), lift(shift), lift(skip), proj_out, lift(ffn_gain), tables
+    )
+    tokens = rows * length
+    flat = lambda a: a.reshape(tokens, model)
+    total, back, ffn_grads = ffn_both(flat(second), flat(out_grad), ffn_in, ffn_out)
+    output, resid_grad, branch_low, ffn_gain_part = norm_back(flat(resid), total, back, flat(out_grad), lift(ffn_gain))
+    shaped = lambda a: a.reshape(rows, length, model)
+    input_grad, pq, pk, pv, norm_gain_part, chan = mixer_backward(
+        x, shaped(resid_grad), shaped(branch_low), split, keep, lift(norm_gain), q, k, v, mixed, proj_out, proj_in, short_filter, cond_filter, lift(slope), lift(shift), lift(skip), tables
+    )
+    turn = lambda a, b: lax.dot_general(flat(a), flat(b), (((0,), (0,)), ((), ())), preferred_element_type=F32).astype(BF)
+    out_grads = turn(gated, branch_low)
+    in_grads = [turn(first, g) for g in (pq, pk, pv)]
+    small = jnp.sum(jnp.concatenate([ffn_gain_part[None], norm_gain_part[None], chan], 0), axis=1)
+    return shaped(output), input_grad, ffn_grads, out_grads, in_grads, small
+
+
+def per_device_rows(inputs, split_point, keep_mask, norm_gain, proj_in, short_filter, cond_filter, spec_slope, spec_shift, skip_gain, proj_out, ffn_gain, ffn_in, ffn_out, out_grad):
+    local_rows, local_len, model = inputs.shape
+    count = lax.axis_size("seq")
+    own = local_rows // count
+    first_row = lax.axis_index("seq") * own
+    gather = functools.partial(lax.all_to_all, axis_name="seq", split_axis=0, concat_axis=1, tiled=True)
+    scatter = functools.partial(lax.all_to_all, axis_name="seq", split_axis=1, concat_axis=0, tiled=True)
+    x = gather(inputs)
+    whole_grad = gather(out_grad)
+    keep = lax.dynamic_slice_in_dim(lax.psum(jnp.sum(keep_mask, axis=1), "seq"), first_row, own)
+    split = lax.dynamic_slice_in_dim(split_point, first_row, own)
+    params = (norm_gain, proj_in, short_filter, cond_filter, spec_slope, spec_shift, skip_gain, proj_out, ffn_gain, ffn_in, ffn_out)
+    length = local_len * count
+    tables = spectral_tables(length, lax.axis_index("seq") * (2 * length))
+    output, input_grad, ffn_grads, out_grads, in_grads, small = layer_rows(x, split, keep, whole_grad, params, tables)
+    output = scatter(output)
+    input_grad = scatter(input_grad).astype(F32)
+    ffn_share = lax.psum_scatter(ffn_grads, "rows", scatter_dimension=1, tiled=True)
+    ffn_share = lax.psum(ffn_share, "seq").astype(F32)
+    mix_share = lax.psum_scatter(jnp.concatenate(in_grads + [out_grads], axis=1), "rows", scatter_dimension=0, tiled=True)
+    mix_share = lax.psum(mix_share, "seq").astype(F32)
+    small = lax.psum(small, ("rows", "seq"))
+    scale = 1.0 / length
+    return (
+        output,
+        input_grad,
+        small[1],
+        mix_share[:, : 3 * model],
+        jnp.concatenate([small[5:8], small[8:11]], axis=1),
+        small[11:14],
+        small[2] * scale,
+        small[3] * scale,
+        small[4],
+        mix_share[:, 3 * model :],
+        small[0],
+        jnp.concatenate([ffn_share[0], ffn_share[1]], axis=1),
+        ffn_share[2].T,
+    )
+
+
 PRECISE = lax.Precision.HIGH
 
 
@@ -297,6 +937,12 @@
     )
 
 
+def per_device_any(*args):
+    rows, width = args[0].shape[0], args[0].shape[2]
+    even = rows % lax.axis_size("seq") == 0 and width % 256 == 0
+    return (per_device_rows if even else per_device)(*args)
+
+
 def solution(mesh):
     in_specs = (
         P("rows", "seq", None),
@@ -331,5 +977,5 @@
         P(None, "rows"),
     )
     return jax.shard_map(
-        per_device, mesh=mesh, in_specs=in_specs, out_specs=out_specs, check_vma=False
-    )
+        per_device_any, mesh=mesh, in_specs=in_specs, out_specs=out_specs, check_vma=False
+    )

time: 1540 us -> 761 us (0.49)
  matrix products: 630 us -> 17.5 us
  other arithmetic: 440 us -> 31.1 us
  Pallas kernels: 0 us -> 317 us
  local copies, waits for them, and re-layouts: 169 us -> 56.4 us
  waiting for transfers between devices: 167 us -> 194 us
  blocking collectives: 81 us -> 106 us
    dot_general x24 -> x4, matrix products: 630 us -> 17.5 us  [layer_rows(): lax.dot_general(flat(a), flat(b), (((0,), (0,)), ((), ())), preferred_ele...]
    pallas_call x0 -> x4, Pallas kernels: none -> 317 us  [the longest x1 124 us: ffn_both(): pl.pallas_call(ffn_kernel, out_shape=[shape((tokens, model), F32), shape(...]
    reduce_sum x9 -> x2, other arithmetic: 161 us -> 0.21 us  [the longest x1 0.12 us: per_device_rows(): jnp.sum(keep_mask, axis=1)]
    add_any x6 -> x0, other arithmetic: 113 us -> none  [the longest x1 46.8 us: glu_local(): jax.nn.gelu(both_parts[:, :hidden_width], approximate=False)]
    convert_element_type x10 -> x2, other arithmetic: 68 us -> 4.22 us  [the longest x1 4.05 us: per_device_rows(): input_grad = scatter(input_grad).astype(F32)]
    psum x1 -> x2, blocking collectives: 42.2 us -> 106 us  [the longest x1 68.4 us: per_device_rows(): small = lax.psum(small, ('rows', 'seq'))]
    add x3 -> x4, other arithmetic: 61.2 us -> 0.02 us  [the longest x3 0.01 us: spectral_tables(): c, sn = cos_sin(8 * m + r)]
    psum x1, waiting for transfers between devices: 0.01 us -> 44.6 us  [per_device_rows(): mix_share = lax.psum(mix_share, 'seq').astype(F32)]
  transfers between devices with their start and end apart: 9 -> 7, of which waited for: 3 -> 4; matrix products, arithmetic and copies ran while one was open for 21% -> 8% of each run, Pallas kernels for 0% -> 0%
where the time goes in v1:
time: 761 us; the launch traced here: 755 us
  Pallas kernels  317 us (42%)
  waiting for transfers between devices  194 us (25%)
  blocking collectives  106 us (14%)
  local copies, waits for them, and re-layouts  56.4 us (7%)
  other arithmetic  31.1 us (4%)
  starting transfers between devices  19.5 us (3%)
  matrix products  17.5 us (2%)
  between operations  14.3 us (2%)
    pallas_call x1, Pallas kernels, ffn_both(): pl.pallas_call(ffn_kernel, out_shape=[shape((tokens, model), F32), shape(...  124 us
    pallas_call x1, Pallas kernels, mixer_backward(): pl.pallas_call(mixer_backward_kernel, out_shape=[low, low, low, low, shap...  104 us
    reduce_scatter x1, waiting for transfers between devices, per_device_rows(): lax.psum_scatter(ffn_grads, 'rows', scatter_dimension=1, tiled=True)  103 us
    pallas_call x1, Pallas kernels, mixer_forward(): pl.pallas_call(mixer_forward_kernel, out_shape=[low, low, low, low, low,...  72.2 us
    psum x1, blocking collectives, per_device_rows(): small = lax.psum(small, ('rows', 'seq'))  68.4 us
    psum x1, waiting for transfers between devices, per_device_rows(): mix_share = lax.psum(mix_share, 'seq').astype(F32)  44.6 us
    psum x1, blocking collectives, per_device_rows(): lax.psum(jnp.sum(keep_mask, axis=1), 'seq')  37.2 us
    all_to_all x1, waiting for transfers between devices, per_device_rows(): output = scatter(output)  27.9 us
  transfers between devices with their start and end apart: 7, of which 4 were waited for; matrix products, arithmetic and copies ran while one was open for 8% of the time, Pallas kernels for 0%

profile of v1, /device:TPU:0, one launch (start us, length us, event | category | flops | bytes accessed | tf_op | source)
XLA Modules:
  0.0 755.0 jit_solution(4085578499201948806)
XLA Ops:
  7.3 4.4 all-to-all-start
  11.8 37.2 %psum.28 = s32[4]{0:T(128)S(1)} all-reduce(s32[4]{0:T(128)S(1)} %reduce_sum.18), channel_id=1, replica_groups=mesh['rows'=16,'seq'=2] {'seq'}, use_global_device_ids=true, to_apply=%region_1.0 | all-reduce | flops 4 | bytes 32 | tf_op jit(solution)/shard_map/psum | solution.py:618
  53.2 4.8 multiply_convert_fusion.1
  61.4 2.9 fusion.51
  65.9 5.2 all-to-all-start.1
  79.6 2.7 copy.48.fwd_ref
  89.1 17.9 %all-to-all-done.1 = bf16[4,512,768]{2,1,0:T(8,128)(2,1)} async-done(((bf16[4,512,768]{2,1,0:T(8,128)(2,1)}), bf16[4,512,768]{2,1,0:T(8,128)(2,1)}, u32[]{:S(2)}, u32[]{:S(2)}) %all-to-all-start.1) | async-done | bytes 3145760 | tf_op jit(solution)/shard_map/all_to_all | solution.py:617
  107.0 2.1 copy.51
  109.1 3.3 copy.53.ogt_ref
  112.4 72.2 %mixer_forward.1 = (bf16[2,1024,768]{2,1,0:T(8,128)(2,1)}, bf16[2,1024,768]{2,1,0:T(8,128)(2,1)}, bf16[2,1024,768]{2,1,0:T(8,128)(2,1)}, bf16[2,1024,768]{2,1,0:...) custom-call(s32[2]{0:T(128)} %dynamic_slice.6.split_ref, ...), custom_call_target="tpu_custom_call" | custom-call | flops 19327352832 | bytes 31457280 | tf_op jit(solution)/shard_map/mixer_forward/pallas_call | solution.py:267
  184.6 4.7 copy.69
  189.3 123.7 %ffn_both.1 = (f32[2048,768]{1,0:T(8,128)}, f32[2048,768]{1,0:T(8,128)}, bf16[3,768,3072]{2,1,0:T(8,128)(2,1)}) custom-call(bf16[2048,768]{1,0:T(8,128)(2,1)} %bitcast.69, bf16[2048,768]{1,0:T(8,128)(2,1)} %bitcast.58, bf16[768,2048]{1,0:T(8,128)(2,1)} %bitcast.70, bf16[768,2048]{1,0:T(8,128)(2,1)} %copy.53.ogt_ref, bf16[768,6144]{1,0:T(8,128)(2,1)} %wu_ref.1, ...), custom_call_target="tpu_custom_call" | custom-call | flops 86973087744 | bytes 66060288 | tf_op jit(solution)/shard_map/ffn_both/pallas_call | solution.py:345
  313.0 17.0 %norm_back.1 = (bf16[2048,768]{1,0:T(8,128)(2,1)}, f32[2048,768]{1,0:T(8,128)}, bf16[2048,768]{1,0:T(8,128)(2,1)}, f32[8,768]{1,0:T(8,128)}) custom-call(f32[2048,768]{1,0:T(8,128)} %bitcast.63, f32[2048,768]{1,0:T(8,128)} %get-tuple-element.36.sum_ref, f32[2048,768]{1,0:T(8,128)} %get-tuple-element.37.back_ref, bf16[2048,768]{1,0:T(8,128)(2,1)} %bitcast.59, ...), custom_call_target="tpu_custom_call" | custom-call | flops 31457280 | bytes 34603008 | tf_op jit(solution)/shard_map/norm_back/pallas_call | solution.py:392
  330.0 6.5 convolution_convert_fusion
  336.5 104.2 %mixer_backward.1 = (bf16[2,1024,768]{2,1,0:T(8,128)(2,1)}, bf16[2,1024,768]{2,1,0:T(8,128)(2,1)}, bf16[2,1024,768]{2,1,0:T(8,128)(2,1)}, bf16[2,1024,768]{2,1,0...) custom-call(s32[2]{0:T(128)} %dynamic_slice.6.split_ref, s32[2]{0:T(128)} %dynamic_slice.7.keep_ref, ...), custom_call_target="tpu_custom_call" | custom-call | flops 25769803776 | bytes 40894464 | tf_op jit(solution)/shard_map/mixer_backward/pallas_call | solution.py:565
  440.8 5.6 bitcast_convert_fusion.2
  446.4 2.7 bitcast_convert_fusion.1
  449.1 2.7 bitcast_convert_fusion
  451.8 2.4 pad_maximum_fusion
  454.2 6.7 copy.70
  463.3 4.9 copy.54
  468.2 4.1 all-to-all-start.2
  472.3 7.0 copy.59
  479.3 27.9 %all-to-all-done.2 = bf16[2,1024,768]{2,0,1:T(2,128)(2,1)S(1)} async-done(((bf16[2,1024,768]{2,0,1:T(2,128)(2,1)}), bf16[2,1024,768]{2,0,1:T(2,128)(2,1)S(1)}, u32[]{:S(2)}, u32[]{:S(2)}) %all-to-all-start.2) | async-done | bytes 3145760 | tf_op jit(solution)/shard_map/all_to_all | solution.py:624
  507.2 5.2 all-to-all-start.3
  512.6 68.4 %psum.29 = f32[14,768]{1,0:T(8,128)S(1)} all-reduce(f32[14,768]{1,0:T(8,128)S(1)} %maximum_reduce_fusion), channel_id=1, replica_groups=mesh['rows'=16,'seq'=2] {'rows','seq'}, use_global_device_ids=true, to_apply=%region_3.4 | all-reduce | flops 10752 | bytes 86016 | tf_op jit(solution)/shard_map/psum | solution.py:630
  581.0 2.1 copy.71
  583.1 102.9 %reduce-scatter.5.cloned.1.call-done = bf16[3,48,3072]{2,1,0:T(8,128)(2,1)} async-done(((bf16[3,768,3072]{2,1,0:T(8,128)(2,1)}), bf16[3,48,3072]{2,1,0:T(8,128)(2,1)}) %reduce-scatter.5.cloned.1.call-update) | async-done | bytes 884752 | tf_op jit(solution)/shard_map/reduce_scatter | solution.py:626
  687.9 2.1 copy.55
  690.0 4.0 convert_bitcast_fusion
  694.1 3.3 copy.60
  697.3 44.6 %all-reduce.3.cloned.1.call-done = (bf16[48,3072]{0,1:T(8,128)(2,1)}, bf16[3,48,3072]{2,1,0:T(8,128)(2,1)}) async-done(((bf16[48,3072]{0,1:T(8,128)(2,1)}, bf16[3,48,3072]{2,1,0:T(8,128)(2,1)}), (bf16[48,3072]{0,1:T(8,128)(2,1)}, bf16[3,48,3072]{2,1,0:T(8,128)(2,1)})) %all-reduce.3.cloned.1.call-update) | async-done | bytes 1179664 | tf_op jit(solution)/shard_map/psum | solution.py:629
  (97 shorter events, 35.2 us)
Async XLA Ops:
  7.2 4.5 copy-start.12
  7.2 41.8 %copy-start.18 = (s32[4]{0:T(128)S(1)}, s32[4]{0:T(128)}, u32[]{:S(2)}) copy-start(s32[4]{0:T(128)} %param.16) | copy-start | bytes 52
  7.2 43.1 %copy-start.13 = (f32[768]{0:T(1024)S(1)}, f32[768]{0:T(1024)}, u32[]{:S(2)}) copy-start(f32[768]{0:T(1024)} %param.18) | copy-start | bytes 9220
  7.2 43.6 %copy-start.14 = (f32[768]{0:T(1024)S(1)}, f32[768]{0:T(1024)}, u32[]{:S(2)}) copy-start(f32[768]{0:T(1024)} %param.22) | copy-start | bytes 9220
  7.2 44.2 %copy-start.15 = (f32[768]{0:T(1024)S(1)}, f32[768]{0:T(1024)}, u32[]{:S(2)}) copy-start(f32[768]{0:T(1024)} %param.23) | copy-start | bytes 9220
  7.2 44.8 %copy-start.16 = (f32[768]{0:T(1024)S(1)}, f32[768]{0:T(1024)}, u32[]{:S(2)}) copy-start(f32[768]{0:T(1024)} %param.24) | copy-start | bytes 9220
  7.2 45.4 %copy-start.17 = (f32[768]{0:T(1024)S(1)}, f32[768]{0:T(1024)}, u32[]{:S(2)}) copy-start(f32[768]{0:T(1024)} %param.26) | copy-start | bytes 9220
  7.3 58.6 %all-to-all-start = ((bf16[4,512,768]{2,1,0:T(8,128)(2,1)}), bf16[4,512,768]{2,1,0:T(8,128)(2,1)S(1)}, u32[]{:S(2)}, u32[]{:S(2)}) async-start(bf16[4,512,768]{2,1,0:T(8,128)(2,1)} %param.15), calls=%async_computation | async-start | bytes 6291456 | tf_op jit(solution)/shard_map/all_to_all | solution.py:616
  64.4 0.7 copy-start.2
  64.4 0.8 copy-start.6
  64.4 10.3 %copy-start.1 = (f32[256,256]{0,1:T(8,128)}, f32[256,256]{0,1:T(8,128)S(1)}, u32[]{:S(2)}) copy-start(f32[256,256]{0,1:T(8,128)S(1)} %get-tuple-element.110) | copy-start | bytes 786436
  65.9 41.1 %all-to-all-start.1 = ((bf16[4,512,768]{2,1,0:T(8,128)(2,1)}), bf16[4,512,768]{2,1,0:T(8,128)(2,1)}, u32[]{:S(2)}, u32[]{:S(2)}) async-start(bf16[4,512,768]{2,1,0:T(8,128)(2,1)} %param.29), calls=%async_computation.1 | async-start | bytes 6291456 | tf_op jit(solution)/shard_map/all_to_all | solution.py:617
  71.1 509.8 %reduce-scatter.7.cloned.1.call-start = ((), (), s32[]{:S(2)}) async-start(), calls=%async_computation.7 | async-start | bytes 5013504
  77.4 0.7 copy-start.5
  77.4 1.4 copy-start.4
  109.1 3.4 copy-start
  440.7 5.7 copy-start.19
  440.7 5.7 copy-start.21
  446.4 2.7 copy-start.20
  449.1 2.7 copy-start.7
  460.9 225.1 %reduce-scatter.5.cloned.1.call-start = ((), (), s32[]{:S(2)}) async-start(), calls=%async_computation.6 | async-start | bytes 15040512 | tf_op jit(solution)/shard_map/reduce_scatter | solution.py:626
  461.4 1.9 copy-start.3
  468.2 38.9 %all-to-all-start.2 = ((bf16[2,1024,768]{2,0,1:T(2,128)(2,1)}), bf16[2,1024,768]{2,0,1:T(2,128)(2,1)S(1)}, u32[]{:S(2)}, u32[]{:S(2)}) async-start(bf16[2,1024,768]{2,0,1:T(2,128)(2,1)} %copy.54), calls=%async_computation.2 | async-start | bytes 6291456 | tf_op jit(solution)/shard_map/all_to_all | solution.py:624
  479.3 33.2 %copy-start.9 = (f32[12,8,768]{2,1,0:T(8,128)S(1)}, f32[12,8,768]{2,1,0:T(8,128)}, u32[]{:S(2)}) copy-start(f32[12,8,768]{2,1,0:T(8,128)} %get-tuple-element.48) | copy-start | bytes 884740
  479.3 33.2 %copy-start.10 = (f32[8,768]{1,0:T(8,128)S(1)}, f32[8,768]{1,0:T(8,128)}, u32[]{:S(2)}) copy-start(f32[8,768]{1,0:T(8,128)} %get-tuple-element.46) | copy-start | bytes 73732
  479.3 33.2 %copy-start.11 = (f32[8,768]{1,0:T(8,128)S(1)}, f32[8,768]{1,0:T(8,128)}, u32[]{:S(2)}) copy-start(f32[8,768]{1,0:T(8,128)} %get-tuple-element.47) | copy-start | bytes 73732
  507.2 182.8 %all-to-all-start.3 = ((bf16[2,1024,768]{2,0,1:T(2,128)(2,1)}), bf16[2,1024,768]{2,0,1:T(2,128)(2,1)}, u32[]{:S(2)}, u32[]{:S(2)}) async-start(bf16[2,1024,768]{2,0,1:T(2,128)(2,1)} %copy.59), calls=%async_computation.3 | async-start | bytes 6291456 | tf_op jit(solution)/shard_map/all_to_all | solution.py:625
  512.4 229.5 %all-reduce.3.cloned.1.call-start = ((), (), s32[]{:S(2)}) async-start(), calls=%async_computation.8 | async-start | bytes 3342336 | tf_op jit(solution)/shard_map/psum | solution.py:629
  741.9 4.1 copy-start.8
Sparse Core Ops, SparseCore 0:
  461.0 75.7 reduce-scatter.6
  541.0 144.9 reduce-scatter.4
  689.0 52.8 all-reduce.2

commit v2 on v1

--- a/solution.py
+++ b/solution.py
@@ -335,10 +335,12 @@
     grads_ref[2] = mm(ogt_ref[...], hid[...]).astype(BF)
 
 
-def ffn_both(second_act, out_grad, ffn_in, ffn_out, width=512, tile=256):
+def ffn_both(second_act, out_grad, second_turned, grad_turned, ffn_in, ffn_out, piece, pieces, width=512, tile=256):
     tokens, model = second_act.shape
-    hidden = ffn_out.shape[0]
-    blocks = hidden // width
+    total_blocks = ffn_out.shape[0] // width
+    blocks = total_blocks // pieces
+    first = piece * blocks
+    hidden = blocks * width
     shape = jax.ShapeDtypeStruct
     whole = once((tokens, model), lambda j: (0, 0))
     turned = once((model, tokens), lambda j: (0, 0))
@@ -348,19 +350,22 @@
         grid=(blocks,),
         in_specs=[
             whole, whole, turned, turned,
-            pl.BlockSpec((model, width), lambda j: (0, j)),
-            pl.BlockSpec((model, width), lambda j: (0, j + blocks)),
-            pl.BlockSpec((width, model), lambda j: (j, 0)),
+            pl.BlockSpec((model, width), lambda j: (0, j + first)),
+            pl.BlockSpec((model, width), lambda j: (0, j + first + total_blocks)),
+            pl.BlockSpec((width, model), lambda j: (j + first, 0)),
         ],
         out_specs=[whole, whole, pl.BlockSpec((3, model, width), lambda j: (0, 0, j))],
         scratch_shapes=[pltpu.VMEM((tile, width), F32)] * 3 + [pltpu.VMEM((tokens, width), BF)] * 3,
         compiler_params=pltpu.CompilerParams(dimension_semantics=("arbitrary",), vmem_limit_bytes=LIMIT),
         cost_estimate=pl.CostEstimate(flops=18 * tokens * model * hidden, bytes_accessed=tokens * model * 24 + model * hidden * 12, transcendentals=tokens * hidden),
         name="ffn_both",
-    )(second_act, out_grad, second_act.T, out_grad.T, ffn_in, ffn_in, ffn_out)
-
-
-def norm_back_kernel(resid_ref, sum_ref, back_ref, og_ref, gain_ref, out_ref, grad_ref, low_ref, gain_grad_ref):
+    )(second_act, out_grad, second_turned, grad_turned, ffn_in, ffn_in, ffn_out)
+
+
+def norm_back_kernel(pieces, resid_ref, *refs):
+    sum_refs, back_refs = refs[:pieces], refs[pieces : 2 * pieces]
+    og_ref, gain_ref, out_ref, grad_ref, low_ref, gain_grad_ref = refs[2 * pieces :]
+
     @pl.when(pl.program_id(0) == 0)
     def _():
         gain_grad_ref[...] = jnp.zeros_like(gain_grad_ref)
@@ -371,12 +376,12 @@
         rows = rows_of(i, tile)
         resid = resid_ref[rows, :]
         n, scale = norm_stats(resid)
-        u = back_ref[rows, :]
+        u = sum(ref[rows, :] for ref in back_refs)
         ug = u * gain_ref[...]
         un = u * n
         part = ug - jnp.mean(ug, axis=-1, keepdims=True) - n * jnp.mean(ug * n, axis=-1, keepdims=True)
         grad = og_ref[rows, :].astype(F32) + scale * part
-        out_ref[rows, :] = (resid + sum_ref[rows, :]).astype(BF)
+        out_ref[rows, :] = (resid + sum(ref[rows, :] for ref in sum_refs)).astype(BF)
         grad_ref[rows, :] = grad
         low_ref[rows, :] = grad.astype(BF)
         gain_grad_ref[...] += jnp.sum(un.reshape(tile // 8, 8, un.shape[1]), axis=0)
@@ -384,21 +389,22 @@
     loop(resid_ref.shape[0] // tile, body)
 
 
-def norm_back(resid, total, back, out_grad, gain, tile=512):
+def norm_back(resid, totals, backs, out_grad, gain, tile=512):
     tokens, model = resid.shape
+    pieces = len(totals)
     shape = jax.ShapeDtypeStruct
     block = pl.BlockSpec((tile, model), lambda i: (i, 0))
     fixed = pl.BlockSpec((8, model), lambda i: (0, 0))
     return pl.pallas_call(
-        norm_back_kernel,
+        functools.partial(norm_back_kernel, pieces),
         out_shape=[shape((tokens, model), BF), shape((tokens, model), F32), shape((tokens, model), BF), shape((8, model), F32)],
         grid=(tokens // tile,),
-        in_specs=[block, block, block, block, pl.BlockSpec((1, model), lambda i: (0, 0))],
+        in_specs=[block] * (2 * pieces + 2) + [pl.BlockSpec((1, model), lambda i: (0, 0))],
         out_specs=[block, block, block, fixed],
         compiler_params=pltpu.CompilerParams(dimension_semantics=("arbitrary",), vmem_limit_bytes=LIMIT),
         cost_estimate=pl.CostEstimate(flops=20 * tokens * model, bytes_accessed=tokens * model * 22, transcendentals=tokens),
         name="norm_back",
-    )(resid, total, back, out_grad, gain)
+    )(resid, *totals, *backs, out_grad, gain)
 
 
 def eight_sum(v):
@@ -406,26 +412,20 @@
 
 
 def mixer_backward_kernel(
-    split_ref, keep_ref, x_ref, grad_ref, low_ref, norm_gain_ref, q_ref, k_ref, v_ref, mixed_ref, wo_ref, wq_ref, wk_ref, wv_ref,
+    split_ref, keep_ref, low_ref, q_ref, k_ref, v_ref, mixed_ref, wo_ref,
     fq_ref, fv_ref, fk_ref, slope_ref, shift_ref, skip_ref, fwd_real_ref, fwd_ref, inv_real_ref, inv_ref,
-    in_grad_ref, pq_ref, pk_ref, pv_ref, gain_grad_ref, chan_ref,
-    qs, ks, vs, xv, xc, xy, y_s, spec_s, u_s, o_s, acc,
+    p_ref, chan_ref,
+    qs, ks, vs, xv, xc, xy, y_s, spec_s, u_s, o_s,
 ):
-    r, j = pl.program_id(0), pl.program_id(1)
+    r = pl.program_id(0)
     length, width = q_ref.shape
     quarter = length // 4
     split, keep = split_ref[r], keep_ref[r]
     tile = 64
-    lanes = pl.ds(pl.multiple_of(j * width, width), width)
-
-    @pl.when((r == 0) & (j == 0))
+
+    @pl.when(r == 0)
     def _():
-        gain_grad_ref[...] = jnp.zeros_like(gain_grad_ref)
         chan_ref[...] = jnp.zeros_like(chan_ref)
-
-    @pl.when(j == 0)
-    def _():
-        acc[...] = jnp.zeros_like(acc)
 
     for ref, source in ((qs, q_ref), (ks, k_ref), (vs, v_ref)):
         ref[0:8, :] = jnp.zeros((8, width), F32)
@@ -447,7 +447,7 @@
         value = jnp.where(kept, conv_back(vs, t, tile, fv_ref, split), 0.0).astype(BF)
         xv[rows, :] = value
         xc[rows, :] = jnp.where(kept, conv_back(ks, t, tile, fk_ref, split), 0.0).astype(BF)
-        chan_ref[2, :, lanes] += eight_sum(low.astype(F32) * value.astype(F32))
+        chan_ref[2, :, :] += eight_sum(low.astype(F32) * value.astype(F32))
 
     loop(length // tile, conv)
     butterfly(xv, y_s, 0, width, quarter)
@@ -495,8 +495,8 @@
             er, ei = hr * yr + hi * yi, hr * yi - hi * yr
             k = 2.0 * slope * ws
             dr, di = g * ar + k * cr, k * ci - g * ai
-        chan_ref[0, :, lanes] += eight_sum(wp)
-        chan_ref[1, :, lanes] += eight_sum(ws)
+        chan_ref[0, :, :] += eight_sum(wp)
+        chan_ref[1, :, :] += eight_sum(ws)
         u_s[re, 0:width] = er.astype(BF)
         u_s[im, 0:width] = ei.astype(BF)
         u_s[re, width : 2 * width] = dr.astype(BF)
@@ -520,9 +520,9 @@
     for ref in (qs, ks, vs):
         ref[length : length + 8, :] = jnp.zeros((8, width), F32)
 
-    for slot, (ref, source, f_ref, out_ref) in enumerate(((qs, q_ref, fq_ref, pq_ref), (vs, v_ref, fv_ref, pv_ref), (ks, k_ref, fk_ref, pk_ref))):
-
-        def adjoint(i, slot=slot, ref=ref, source=source, f_ref=f_ref, out_ref=out_ref):
+    for slot, (ref, source, f_ref) in enumerate(((qs, q_ref, fq_ref), (vs, v_ref, fv_ref), (ks, k_ref, fk_ref))):
+
+        def adjoint(i, slot=slot, ref=ref, source=source, f_ref=f_ref):
             t = i * tile
             rows = rows_of(i, tile)
             block = ref[pl.ds(pl.multiple_of(t, tile), tile + 8), :]
@@ -531,118 +531,262 @@
             g1 = jnp.where(position + 1 != split, block[1 : tile + 1], 0.0)
             g2 = jnp.where((position + 2 != split) & (position + 1 != split), block[2 : tile + 2], 0.0)
             s = source[rows, :].astype(F32)
-            out_ref[rows, :] = (f_ref[0:1, :] * g0 + f_ref[1:2, :] * g1 + f_ref[2:3, :] * g2).astype(BF)
+            place = slice((0, 2, 1)[slot] * width, ((0, 2, 1)[slot] + 1) * width)
+            p_ref[rows, place] = (f_ref[0:1, :] * g0 + f_ref[1:2, :] * g1 + f_ref[2:3, :] * g2).astype(BF)
             for k, g in enumerate((g0, g1, g2)):
-                chan_ref[3 + 3 * slot + k, :, lanes] += eight_sum(g * s)
+                chan_ref[3 + 3 * slot + k, :, :] += eight_sum(g * s)
 
         loop(length // tile, adjoint)
 
-    acc[...] += mm_t(pq_ref[...], wq_ref[...]) + mm_t(pk_ref[...], wk_ref[...]) + mm_t(pv_ref[...], wv_ref[...])
-
-    @pl.when(j == pl.num_programs(1) - 1)
-    def _():
-        def body(i):
-            rows = rows_of(i, tile)
-            n, scale = norm_stats(x_ref[rows, :].astype(F32))
-            u = acc[rows, :]
-            ug = u * norm_gain_ref[...]
-            part = ug - jnp.mean(ug, axis=-1, keepdims=True) - n * jnp.mean(ug * n, axis=-1, keepdims=True)
-            in_grad_ref[rows, :] = (grad_ref[rows, :] + scale * part).astype(in_grad_ref.dtype)
-            gain_grad_ref[...] += eight_sum(u * n)
-
-        loop(length // tile, body)
-
-
-def mixer_backward(x, resid_grad, branch_low, split, keep, norm_gain, q, k, v, mixed, proj_out, proj_in, short_filter, cond_filter, slope, shift, skip, tables, width=256):
-    rows, length, model = x.shape
-    blocks, row, part, columns, out_rows, gain, table_specs = mixer_specs(length, model, width)
+
+def mixer_backward(branch_low, split, keep, q, k, v, mixed, proj_out, short_filter, cond_filter, slope, shift, skip, tables, block, width=256):
+    rows, length, model = q.shape
+    blocks = model // width
+    shape = jax.ShapeDtypeStruct
+    pad = pltpu.VMEM((length + 8, width), F32)
+    quarter = length // 4
+    row = pl.BlockSpec((None, length, model), lambda r, *_: (r, 0, 0))
+    part = pl.BlockSpec((None, length, width), lambda r, *_: (r, 0, block))
+
+    def columns(size, offset):
+        return pl.BlockSpec((size, width), lambda r, *_: (0, block + offset * blocks))
+
+    fixed = lambda r, *_: (0, 0)
+    table_specs = [once((2 * quarter, quarter), fixed), once((6 * quarter, 2 * quarter), fixed)] * 2
     one = columns(1, 0)
-    shape = jax.ShapeDtypeStruct
-    low = shape((rows, length, model), BF)
-    pad = pltpu.VMEM((length + 8, width), F32)
-    single = once((None, length, model), lambda r, j, *_: (r, 0, 0))
-    flops = rows * (2 * length * model * (3 * model + model) + 2 * 5 * model * (2 * length) * length // 2)
+    flops = rows * (2 * length * model * width + 2 * 5 * width * (2 * length) * length // 2)
     return pl.pallas_call(
         mixer_backward_kernel,
-        out_shape=[low, low, low, low, shape((8, model), F32), shape((12, 8, model), F32)],
+        out_shape=[shape((rows, length, 3 * width), BF), shape((12, 8, width), F32)],
         grid_spec=pltpu.PrefetchScalarGridSpec(
             num_scalar_prefetch=2,
-            grid=(rows, blocks),
-            in_specs=[row, single, row, gain, part, part, part, part, out_rows, columns(model, 0), columns(model, 1), columns(model, 2), columns(3, 0), columns(3, 1), columns(3, 0), one, one, one] + table_specs,
-            out_specs=[row, part, part, part, once((8, model), lambda r, j, *_: (0, 0)), once((12, 8, model), lambda r, j, *_: (0, 0, 0))],
+            grid=(rows,),
+            in_specs=[row, part, part, part, part, pl.BlockSpec((width, model), lambda r, *_: (block, 0)), columns(3, 0), columns(3, 1), columns(3, 0), one, one, one] + table_specs,
+            out_specs=[pl.BlockSpec((None, length, 3 * width), lambda r, *_: (r, 0, 0)), once((12, 8, width), lambda r, *_: (0, 0, 0))],
             scratch_shapes=[pad, pad, pad] + [pltpu.VMEM((length, width), BF)] * 3 + [
                 pltpu.VMEM((2 * length, 3 * width), BF),
                 pltpu.VMEM((2 * length, 3 * width), F32),
                 pltpu.VMEM((2 * length, 2 * width), BF),
                 pltpu.VMEM((2 * length, 2 * width), F32),
-                pltpu.VMEM((length, model), F32),
             ],
         ),
-        compiler_params=pltpu.CompilerParams(dimension_semantics=("arbitrary", "arbitrary"), vmem_limit_bytes=LIMIT),
-        cost_estimate=pl.CostEstimate(flops=flops, bytes_accessed=rows * length * model * 26, transcendentals=rows * length * model),
+        compiler_params=pltpu.CompilerParams(dimension_semantics=("arbitrary",), vmem_limit_bytes=LIMIT),
+        cost_estimate=pl.CostEstimate(flops=flops, bytes_accessed=rows * length * (model * 2 + width * 14), transcendentals=rows * length * width),
         name="mixer_backward",
-    )(split, keep, x, resid_grad, branch_low, norm_gain, q, k, v, mixed, proj_out, proj_in, proj_in, proj_in, short_filter, short_filter, cond_filter, slope, shift, skip, *tables)
-
-
-def layer_rows(x, split, keep, out_grad, p, tables):
-    rows, length, model = x.shape
-    norm_gain, proj_in, short_filter, cond_filter, slope, shift, skip, proj_out, ffn_gain, ffn_in, ffn_out = p
-    lift = lambda a: a.reshape(1, -1)
-    first, q, k, v, mixed, gated, resid, second = mixer_forward(
-        x, split, keep, lift(norm_gain), proj_in, short_filter, cond_filter, lift(slope), lift(shift), lift(skip), proj_out, lift(ffn_gain), tables
-    )
-    tokens = rows * length
-    flat = lambda a: a.reshape(tokens, model)
-    total, back, ffn_grads = ffn_both(flat(second), flat(out_grad), ffn_in, ffn_out)
-    output, resid_grad, branch_low, ffn_gain_part = norm_back(flat(resid), total, back, flat(out_grad), lift(ffn_gain))
-    shaped = lambda a: a.reshape(rows, length, model)
-    input_grad, pq, pk, pv, norm_gain_part, chan = mixer_backward(
-        x, shaped(resid_grad), shaped(branch_low), split, keep, lift(norm_gain), q, k, v, mixed, proj_out, proj_in, short_filter, cond_filter, lift(slope), lift(shift), lift(skip), tables
-    )
-    turn = lambda a, b: lax.dot_general(flat(a), flat(b), (((0,), (0,)), ((), ())), preferred_element_type=F32).astype(BF)
-    out_grads = turn(gated, branch_low)
-    in_grads = [turn(first, g) for g in (pq, pk, pv)]
-    small = jnp.sum(jnp.concatenate([ffn_gain_part[None], norm_gain_part[None], chan], 0), axis=1)
-    return shaped(output), input_grad, ffn_grads, out_grads, in_grads, small
+    )(split, keep, branch_low, q, k, v, mixed, proj_out, short_filter, short_filter, cond_filter, slope, shift, skip, *tables)
+
+
+def input_back_kernel(blocks, x_ref, grad_ref, gain_ref, w_ref, *refs):
+    p_refs, (in_grad_ref, gain_grad_ref, acc) = refs[:blocks], refs[blocks:]
+    model = x_ref.shape[1]
+    width = model // blocks
+    tile = 64
+
+    @pl.when(pl.program_id(0) == 0)
+    def _():
+        gain_grad_ref[...] = jnp.zeros_like(gain_grad_ref)
+
+    total = None
+    for b, p_ref in enumerate(p_refs):
+        for k in range(3):
+            lanes = slice(k * model + b * width, k * model + (b + 1) * width)
+            term = mm_t(p_ref[:, k * width : (k + 1) * width], w_ref[:, lanes])
+            total = term if total is None else total + term
+    acc[...] = total
+
+    def body(i):
+        rows = rows_of(i, tile)
+        n, scale = norm_stats(x_ref[rows, :].astype(F32))
+        u = acc[rows, :]
+        ug = u * gain_ref[...]
+        part = ug - jnp.mean(ug, axis=-1, keepdims=True) - n * jnp.mean(ug * n, axis=-1, keepdims=True)
+        in_grad_ref[rows, :] = (grad_ref[rows, :] + scale * part).astype(in_grad_ref.dtype)
+        gain_grad_ref[...] += eight_sum(u * n)
+
+    loop(x_ref.shape[0] // tile, body)
+
+
+def input_back(x, resid_grad, gain, proj_in, parts, tile=512):
+    tokens, model = x.shape
+    shape = jax.ShapeDtypeStruct
+    block = pl.BlockSpec((tile, model), lambda i: (i, 0))
+    return pl.pallas_call(
+        functools.partial(input_back_kernel, len(parts)),
+        out_shape=[shape((tokens, model), BF), shape((8, model), F32)],
+        grid=(tokens // tile,),
+        in_specs=[block, block, once((1, model), lambda i: (0, 0)), once((model, 3 * model), lambda i: (0, 0))] + [block] * len(parts),
+        out_specs=[block, pl.BlockSpec((8, model), lambda i: (0, 0))],
+        scratch_shapes=[pltpu.VMEM((tile, model), F32)],
+        compiler_params=pltpu.CompilerParams(dimension_semantics=("arbitrary",), vmem_limit_bytes=LIMIT),
+        cost_estimate=pl.CostEstimate(flops=6 * tokens * model * model, bytes_accessed=tokens * model * 14, transcendentals=tokens),
+        name="input_back",
+    )(x, resid_grad, gain, proj_in, *parts)
+
+
+def turn(a, b):
+    return lax.dot_general(a, b, (((0,), (0,)), ((), ())), preferred_element_type=F32).astype(BF)
+
+
+def after(value, earlier):
+    return lax.optimization_barrier((value, earlier))[0]
+
+
+def exchange_sum_kernel(rows, seq, x_ref, out_ref, slots, total, send_sem, recv_sem):
+    r, s = lax.axis_index("rows"), lax.axis_index("seq")
+    partners = []
+    bit = 1
+    while bit < rows:
+        partners.append((r + bit - 2 * bit * (lax.rem(r // bit, 2)), s))
+        bit *= 2
+    bit = 1
+    while bit < seq:
+        partners.append((r, s + bit - 2 * bit * (lax.rem(s // bit, 2))))
+        bit *= 2
+    barrier = pltpu.get_barrier_semaphore()
+    for partner in partners:
+        pl.semaphore_signal(barrier, inc=1, device_id=partner, device_id_type=pl.DeviceIdType.MESH)
+    pl.semaphore_wait(barrier, len(partners))
+    total[0] = x_ref[...]
+    for step, partner in enumerate(partners):
+        copy = pltpu.make_async_remote_copy(
+            src_ref=total.at[step], dst_ref=slots.at[step], send_sem=send_sem.at[step], recv_sem=recv_sem.at[step],
+            device_id=partner, device_id_type=pl.DeviceIdType.MESH,
+        )
+        copy.start()
+        copy.wait()
+        total[step + 1] = total[step] + slots[step]
+    out_ref[...] = total[len(partners)]
+
+
+def power_of_two(n):
+    return n & (n - 1) == 0
+
+
+def exchange_sum(value):
+    rows, seq = lax.axis_size("rows"), lax.axis_size("seq")
+    if not (power_of_two(rows) and power_of_two(seq)):
+        return lax.psum(value, ("rows", "seq"))
+    steps = (rows.bit_length() - 1) + (seq.bit_length() - 1)
+    return pl.pallas_call(
+        functools.partial(exchange_sum_kernel, rows, seq),
+        out_shape=jax.ShapeDtypeStruct(value.shape, value.dtype),
+        in_specs=[pl.BlockSpec(memory_space=pltpu.VMEM)],
+        out_specs=pl.BlockSpec(memory_space=pltpu.VMEM),
+        scratch_shapes=[
+            pltpu.VMEM((steps, *value.shape), value.dtype),
+            pltpu.VMEM((steps + 1, *value.shape), value.dtype),
+            pltpu.SemaphoreType.DMA((steps,)),
+            pltpu.SemaphoreType.DMA((steps,)),
+        ],
+        compiler_params=pltpu.CompilerParams(collective_id=7, has_side_effects=True),
+        name="exchange_sum",
+    )(value)
+
+
+def swapped(value):
+    count = lax.axis_size("seq")
+    return lax.ppermute(value, "seq", [(i, (i + 1) % count) for i in range(count)])
+
+
+def gather_rows(value):
+    if lax.axis_size("seq") != 2:
+        return lax.all_to_all(value, "seq", split_axis=0, concat_axis=1, tiled=True)
+    s = lax.axis_index("seq")
+    own = value.shape[0] // 2
+    mine = lax.dynamic_slice_in_dim(value, s * own, own)
+    other = swapped(lax.dynamic_slice_in_dim(value, (1 - s) * own, own))
+    return jnp.concatenate([jnp.where(s == 0, mine, other), jnp.where(s == 0, other, mine)], axis=1)
+
+
+def scatter_rows(value):
+    if lax.axis_size("seq") != 2:
+        return lax.all_to_all(value, "seq", split_axis=1, concat_axis=0, tiled=True)
+    s = lax.axis_index("seq")
+    part = value.shape[1] // 2
+    mine = lax.dynamic_slice_in_dim(value, s * part, part, axis=1)
+    other = swapped(lax.dynamic_slice_in_dim(value, (1 - s) * part, part, axis=1))
+    return jnp.concatenate([jnp.where(s == 0, mine, other), jnp.where(s == 0, other, mine)], axis=0)
+
+
+def seq_sum(value):
+    if lax.axis_size("seq") != 2:
+        return lax.psum(value, "seq").astype(F32)
+    return value.astype(F32) + swapped(value).astype(F32)
 
 
 def per_device_rows(inputs, split_point, keep_mask, norm_gain, proj_in, short_filter, cond_filter, spec_slope, spec_shift, skip_gain, proj_out, ffn_gain, ffn_in, ffn_out, out_grad):
     local_rows, local_len, model = inputs.shape
     count = lax.axis_size("seq")
     own = local_rows // count
+    length = local_len * count
+    tokens = own * length
+    width = 256
     first_row = lax.axis_index("seq") * own
-    gather = functools.partial(lax.all_to_all, axis_name="seq", split_axis=0, concat_axis=1, tiled=True)
-    scatter = functools.partial(lax.all_to_all, axis_name="seq", split_axis=1, concat_axis=0, tiled=True)
-    x = gather(inputs)
-    whole_grad = gather(out_grad)
-    keep = lax.dynamic_slice_in_dim(lax.psum(jnp.sum(keep_mask, axis=1), "seq"), first_row, own)
+    flat = lambda a: a.reshape(tokens, model)
+    shaped = lambda a: a.reshape(own, length, model)
+    lift = lambda a: a.reshape(1, -1)
+
+    x = gather_rows(inputs)
+    kept = jnp.sum(keep_mask, axis=1)
+    kept = kept + swapped(kept) if count == 2 else lax.psum(kept, "seq")
+    keep = lax.dynamic_slice_in_dim(kept, first_row, own)
     split = lax.dynamic_slice_in_dim(split_point, first_row, own)
-    params = (norm_gain, proj_in, short_filter, cond_filter, spec_slope, spec_shift, skip_gain, proj_out, ffn_gain, ffn_in, ffn_out)
-    length = local_len * count
+    whole_grad = flat(gather_rows(after(out_grad, x)))
     tables = spectral_tables(length, lax.axis_index("seq") * (2 * length))
-    output, input_grad, ffn_grads, out_grads, in_grads, small = layer_rows(x, split, keep, whole_grad, params, tables)
-    output = scatter(output)
-    input_grad = scatter(input_grad).astype(F32)
-    ffn_share = lax.psum_scatter(ffn_grads, "rows", scatter_dimension=1, tiled=True)
-    ffn_share = lax.psum(ffn_share, "seq").astype(F32)
-    mix_share = lax.psum_scatter(jnp.concatenate(in_grads + [out_grads], axis=1), "rows", scatter_dimension=0, tiled=True)
-    mix_share = lax.psum(mix_share, "seq").astype(F32)
-    small = lax.psum(small, ("rows", "seq"))
+    slope, shift, skip = lift(spec_slope), lift(spec_shift), lift(skip_gain)
+
+    first, q, k, v, mixed, gated, resid, second = mixer_forward(
+        x, split, keep, lift(norm_gain), proj_in, short_filter, cond_filter, slope, shift, skip, proj_out, lift(ffn_gain), tables
+    )
+    second = flat(second)
+    second_turned, grad_turned = second.T, whole_grad.T
+    pieces = 2
+    totals, backs, ffn_shares = [], [], []
+    chain = None
+    for piece in range(pieces):
+        total, back, grads = ffn_both(second, whole_grad, second_turned, grad_turned, ffn_in, ffn_out, piece, pieces)
+        totals.append(total)
+        backs.append(back)
+        if chain is not None:
+            grads = after(grads, chain)
+        chain = lax.psum_scatter(grads, "rows", scatter_dimension=1, tiled=True)
+        ffn_shares.append(seq_sum(chain))
+    output, resid_grad, branch_low, ffn_gain_part = norm_back(flat(resid), totals, backs, whole_grad, lift(ffn_gain))
+    output = scatter_rows(shaped(output))
+    branch_low = shaped(branch_low)
+    parts, mix_shares, chans = [], [], []
+    for block in range(model // width):
+        if block == 2:
+            branch_low = after(branch_low, output)
+        part, chan = mixer_backward(branch_low, split, keep, q, k, v, mixed, proj_out, short_filter, cond_filter, slope, shift, skip, tables, block)
+        parts.append(flat(part))
+        chans.append(chan)
+        grads = turn(flat(first), parts[-1])
+        if block == 0:
+            grads = jnp.concatenate([turn(flat(gated), flat(branch_low)), grads], axis=1)
+        grads = after(grads, chain)
+        chain = lax.psum_scatter(grads, "rows", scatter_dimension=0, tiled=True)
+        mix_shares.append(seq_sum(chain))
+    input_grad, norm_gain_part = input_back(flat(x), resid_grad, lift(norm_gain), proj_in, parts)
+    input_grad = scatter_rows(shaped(input_grad)).astype(F32)
+    small = jnp.sum(jnp.concatenate([ffn_gain_part[None], norm_gain_part[None], jnp.concatenate(chans, axis=2)], 0), axis=1)
+    small = exchange_sum(small)
     scale = 1.0 / length
+    out_share, mix_shares[0] = mix_shares[0][:, :model], mix_shares[0][:, model:]
     return (
         output,
         input_grad,
         small[1],
-        mix_share[:, : 3 * model],
+        jnp.concatenate([share[:, k * width : (k + 1) * width] for k in range(3) for share in mix_shares], axis=1),
         jnp.concatenate([small[5:8], small[8:11]], axis=1),
         small[11:14],
         small[2] * scale,
         small[3] * scale,
         small[4],
-        mix_share[:, 3 * model :],
+        out_share,
         small[0],
-        jnp.concatenate([ffn_share[0], ffn_share[1]], axis=1),
-        ffn_share[2].T,
+        jnp.concatenate([share[k] for k in range(2) for share in ffn_shares], axis=1),
+        jnp.concatenate([share[2] for share in ffn_shares], axis=1).T,
     )
 
 

time: 761 us -> 646 us (0.85)
  blocking collectives: 106 us -> 0 us
  Pallas kernels: 317 us -> 369 us
  waiting for transfers between devices: 194 us -> 149 us
  local copies, waits for them, and re-layouts: 56.4 us -> 38.3 us
    psum x2 -> x0, blocking collectives: 106 us -> none  [the longest x1 68.4 us: per_device_rows(): small = lax.psum(small, ('rows', 'seq'))]
    unnamed x4 -> x8, waiting for transfers between devices: 0.28 us -> 86.1 us
    reduce_scatter x1 -> x2, waiting for transfers between devices: 103 us -> 24.5 us  [per_device_rows(): chain = lax.psum_scatter(grads, 'rows', scatter_dimension=1, tiled=True)]
    all_to_all x4 -> x0, waiting for transfers between devices: 45.8 us -> none  [the longest x1 27.9 us: per_device_rows(): output = scatter(output)]
    psum x1 -> x0, waiting for transfers between devices: 44.6 us -> none  [per_device_rows(): mix_share = lax.psum(mix_share, 'seq').astype(F32)]
    pallas_call x2 -> x6, Pallas kernels: 121 us -> 164 us  [the longest x3 90.4 us: mixer_backward(): pl.pallas_call(mixer_backward_kernel, out_shape=[shape((rows, length, 3 *...]
    ppermute x0 -> x10, waiting for transfers between devices: none -> 38.3 us  [swapped(): lax.ppermute(value, 'seq', [(i, (i + 1) % count) for i in range(count)])]
    all_to_all x4 -> x0, starting transfers between devices: 18.9 us -> none  [the longest x1 5.23 us: per_device_rows(): input_grad = scatter(input_grad).astype(F32)]
  transfers between devices with their start and end apart: 7 -> 15, of which waited for: 4 -> 9; matrix products, arithmetic and copies ran while one was open for 8% -> 12% of each run, Pallas kernels for 0% -> 47%
where the time goes in v2:
time: 646 us; the launch traced here: 642 us
  Pallas kernels  369 us (57%)
  waiting for transfers between devices  149 us (23%)
  local copies, waits for them, and re-layouts  38.3 us (6%)
  other arithmetic  36.6 us (6%)
  matrix products  20.9 us (3%)
  between operations  14.7 us (2%)
  starting transfers between devices  14.1 us (2%)
    pallas_call x2, Pallas kernels, ffn_both(): pl.pallas_call(ffn_kernel, out_shape=[shape((tokens, model), F32), shape(...  132 us
    pallas_call x3, Pallas kernels, mixer_backward(): pl.pallas_call(mixer_backward_kernel, out_shape=[shape((rows, length, 3 *...  90.4 us
    unnamed x8, waiting for transfers between devices  86.1 us
    pallas_call x1, Pallas kernels, mixer_forward(): pl.pallas_call(mixer_forward_kernel, out_shape=[low, low, low, low, low,...  72.2 us
    ppermute x10, waiting for transfers between devices, swapped(): lax.ppermute(value, 'seq', [(i, (i + 1) % count) for i in range(count)])  38.3 us
    pallas_call x1, Pallas kernels, exchange_sum(): pl.pallas_call(functools.partial(exchange_sum_kernel, rows, seq), out_sha...  30.1 us
    reduce_scatter x2, waiting for transfers between devices, per_device_rows(): chain = lax.psum_scatter(grads, 'rows', scatter_dimension=1, tiled=True)  24.5 us
    pallas_call x1, Pallas kernels, input_back(): pl.pallas_call(functools.partial(input_back_kernel, len(parts)), out_shap...  23.5 us
  transfers between devices with their start and end apart: 15, of which 9 were waited for; matrix products, arithmetic and copies ran while one was open for 12% of the time, Pallas kernels for 47%

profile of v2, /device:TPU:0, one launch (start us, length us, event | category | flops | bytes accessed | tf_op | source)
XLA Modules:
  0.0 642.1 jit_solution(12039789235634486287)
XLA Ops:
  7.2 2.7 constant_dynamic-slice_fusion.3
  9.9 3.0 collective-permute-start.1
  20.7 2.9 copy.53.fwd_ref
  23.6 4.8 multiply_convert_fusion.1
  35.2 12.4 %collective-permute-done = s32[4]{0:T(128)S(1)} collective-permute-done((s32[4]{0:T(128)S(1)}, s32[4]{0:T(128)S(1)}, u32[]{:S(2)}, u32[]{:S(2)}) %collective-permute-start) | collective-permute-done | bytes 48 | tf_op jit(solution)/shard_map/ppermute | solution.py:688
  55.8 72.2 %mixer_forward.1 = (bf16[2,1024,768]{2,1,0:T(8,128)(2,1)}, bf16[2,1024,768]{2,1,0:T(8,128)(2,1)}, bf16[2,1024,768]{2,1,0:T(8,128)(2,1)}, bf16[2,1024,768]{2,1,0:...) custom-call(s32[2]{0:T(128)} %dynamic_slice.30.split_ref, ...), custom_call_target="tpu_custom_call" | custom-call | flops 19327352832 | bytes 31457280 | tf_op jit(solution)/shard_map/mixer_forward/pallas_call | solution.py:267
  128.0 4.9 copy.87
  134.8 3.5 copy.57.ogt_ref
  138.3 66.3 %ffn_both.2 = (f32[2048,768]{1,0:T(8,128)}, f32[2048,768]{1,0:T(8,128)}, bf16[3,768,1536]{2,1,0:T(8,128)(2,1)}) custom-call(bf16[2048,768]{1,0:T(8,128)(2,1)} %bitcast.60, bf16[2048,768]{1,0:T(8,128)(2,1)} %bitcast.54, bf16[768,2048]{1,0:T(8,128)(2,1)} %bitcast.62, bf16[768,2048]{1,0:T(8,128)(2,1)} %copy.57.ogt_ref, bf16[768,6144]{1,0:T(8,128)(2,1)} %wu_ref.3, ...), custom_call_target="tpu_custom_call" | custom-call | flops 43486543872 | bytes 51904512 | tf_op jit(solution)/shard_map/ffn_both/pallas_call | solution.py:347
  204.7 65.8 %ffn_both.3 = (f32[2048,768]{1,0:T(8,128)}, f32[2048,768]{1,0:T(8,128)}, bf16[3,768,1536]{2,1,0:T(8,128)(2,1)}) custom-call(bf16[2048,768]{1,0:T(8,128)(2,1)} %bitcast.61, bf16[2048,768]{1,0:T(8,128)(2,1)} %bitcast.55, bf16[768,2048]{1,0:T(8,128)(2,1)} %bitcast.63, bf16[768,2048]{1,0:T(8,128)(2,1)} %copy.57.ogt_ref, bf16[768,6144]{1,0:T(8,128)(2,1)} %wu_ref.3, ...), custom_call_target="tpu_custom_call" | custom-call | flops 43486543872 | bytes 51904512 | tf_op jit(solution)/shard_map/ffn_both/pallas_call | solution.py:347
  270.5 24.5 %reduce-scatter.12.cloned.1.call-done = bf16[3,48,1536]{2,1,0:T(8,128)(2,1)} async-done(((bf16[3,768,1536]{2,1,0:T(8,128)(2,1)}), bf16[3,48,1536]{2,1,0:T(8,128)(2,1)}) %reduce-scatter.12.cloned.1.call-update) | async-done | bytes 442384 | tf_op jit(solution)/shard_map/reduce_scatter | solution.py:752
  295.0 20.5 %norm_back.1 = (bf16[2048,768]{1,0:T(8,128)(2,1)}, f32[2048,768]{1,0:T(8,128)}, bf16[2048,768]{1,0:T(8,128)(2,1)}, f32[8,768]{1,0:T(8,128)}) custom-call(f32[2048,768]{1,0:T(8,128)} %bitcast.57, f32[2048,768]{1,0:T(8,128)} %get-tuple-element.48.refs_0_, f32[2048,768]{1,0:T(8,128)} %get-tuple-element.49.refs_1_, f32[2048,768]{1,0:T(8,128)} %get-tuple-element.50.refs_2_, ...), custom_call_target="tpu_custom_call" | custom-call | flops 31457280 | bytes 34603008 | tf_op jit(solution)/shard_map/norm_back/pallas_call | solution.py:398
  315.5 2.8 constant_dynamic-slice_fusion.1
  319.9 30.0 %mixer_backward.3 = (bf16[2,1024,768]{2,1,0:T(8,128)(2,1)}, f32[12,8,256]{2,1,0:T(8,128)}) custom-call(s32[2]{0:T(128)} %dynamic_slice.30.split_ref, s32[2]{0:T(128)} %dynamic_slice.31.keep_ref, bf16[2,1024,768]{2,1,0:T(8,128)(2,1)} %bitcast.70, bf16[2,1024,768]{2,1,0:T(8,128)(2,1)} %get-tuple-element.55.q_ref, ...), custom_call_target="tpu_custom_call" | custom-call | flops 6174015488 | bytes 10485760 | tf_op jit(solution)/shard_map/mixer_backward/pallas_call | solution.py:558
  350.0 5.8 convolution_convert_fusion
  355.8 2.7 bitcast_convert_fusion.2
  360.1 30.3 %mixer_backward.4 = (bf16[2,1024,768]{2,1,0:T(8,128)(2,1)}, f32[12,8,256]{2,1,0:T(8,128)}) custom-call(s32[2]{0:T(128)} %dynamic_slice.30.split_ref, s32[2]{0:T(128)} %dynamic_slice.31.keep_ref, bf16[2,1024,768]{2,1,0:T(8,128)(2,1)} %bitcast.71, bf16[2,1024,768]{2,1,0:T(8,128)(2,1)} %get-tuple-element.55.q_ref, ...), custom_call_target="tpu_custom_call" | custom-call | flops 6174015488 | bytes 10485760 | tf_op jit(solution)/shard_map/mixer_backward/pallas_call | solution.py:558
  390.4 2.5 broadcast_select_fusion.3
  398.0 30.1 %mixer_backward.5 = (bf16[2,1024,768]{2,1,0:T(8,128)(2,1)}, f32[12,8,256]{2,1,0:T(8,128)}) custom-call(s32[2]{0:T(128)} %dynamic_slice.30.split_ref, s32[2]{0:T(128)} %dynamic_slice.31.keep_ref, bf16[2,1024,768]{2,1,0:T(8,128)(2,1)} %bitcast.72, bf16[2,1024,768]{2,1,0:T(8,128)(2,1)} %get-tuple-element.55.q_ref, ...), custom_call_target="tpu_custom_call" | custom-call | flops 6174015488 | bytes 10485760 | tf_op jit(solution)/shard_map/mixer_backward/pallas_call | solution.py:558
  428.1 23.5 %input_back.1 = (bf16[2048,768]{1,0:T(8,128)(2,1)}, f32[8,768]{1,0:T(8,128)}) custom-call(bf16[2048,768]{1,0:T(8,128)(2,1)} %bitcast.58, f32[2048,768]{1,0:T(8,128)} %get-tuple-element.53.grad_ref, f32[1,768]{1,0:T(1,128)} %reshape.83.norm_gain_ref.gain_ref, bf16[768,2304]{1,0:T(8,128)(2,1)} %w_ref.1, bf16[2048,768]{1,0:T(8,128)(2,1)} %bitcast.74, ...), custom_call_target="tpu_custom_call" | custom-call | flops 7247757312 | bytes 22020096 | tf_op jit(solution)/shard_map/input_back/pallas_call | solution.py:613
  451.6 2.8 constant_dynamic-slice_fusion
  454.8 5.7 bitcast_convert_fusion.1
  461.2 30.1 %exchange_sum.1 = f32[14,768]{1,0:T(8,128)} custom-call(f32[14,768]{1,0:T(8,128)} %maximum_reduce_fusion.x_ref), custom_call_target="tpu_custom_call" | custom-call | tf_op jit(solution)/shard_map/exchange_sum/pallas_call | solution.py:670
  495.0 6.8 %bitcast_convert_fusion = bf16[768,768]{1,0:T(8,128)(2,1)} fusion(bf16[2,1024,768]{2,1,0:T(8,128)(2,1)} %get-tuple-element.70, bf16[2,1024,768]{2,1,0:T(8,128)(2,1)} %get-tuple-element.62), kind=kOutput, calls=%fused_computation.5 | convolution fusion | flops 2416508928 | bytes 7471104 | tf_op jit(solution)/shard_map/dot_general | solution.py:627
  504.7 3.1 maximum_convert_fusion
  509.1 2.8 collective-permute-done.8
  514.8 7.9 %collective-permute-done.9 = bf16[3,48,1536]{2,1,0:T(8,128)(2,1)S(1)} collective-permute-done((bf16[3,48,1536]{2,1,0:T(8,128)(2,1)S(1)}, bf16[3,48,1536]{2,1,0:T(8,128)(2,1)S(1)}, u32[]{:S(2)}, u32[]{:S(2)}) %collective-permute-start.9) | collective-permute-done | bytes 442400 | tf_op jit(solution)/shard_map/ppermute | solution.py:688
  522.9 43.7 %reduce-scatter.18.cloned.1.call-done = bf16[48,768]{1,0:T(8,128)(2,1)} async-done(((bf16[768,768]{1,0:T(8,128)(2,1)}), bf16[48,768]{1,0:T(8,128)(2,1)}) %reduce-scatter.18.cloned.1.call-update) | async-done | bytes 73744
  571.1 6.7 %collective-permute-done.5 = bf16[48,1536]{0,1:T(8,128)(2,1)S(1)} collective-permute-done((bf16[48,1536]{0,1:T(8,128)(2,1)S(1)}, bf16[48,1536]{0,1:T(8,128)(2,1)S(1)}, u32[]{:S(2)}, u32[]{:S(2)}) %collective-permute-start.5) | collective-permute-done | bytes 147488 | tf_op jit(solution)/shard_map/ppermute | solution.py:688
  580.5 4.2 collective-permute-done.6
  585.0 42.3 %reduce-scatter.20.cloned.1.call-done = bf16[48,768]{1,0:T(8,128)(2,1)} async-done(((bf16[768,768]{1,0:T(8,128)(2,1)}), bf16[48,768]{1,0:T(8,128)(2,1)}) %reduce-scatter.20.cloned.1.call-update) | async-done | bytes 73744
  629.9 4.3 collective-permute-done.7
  (155 shorter events, 56.1 us)
Async XLA Ops:
  7.2 5.7 copy-start.13
  7.2 287.8 %reduce-scatter.12.cloned.1.call-start = ((), (), s32[]{:S(2)}) async-start(), calls=%async_computation.5 | async-start | bytes 7520256 | tf_op jit(solution)/shard_map/reduce_scatter | solution.py:752
  9.9 38.3 %collective-permute-start.1 = (bf16[2,512,768]{2,1,0:T(8,128)(2,1)}, bf16[2,512,768]{2,1,0:T(8,128)(2,1)}, u32[]{:S(2)}, u32[]{:S(2)}) collective-permute-start(bf16[2,512,768]{2,1,0:T(8,128)(2,1)} %constant_dynamic-slice_fusion.3), channel_id=1, source_target_pairs={{0,1},{1,0},{2,3},{3,2},{4,5},{5,4},{6,7},{7,6},{8,9},{9,8},{10,11... | collective-permute-start | bytes 4718600 | tf_op jit(solution)/shard_map/ppermute | solution.py:688
  13.0 34.6 %collective-permute-start = (s32[4]{0:T(128)S(1)}, s32[4]{0:T(128)S(1)}, u32[]{:S(2)}, u32[]{:S(2)}) collective-permute-start(s32[4]{0:T(128)S(1)} %reduce_sum.18), channel_id=1, source_target_pairs={{0,1},{1,0},{2,3},{3,2},{4,5},{5,4},{6,7},{7,6},{8,9},{9,8},{10,11... | collective-permute-start | bytes 56 | tf_op jit(solution)/shard_map/ppermute | solution.py:688
  20.7 9.5 %copy-start.15 = (f32[768]{0:T(1024)S(1)}, f32[768]{0:T(1024)}, u32[]{:S(2)}) copy-start(f32[768]{0:T(1024)} %param.22) | copy-start | bytes 9220
  20.7 10.1 %copy-start.16 = (f32[768]{0:T(1024)S(1)}, f32[768]{0:T(1024)}, u32[]{:S(2)}) copy-start(f32[768]{0:T(1024)} %param.23) | copy-start | bytes 9220
  20.7 10.7 %copy-start.17 = (f32[768]{0:T(1024)S(1)}, f32[768]{0:T(1024)}, u32[]{:S(2)}) copy-start(f32[768]{0:T(1024)} %param.24) | copy-start | bytes 9220
  20.7 11.3 %copy-start.18 = (f32[768]{0:T(1024)S(1)}, f32[768]{0:T(1024)}, u32[]{:S(2)}) copy-start(f32[768]{0:T(1024)} %param.18) | copy-start | bytes 9220
  20.7 11.8 %copy-start.19 = (f32[768]{0:T(1024)S(1)}, f32[768]{0:T(1024)}, u32[]{:S(2)}) copy-start(f32[768]{0:T(1024)} %param.26) | copy-start | bytes 9220
  23.6 9.5 %copy-start.20 = (s32[4]{0:T(128)S(1)}, s32[4]{0:T(128)}, u32[]{:S(2)}) copy-start(s32[4]{0:T(128)} %param.16) | copy-start | bytes 52
  33.8 14.4 %copy-start.2 = (bf16[4,512,768]{2,1,0:T(8,128)(2,1)S(1)}, bf16[4,512,768]{2,1,0:T(8,128)(2,1)}, u32[]{:S(2)}) copy-start(bf16[4,512,768]{2,1,0:T(8,128)(2,1)} %param.15) | copy-start | bytes 9437188
  54.1 78.9 %collective-permute-start.2 = (bf16[2,512,768]{2,1,0:T(8,128)(2,1)}, bf16[2,512,768]{2,1,0:T(8,128)(2,1)}, u32[]{:S(2)}, u32[]{:S(2)}) collective-permute-start(bf16[2,512,768]{2,1,0:T(8,128)(2,1)} %constant_dynamic-slice_fusion.2), channel_id=1, source_target_pairs={{0,1},{1,0},{2,3},{3,2},{4,5},{5,4},{6,7},{7,6},{8,9},{9,8},{10,11... | collective-permute-start | bytes 4718600 | tf_op jit(solution)/shard_map/ppermute | solution.py:688
  204.6 190.2 %reduce-scatter.14.cloned.1.call-start = ((), (), s32[]{:S(2)}) async-start(), calls=%async_computation.6 | async-start | bytes 7520256 | tf_op jit(solution)/shard_map/reduce_scatter | solution.py:752
  295.0 212.8 %reduce-scatter.16.cloned.1.call-start = ((), (), s32[]{:S(2)}) async-start(), calls=%async_computation.7 | async-start | bytes 2506752
  318.4 72.0 %collective-permute-start.3 = (bf16[2,512,768]{2,1,0:T(8,128)(2,1)}, bf16[2,512,768]{2,1,0:T(8,128)(2,1)}, u32[]{:S(2)}, u32[]{:S(2)}) collective-permute-start(bf16[2,512,768]{2,1,0:T(8,128)(2,1)} %constant_dynamic-slice_fusion.1), channel_id=1, source_target_pairs={{0,1},{1,0},{2,3},{3,2},{4,5},{5,4},{6,7},{7,6},{8,9},{9,8},{10,11... | collective-permute-start | bytes 4718600 | tf_op jit(solution)/shard_map/ppermute | solution.py:688
  349.9 5.8 copy-start.21
  350.0 5.8 copy-start.23
  398.0 168.6 %reduce-scatter.18.cloned.1.call-start = ((), (), s32[]{:S(2)}) async-start(), calls=%async_computation.8 | async-start | bytes 1253376
  454.4 6.1 copy-start.8
  454.4 6.1 copy-start.9
  454.4 6.1 copy-start.10
  454.4 6.1 copy-start.11
  454.4 6.1 copy-start.12
  454.4 48.3 %collective-permute-start.4 = (bf16[2,512,768]{2,1,0:T(8,128)(2,1)}, bf16[2,512,768]{2,1,0:T(8,128)(2,1)}, u32[]{:S(2)}, u32[]{:S(2)}) collective-permute-start(bf16[2,512,768]{2,1,0:T(8,128)(2,1)} %constant_dynamic-slice_fusion), channel_id=1, source_target_pairs={{0,1},{1,0},{2,3},{3,2},{4,5},{5,4},{6,7},{7,6},{8,9},{9,8},{10,11... | collective-permute-start | bytes 4718600 | tf_op jit(solution)/shard_map/ppermute | solution.py:688
  495.0 7.7 %copy-start.5 = (bf16[2048,768]{1,0:T(8,128)(2,1)S(1)}, bf16[2048,768]{1,0:T(8,128)(2,1)}, u32[]{:S(2)}) copy-start(bf16[2048,768]{1,0:T(8,128)(2,1)} %get-tuple-element.63) | copy-start | bytes 9437188
  501.7 10.2 %collective-permute-start.8 = (bf16[3,48,1536]{2,1,0:T(8,128)(2,1)}, bf16[3,48,1536]{2,1,0:T(8,128)(2,1)}, u32[]{:S(2)}, u32[]{:S(2)}) collective-permute-start(bf16[3,48,1536]{2,1,0:T(8,128)(2,1)} %reduce-scatter.12.cloned.1.call-done), channel_id=1, source_target_pairs={{0,1},{1,0},{2,3},{3,2},{4,5},{5,4},{6,7},{7,6},{8,9},{9,8},{10,11... | collective-permute-start | bytes 1327112 | tf_op jit(solution)/shard_map/ppermute | solution.py:688
  504.7 7.2 %copy-start.6 = (bf16[3,48,1536]{2,1,0:T(8,128)(2,1)S(1)}, bf16[3,48,1536]{2,1,0:T(8,128)(2,1)}, u32[]{:S(2)}) copy-start(bf16[3,48,1536]{2,1,0:T(8,128)(2,1)} %reduce-scatter.12.cloned.1.call-done) | copy-start | bytes 1327108
  509.0 118.3 %reduce-scatter.20.cloned.1.call-start = ((), (), s32[]{:S(2)}) async-start(), calls=%async_computation.9 | async-start | bytes 1253376
  513.0 9.7 %collective-permute-start.9 = (bf16[3,48,1536]{2,1,0:T(8,128)(2,1)S(1)}, bf16[3,48,1536]{2,1,0:T(8,128)(2,1)S(1)}, u32[]{:S(2)}, u32[]{:S(2)}) collective-permute-start(bf16[3,48,1536]{2,1,0:T(8,128)(2,1)S(1)} %copy-done.7), channel_id=1, source_target_pairs={{0,1},{1,0},{2,3},{3,2},{4,5},{5,4},{6,7},{7,6},{8,9},{9,8},{10,11... | collective-permute-start | bytes 1327112 | tf_op jit(solution)/shard_map/ppermute | solution.py:688
  568.8 9.0 %collective-permute-start.5 = (bf16[48,1536]{0,1:T(8,128)(2,1)S(1)}, bf16[48,1536]{0,1:T(8,128)(2,1)S(1)}, u32[]{:S(2)}, u32[]{:S(2)}) collective-permute-start(bf16[48,1536]{0,1:T(8,128)(2,1)S(1)} %copy.89), channel_id=1, source_target_pairs={{0,1},{1,0},{2,3},{3,2},{4,5},{5,4},{6,7},{7,6},{8,9},{9,8},{10,11... | collective-permute-start | bytes 442376 | tf_op jit(solution)/shard_map/ppermute | solution.py:688
  579.0 5.7 collective-permute-start.6
  628.4 5.7 collective-permute-start.7
  (7 other events, 23.3 us)
Sparse Core Ops, SparseCore 0:
  204.7 90.1 reduce-scatter.11
  299.0 89.5 reduce-scatter.13
  398.1 61.7 reduce-scatter.15
  509.2 57.3 reduce-scatter.17
  570.1 57.2 reduce-scatter.19

commit v3 on v2

--- a/solution.py
+++ b/solution.py
@@ -417,7 +417,7 @@
     p_ref, chan_ref,
     qs, ks, vs, xv, xc, xy, y_s, spec_s, u_s, o_s,
 ):
-    r = pl.program_id(0)
+    r = pl.program_id(1)
     length, width = q_ref.shape
     quarter = length // 4
     split, keep = split_ref[r], keep_ref[r]
@@ -539,30 +539,30 @@
         loop(length // tile, adjoint)
 
 
-def mixer_backward(branch_low, split, keep, q, k, v, mixed, proj_out, short_filter, cond_filter, slope, shift, skip, tables, block, width=256):
+def mixer_backward(branch_low, split, keep, q, k, v, mixed, proj_out, short_filter, cond_filter, slope, shift, skip, tables, width=256):
     rows, length, model = q.shape
     blocks = model // width
     shape = jax.ShapeDtypeStruct
     pad = pltpu.VMEM((length + 8, width), F32)
     quarter = length // 4
-    row = pl.BlockSpec((None, length, model), lambda r, *_: (r, 0, 0))
-    part = pl.BlockSpec((None, length, width), lambda r, *_: (r, 0, block))
+    row = pl.BlockSpec((None, length, model), lambda j, r, *_: (r, 0, 0))
+    part = pl.BlockSpec((None, length, width), lambda j, r, *_: (r, 0, j))
 
     def columns(size, offset):
-        return pl.BlockSpec((size, width), lambda r, *_: (0, block + offset * blocks))
-
-    fixed = lambda r, *_: (0, 0)
+        return pl.BlockSpec((size, width), lambda j, r, *_: (0, j + offset * blocks))
+
+    fixed = lambda j, r, *_: (0, 0)
     table_specs = [once((2 * quarter, quarter), fixed), once((6 * quarter, 2 * quarter), fixed)] * 2
     one = columns(1, 0)
-    flops = rows * (2 * length * model * width + 2 * 5 * width * (2 * length) * length // 2)
+    flops = rows * (2 * length * model * model + 2 * 5 * model * (2 * length) * length // 2)
     return pl.pallas_call(
         mixer_backward_kernel,
-        out_shape=[shape((rows, length, 3 * width), BF), shape((12, 8, width), F32)],
+        out_shape=[shape((rows, length, 3 * model), BF), shape((12, 8, model), F32)],
         grid_spec=pltpu.PrefetchScalarGridSpec(
             num_scalar_prefetch=2,
-            grid=(rows,),
-            in_specs=[row, part, part, part, part, pl.BlockSpec((width, model), lambda r, *_: (block, 0)), columns(3, 0), columns(3, 1), columns(3, 0), one, one, one] + table_specs,
-            out_specs=[pl.BlockSpec((None, length, 3 * width), lambda r, *_: (r, 0, 0)), once((12, 8, width), lambda r, *_: (0, 0, 0))],
+            grid=(blocks, rows),
+            in_specs=[row, part, part, part, part, pl.BlockSpec((width, model), lambda j, r, *_: (j, 0)), columns(3, 0), columns(3, 1), columns(3, 0), one, one, one] + table_specs,
+            out_specs=[pl.BlockSpec((None, length, 3 * width), lambda j, r, *_: (r, 0, j)), pl.BlockSpec((12, 8, width), lambda j, r, *_: (0, 0, j))],
             scratch_shapes=[pad, pad, pad] + [pltpu.VMEM((length, width), BF)] * 3 + [
                 pltpu.VMEM((2 * length, 3 * width), BF),
                 pltpu.VMEM((2 * length, 3 * width), F32),
@@ -570,16 +570,14 @@
                 pltpu.VMEM((2 * length, 2 * width), F32),
             ],
         ),
-        compiler_params=pltpu.CompilerParams(dimension_semantics=("arbitrary",), vmem_limit_bytes=LIMIT),
-        cost_estimate=pl.CostEstimate(flops=flops, bytes_accessed=rows * length * (model * 2 + width * 14), transcendentals=rows * length * width),
+        compiler_params=pltpu.CompilerParams(dimension_semantics=("arbitrary", "arbitrary"), vmem_limit_bytes=LIMIT),
+        cost_estimate=pl.CostEstimate(flops=flops, bytes_accessed=rows * length * (model * 2 * blocks + model * 14), transcendentals=rows * length * model),
         name="mixer_backward",
     )(split, keep, branch_low, q, k, v, mixed, proj_out, short_filter, short_filter, cond_filter, slope, shift, skip, *tables)
 
 
-def input_back_kernel(blocks, x_ref, grad_ref, gain_ref, w_ref, *refs):
-    p_refs, (in_grad_ref, gain_grad_ref, acc) = refs[:blocks], refs[blocks:]
+def input_back_kernel(width, x_ref, grad_ref, gain_ref, w_ref, p_ref, in_grad_ref, gain_grad_ref, acc):
     model = x_ref.shape[1]
-    width = model // blocks
     tile = 64
 
     @pl.when(pl.program_id(0) == 0)
@@ -587,10 +585,10 @@
         gain_grad_ref[...] = jnp.zeros_like(gain_grad_ref)
 
     total = None
-    for b, p_ref in enumerate(p_refs):
+    for b in range(model // width):
         for k in range(3):
-            lanes = slice(k * model + b * width, k * model + (b + 1) * width)
-            term = mm_t(p_ref[:, k * width : (k + 1) * width], w_ref[:, lanes])
+            place = (3 * b + k) * width
+            term = mm_t(p_ref[:, place : place + width], w_ref[:, k * model + b * width : k * model + (b + 1) * width])
             total = term if total is None else total + term
     acc[...] = total
 
@@ -606,21 +604,21 @@
     loop(x_ref.shape[0] // tile, body)
 
 
-def input_back(x, resid_grad, gain, proj_in, parts, tile=512):
+def input_back(x, resid_grad, gain, proj_in, proj_grad, width, tile=512):
     tokens, model = x.shape
     shape = jax.ShapeDtypeStruct
     block = pl.BlockSpec((tile, model), lambda i: (i, 0))
     return pl.pallas_call(
-        functools.partial(input_back_kernel, len(parts)),
+        functools.partial(input_back_kernel, width),
         out_shape=[shape((tokens, model), BF), shape((8, model), F32)],
         grid=(tokens // tile,),
-        in_specs=[block, block, once((1, model), lambda i: (0, 0)), once((model, 3 * model), lambda i: (0, 0))] + [block] * len(parts),
+        in_specs=[block, block, once((1, model), lambda i: (0, 0)), once((model, 3 * model), lambda i: (0, 0)), pl.BlockSpec((tile, 3 * model), lambda i: (i, 0))],
         out_specs=[block, pl.BlockSpec((8, model), lambda i: (0, 0))],
         scratch_shapes=[pltpu.VMEM((tile, model), F32)],
         compiler_params=pltpu.CompilerParams(dimension_semantics=("arbitrary",), vmem_limit_bytes=LIMIT),
         cost_estimate=pl.CostEstimate(flops=6 * tokens * model * model, bytes_accessed=tokens * model * 14, transcendentals=tokens),
         name="input_back",
-    )(x, resid_grad, gain, proj_in, *parts)
+    )(x, resid_grad, gain, proj_in, proj_grad)
 
 
 def turn(a, b):
@@ -723,6 +721,7 @@
     width = 256
     first_row = lax.axis_index("seq") * own
     flat = lambda a: a.reshape(tokens, model)
+    flat_wide = lambda a: a.reshape(tokens, 3 * model)
     shaped = lambda a: a.reshape(own, length, model)
     lift = lambda a: a.reshape(1, -1)
 
@@ -741,49 +740,46 @@
     second = flat(second)
     second_turned, grad_turned = second.T, whole_grad.T
     pieces = 2
-    totals, backs, ffn_shares = [], [], []
-    chain = None
+    totals, backs, grads = [], [], []
     for piece in range(pieces):
-        total, back, grads = ffn_both(second, whole_grad, second_turned, grad_turned, ffn_in, ffn_out, piece, pieces)
+        total, back, grad = ffn_both(second, whole_grad, second_turned, grad_turned, ffn_in, ffn_out, piece, pieces)
         totals.append(total)
         backs.append(back)
-        if chain is not None:
-            grads = after(grads, chain)
-        chain = lax.psum_scatter(grads, "rows", scatter_dimension=1, tiled=True)
-        ffn_shares.append(seq_sum(chain))
+        grads.append(grad)
+    chain = lax.psum_scatter(grads[0], "rows", scatter_dimension=1, tiled=True)
+    ffn_shares = [chain]
     output, resid_grad, branch_low, ffn_gain_part = norm_back(flat(resid), totals, backs, whole_grad, lift(ffn_gain))
     output = scatter_rows(shaped(output))
-    branch_low = shaped(branch_low)
-    parts, mix_shares, chans = [], [], []
-    for block in range(model // width):
-        if block == 2:
-            branch_low = after(branch_low, output)
-        part, chan = mixer_backward(branch_low, split, keep, q, k, v, mixed, proj_out, short_filter, cond_filter, slope, shift, skip, tables, block)
-        parts.append(flat(part))
-        chans.append(chan)
-        grads = turn(flat(first), parts[-1])
-        if block == 0:
-            grads = jnp.concatenate([turn(flat(gated), flat(branch_low)), grads], axis=1)
-        grads = after(grads, chain)
-        chain = lax.psum_scatter(grads, "rows", scatter_dimension=0, tiled=True)
-        mix_shares.append(seq_sum(chain))
-    input_grad, norm_gain_part = input_back(flat(x), resid_grad, lift(norm_gain), proj_in, parts)
+    out_part = turn(flat(gated), branch_low)
+    for grad in grads[1:]:
+        grad, chain, branch_low = lax.optimization_barrier((grad, chain, branch_low))
+        chain = lax.psum_scatter(grad, "rows", scatter_dimension=1, tiled=True)
+        ffn_shares.append(chain)
+    proj_grad, chan = mixer_backward(shaped(branch_low), split, keep, q, k, v, mixed, proj_out, short_filter, cond_filter, slope, shift, skip, tables)
+    proj_grad = flat_wide(proj_grad)
+    mix_part = jnp.concatenate([out_part, turn(flat(first), proj_grad)], axis=1)
+    mix_part, *ffn_shares = lax.optimization_barrier((mix_part, *ffn_shares))
+    mix_share = lax.psum_scatter(mix_part, "rows", scatter_dimension=0, tiled=True)
+    proj_grad = after(proj_grad, mix_part)
+    input_grad, norm_gain_part = input_back(flat(x), resid_grad, lift(norm_gain), proj_in, proj_grad, width)
     input_grad = scatter_rows(shaped(input_grad)).astype(F32)
-    small = jnp.sum(jnp.concatenate([ffn_gain_part[None], norm_gain_part[None], jnp.concatenate(chans, axis=2)], 0), axis=1)
+    ffn_shares = [seq_sum(share) for share in ffn_shares]
+    small = jnp.sum(jnp.concatenate([ffn_gain_part[None], norm_gain_part[None], chan], 0), axis=1)
     small = exchange_sum(small)
     scale = 1.0 / length
-    out_share, mix_shares[0] = mix_shares[0][:, :model], mix_shares[0][:, model:]
+    mix_share = seq_sum(mix_share)
+    in_share = mix_share[:, model:].reshape(-1, model // width, 3, width).transpose(0, 2, 1, 3)
     return (
         output,
         input_grad,
         small[1],
-        jnp.concatenate([share[:, k * width : (k + 1) * width] for k in range(3) for share in mix_shares], axis=1),
+        in_share.reshape(-1, 3 * model),
         jnp.concatenate([small[5:8], small[8:11]], axis=1),
         small[11:14],
         small[2] * scale,
         small[3] * scale,
         small[4],
-        out_share,
+        mix_share[:, :model],
         small[0],
         jnp.concatenate([share[k] for k in range(2) for share in ffn_shares], axis=1),
         jnp.concatenate([share[2] for share in ffn_shares], axis=1).T,

time: 646 us -> 540 us (0.84)
  waiting for transfers between devices: 149 us -> 66 us
  Pallas kernels: 369 us -> 348 us
  local copies, waits for them, and re-layouts: 38.3 us -> 31 us
    unnamed x8 -> x3, waiting for transfers between devices: 86.1 us -> 0.05 us
    ppermute x10 -> x8, waiting for transfers between devices: 38.3 us -> 59.4 us  [swapped(): lax.ppermute(value, 'seq', [(i, (i + 1) % count) for i in range(count)])]
    reduce_scatter x2 -> x3, waiting for transfers between devices: 24.5 us -> 6.54 us  [the longest x1 6.54 us: per_device_rows(): chain = lax.psum_scatter(grads[0], 'rows', scatter_dimension=1, tiled=True)]
    pallas_call x3 -> x1, Pallas kernels: 90.4 us -> 79.9 us  [mixer_backward(): pl.pallas_call(mixer_backward_kernel, out_shape=[shape((rows, length, 3 *...]
    reduce_scatter x2 -> x3, starting transfers between devices: 0.08 us -> 9.3 us  [the longest x1 9.22 us: per_device_rows(): lax.psum_scatter(mix_part, 'rows', scatter_dimension=0, tiled=True)]
    pallas_call x1, Pallas kernels: 30.1 us -> 21.5 us  [exchange_sum(): pl.pallas_call(functools.partial(exchange_sum_kernel, rows, seq), out_sha...]
    ppermute x10 -> x8, starting transfers between devices: 13.9 us -> 9.04 us  [swapped(): lax.ppermute(value, 'seq', [(i, (i + 1) % count) for i in range(count)])]
    dot_general x4 -> x2, matrix products: 20.9 us -> 18 us  [turn(): lax.dot_general(a, b, (((0,), (0,)), ((), ())), preferred_element_type=F32)]
  transfers between devices with their start and end apart: 15 -> 11, of which waited for: 9 -> 5; matrix products, arithmetic and copies ran while one was open for 12% -> 14% of each run, Pallas kernels for 47% -> 53%
where the time goes in v3:
time: 540 us; the launch traced here: 535 us
  Pallas kernels  348 us (64%)
  waiting for transfers between devices  66 us (12%)
  other arithmetic  39.4 us (7%)
  local copies, waits for them, and re-layouts  31 us (6%)
  starting transfers between devices  18.3 us (3%)
  matrix products  18 us (3%)
  between operations  14.4 us (3%)
    pallas_call x2, Pallas kernels, ffn_both(): pl.pallas_call(ffn_kernel, out_shape=[shape((tokens, model), F32), shape(...  131 us
    pallas_call x1, Pallas kernels, mixer_backward(): pl.pallas_call(mixer_backward_kernel, out_shape=[shape((rows, length, 3 *...  79.9 us
    pallas_call x1, Pallas kernels, mixer_forward(): pl.pallas_call(mixer_forward_kernel, out_shape=[low, low, low, low, low,...  72.3 us
    ppermute x8, waiting for transfers between devices, swapped(): lax.ppermute(value, 'seq', [(i, (i + 1) % count) for i in range(count)])  59.4 us
    pallas_call x1, Pallas kernels, input_back(): pl.pallas_call(functools.partial(input_back_kernel, width), out_shape=[sh...  23.6 us
    pallas_call x1, Pallas kernels, exchange_sum(): pl.pallas_call(functools.partial(exchange_sum_kernel, rows, seq), out_sha...  21.5 us
    pallas_call x1, Pallas kernels, norm_back(): pl.pallas_call(functools.partial(norm_back_kernel, pieces), out_shape=[sh...  19.2 us
    dot_general x2, matrix products, turn(): lax.dot_general(a, b, (((0,), (0,)), ((), ())), preferred_element_type=F32)  18 us
  transfers between devices with their start and end apart: 11, of which 5 were waited for; matrix products, arithmetic and copies ran while one was open for 14% of the time, Pallas kernels for 53%

profile of v3, /device:TPU:0, one launch (start us, length us, event | category | flops | bytes accessed | tf_op | source)
XLA Modules:
  0.0 535.1 jit_solution(7455251819170023259)
XLA Ops:
  8.1 3.1 collective-permute-start
  11.1 2.7 constant_dynamic-slice_fusion.3
  16.9 4.8 multiply_convert_fusion.1
  30.9 2.6 copy.43.fwd_ref
  36.2 13.8 %collective-permute-done.1 = bf16[2,512,768]{2,1,0:T(8,128)(2,1)} collective-permute-done((bf16[2,512,768]{2,1,0:T(8,128)(2,1)}, bf16[2,512,768]{2,1,0:T(8,128)(2,1)}, u32[]{:S(2)}, u32[]{:S(2)}) %collective-permute-start.1) | collective-permute-done | bytes 1572896 | tf_op jit(solution)/shard_map/ppermute | solution.py:686
  50.0 1.6 broadcast_select_fusion.7
  51.6 1.9 pad_maximum_fusion.1.x_ref
  56.2 72.3 %mixer_forward.1 = (bf16[2,1024,768]{2,1,0:T(8,128)(2,1)}, bf16[2,1024,768]{2,1,0:T(8,128)(2,1)}, bf16[2,1024,768]{2,1,0:T(8,128)(2,1)}, bf16[2,1024,768]{2,1,0:...) custom-call(s32[2]{0:T(128)} %dynamic_slice.30.split_ref, ...), custom_call_target="tpu_custom_call" | custom-call | flops 19327352832 | bytes 31457280 | tf_op jit(solution)/shard_map/mixer_forward/pallas_call | solution.py:267
  128.5 5.1 copy.57
  133.6 1.6 broadcast_select_fusion.5
  135.4 3.4 copy.47.ogt_ref
  138.8 65.7 %ffn_both.2 = (f32[2048,768]{1,0:T(8,128)}, f32[2048,768]{1,0:T(8,128)}, bf16[3,768,1536]{2,1,0:T(8,128)(2,1)}) custom-call(bf16[2048,768]{1,0:T(8,128)(2,1)} %bitcast.52, bf16[2048,768]{1,0:T(8,128)(2,1)} %bitcast.42, bf16[768,2048]{1,0:T(8,128)(2,1)} %bitcast.54, bf16[768,2048]{1,0:T(8,128)(2,1)} %copy.47.ogt_ref, bf16[768,6144]{1,0:T(8,128)(2,1)} %wu_ref.3, ...), custom_call_target="tpu_custom_call" | custom-call | flops 43486543872 | bytes 51904512 | tf_op jit(solution)/shard_map/ffn_both/pallas_call | solution.py:347
  204.6 65.7 %ffn_both.3 = (f32[2048,768]{1,0:T(8,128)}, f32[2048,768]{1,0:T(8,128)}, bf16[3,768,1536]{2,1,0:T(8,128)(2,1)}) custom-call(bf16[2048,768]{1,0:T(8,128)(2,1)} %bitcast.53, bf16[2048,768]{1,0:T(8,128)(2,1)} %bitcast.43, bf16[768,2048]{1,0:T(8,128)(2,1)} %bitcast.55, bf16[768,2048]{1,0:T(8,128)(2,1)} %copy.47.ogt_ref, bf16[768,6144]{1,0:T(8,128)(2,1)} %wu_ref.3, ...), custom_call_target="tpu_custom_call" | custom-call | flops 43486543872 | bytes 51904512 | tf_op jit(solution)/shard_map/ffn_both/pallas_call | solution.py:347
  270.3 19.2 %norm_back.1 = (bf16[2048,768]{1,0:T(8,128)(2,1)}, f32[2048,768]{1,0:T(8,128)}, bf16[2048,768]{1,0:T(8,128)(2,1)}, f32[8,768]{1,0:T(8,128)}) custom-call(f32[2048,768]{1,0:T(8,128)} %bitcast.45, f32[2048,768]{1,0:T(8,128)} %get-tuple-element.45.refs_0_, f32[2048,768]{1,0:T(8,128)} %get-tuple-element.46.refs_1_, f32[2048,768]{1,0:T(8,128)} %get-tuple-element.47.refs_2_, ...), custom_call_target="tpu_custom_call" | custom-call | flops 31457280 | bytes 34603008 | tf_op jit(solution)/shard_map/norm_back/pallas_call | solution.py:398
  289.5 6.5 %reduce-scatter.4.cloned.1.call-done = bf16[3,48,1536]{2,1,0:T(8,128)(2,1)} async-done(((bf16[3,768,1536]{2,1,0:T(8,128)(2,1)}), bf16[3,48,1536]{2,1,0:T(8,128)(2,1)}) %reduce-scatter.4.cloned.1.call-update) | async-done | bytes 442384 | tf_op jit(solution)/shard_map/reduce_scatter | solution.py:749
  296.1 9.2 %reduce-scatter.8.cloned.1.call-start = ((), (), s32[]{:S(2)}) async-start(), calls=%async_computation.5 | async-start | bytes 5013504 | tf_op jit(solution)/shard_map/reduce_scatter | solution.py:762
  305.3 6.0 %convolution_convert_fusion = bf16[768,768]{0,1:T(8,128)(2,1)S(1)} fusion(bf16[2048,768]{1,0:T(8,128)(2,1)} %bitcast.61, bf16[2048,768]{1,0:T(8,128)(2,1)} %get-tuple-element.54), kind=kOutput, calls=%fused_computation.15 | convolution fusion | flops 2416508928 | bytes 7471104 | tf_op jit(solution)/shard_map/dot_general | solution.py:625
  312.8 79.9 %mixer_backward.1 = (bf16[2,1024,2304]{2,1,0:T(8,128)(2,1)}, f32[12,8,768]{2,1,0:T(8,128)}) custom-call(s32[2]{0:T(128)} %dynamic_slice.30.split_ref, s32[2]{0:T(128)} %dynamic_slice.31.keep_ref, bf16[2,1024,768]{2,1,0:T(8,128)(2,1)} %bitcast.59, bf16[2,1024,768]{2,1,0:T(8,128)(2,1)} %get-tuple-element.55.q_ref, ...), custom_call_target="tpu_custom_call" | custom-call | flops 18522046464 | bytes 31457280 | tf_op jit(solution)/shard_map/mixer_backward/pallas_call | solution.py:558
  392.7 12.1 %bitcast_convert_fusion = bf16[768,2304]{1,0:T(8,128)(2,1)S(1)} fusion(bf16[2,1024,768]{2,1,0:T(8,128)(2,1)} %get-tuple-element.61, bf16[2,1024,2304]{2,1,0:T(8,128)(2,1)} %get-tuple-element.59), kind=kOutput, calls=%fused_computation | convolution fusion | flops 7249526784 | bytes 16121856 | tf_op jit(solution)/shard_map/dot_general | solution.py:625
  404.8 2.8 pad_maximum_fusion
  407.6 1.9 copy-done.2
  410.8 1.5 collective-permute-start.3
  412.2 23.6 %input_back.1 = (bf16[2048,768]{1,0:T(8,128)(2,1)}, f32[8,768]{1,0:T(8,128)}) custom-call(bf16[2048,768]{1,0:T(8,128)(2,1)} %bitcast.48, f32[2048,768]{1,0:T(8,128)} %get-tuple-element.50.grad_ref, f32[1,768]{1,0:T(1,128)} %reshape.81.norm_gain_ref.gain_ref, bf16[768,2304]{1,0:T(8,128)(2,1)} %w_ref.1, bf16[2048,2304]{1,0:T(8,128)(2,1)} %bitcast.60), custom_call_target="tpu_custom_call" | custom-call | flops 7247757312 | bytes 22020096 | tf_op jit(solution)/shard_map/input_back/pallas_call | solution.py:611
  435.9 1.8 maximum_reduce_fusion.x_ref
  437.7 21.5 %exchange_sum.1 = f32[14,768]{1,0:T(8,128)} custom-call(f32[14,768]{1,0:T(8,128)} %maximum_reduce_fusion.x_ref), custom_call_target="tpu_custom_call" | custom-call | tf_op jit(solution)/shard_map/exchange_sum/pallas_call | solution.py:668
  461.3 1.5 constant_dynamic-slice_fusion
  465.5 7.0 %collective-permute-done.6 = bf16[3,48,1536]{2,1,0:T(8,128)(2,1)S(1)} collective-permute-done((bf16[3,48,1536]{2,1,0:T(8,128)(2,1)}, bf16[3,48,1536]{2,1,0:T(8,128)(2,1)S(1)}, u32[]{:S(2)}, u32[]{:S(2)}) %collective-permute-start.6) | collective-permute-done | bytes 442400 | tf_op jit(solution)/shard_map/ppermute | solution.py:686
  472.7 9.4 %collective-permute-done.7 = bf16[3,48,1536]{2,1,0:T(8,128)(2,1)S(1)} collective-permute-done((bf16[3,48,1536]{2,1,0:T(8,128)(2,1)}, bf16[3,48,1536]{2,1,0:T(8,128)(2,1)S(1)}, u32[]{:S(2)}, u32[]{:S(2)}) %collective-permute-start.7) | collective-permute-done | bytes 442400 | tf_op jit(solution)/shard_map/ppermute | solution.py:686
  484.3 29.2 %collective-permute-done.4 = bf16[2,512,768]{2,1,0:T(8,128)(2,1)S(1)} collective-permute-done((bf16[2,512,768]{2,1,0:T(8,128)(2,1)S(1)}, bf16[2,512,768]{2,1,0:T(8,128)(2,1)S(1)}, u32[]{:S(2)}, u32[]{:S(2)}) %collective-permute-start.4) | collective-permute-done | bytes 1572896 | tf_op jit(solution)/shard_map/ppermute | solution.py:686
  513.5 4.4 broadcast_select_fusion.1
  519.2 3.8 pad_maximum_fusion.3
  523.0 3.1 maximum_convert_fusion
  (107 shorter events, 32.1 us)
Async XLA Ops:
  7.2 6.8 %copy-start.12 = (f32[768]{0:T(1024)S(1)}, f32[768]{0:T(1024)}, u32[]{:S(2)}) copy-start(f32[768]{0:T(1024)} %param.18) | copy-start | bytes 9220
  7.2 7.3 %copy-start.13 = (f32[768]{0:T(1024)S(1)}, f32[768]{0:T(1024)}, u32[]{:S(2)}) copy-start(f32[768]{0:T(1024)} %param.22) | copy-start | bytes 9220
  7.2 7.9 %copy-start.14 = (f32[768]{0:T(1024)S(1)}, f32[768]{0:T(1024)}, u32[]{:S(2)}) copy-start(f32[768]{0:T(1024)} %param.23) | copy-start | bytes 9220
  7.2 8.5 %copy-start.15 = (f32[768]{0:T(1024)S(1)}, f32[768]{0:T(1024)}, u32[]{:S(2)}) copy-start(f32[768]{0:T(1024)} %param.24) | copy-start | bytes 9220
  7.2 9.1 %copy-start.16 = (f32[768]{0:T(1024)S(1)}, f32[768]{0:T(1024)}, u32[]{:S(2)}) copy-start(f32[768]{0:T(1024)} %param.26) | copy-start | bytes 9220
  7.2 288.9 %reduce-scatter.4.cloned.1.call-start = ((), (), s32[]{:S(2)}) async-start(), calls=%async_computation.3 | async-start | bytes 7520256 | tf_op jit(solution)/shard_map/reduce_scatter | solution.py:749
  8.1 27.5 %collective-permute-start = (s32[4]{0:T(128)S(1)}, s32[4]{0:T(128)S(1)}, u32[]{:S(2)}, u32[]{:S(2)}) collective-permute-start(s32[4]{0:T(128)S(1)} %reduce_sum.18), channel_id=1, source_target_pairs={{0,1},{1,0},{2,3},{3,2},{4,5},{5,4},{6,7},{7,6},{8,9},{9,8},{10,11... | collective-permute-start | bytes 56 | tf_op jit(solution)/shard_map/ppermute | solution.py:686
  13.8 36.2 %collective-permute-start.1 = (bf16[2,512,768]{2,1,0:T(8,128)(2,1)}, bf16[2,512,768]{2,1,0:T(8,128)(2,1)}, u32[]{:S(2)}, u32[]{:S(2)}) collective-permute-start(bf16[2,512,768]{2,1,0:T(8,128)(2,1)} %constant_dynamic-slice_fusion.3), channel_id=1, source_target_pairs={{0,1},{1,0},{2,3},{3,2},{4,5},{5,4},{6,7},{7,6},{8,9},{9,8},{10,11... | collective-permute-start | bytes 4718600 | tf_op jit(solution)/shard_map/ppermute | solution.py:686
  27.7 5.9 %copy-start.17 = (s32[4]{0:T(128)S(1)}, s32[4]{0:T(128)}, u32[]{:S(2)}) copy-start(s32[4]{0:T(128)} %param.16) | copy-start | bytes 52
  34.2 15.8 %copy-start.5 = (bf16[4,512,768]{2,1,0:T(8,128)(2,1)S(1)}, bf16[4,512,768]{2,1,0:T(8,128)(2,1)}, u32[]{:S(2)}) copy-start(bf16[4,512,768]{2,1,0:T(8,128)(2,1)} %param.15) | copy-start | bytes 9437188
  51.6 3.0 copy-start.6
  55.9 77.7 %collective-permute-start.2 = (bf16[2,512,768]{2,1,0:T(8,128)(2,1)}, bf16[2,512,768]{2,1,0:T(8,128)(2,1)}, u32[]{:S(2)}, u32[]{:S(2)}) collective-permute-start(bf16[2,512,768]{2,1,0:T(8,128)(2,1)} %constant_dynamic-slice_fusion.2), channel_id=1, source_target_pairs={{0,1},{1,0},{2,3},{3,2},{4,5},{5,4},{6,7},{7,6},{8,9},{9,8},{10,11... | collective-permute-start | bytes 4718600 | tf_op jit(solution)/shard_map/ppermute | solution.py:686
  128.5 5.1 copy-start.7
  135.4 3.4 copy-start
  204.6 203.1 %reduce-scatter.6.cloned.1.call-start = ((), (), s32[]{:S(2)}) async-start(), calls=%async_computation.4 | async-start | bytes 7520256 | tf_op jit(solution)/shard_map/reduce_scatter | solution.py:756
  296.1 221.8 %reduce-scatter.8.cloned.1.call-start = ((), (), s32[]{:S(2)}) async-start(), calls=%async_computation.5 | async-start | bytes 5013504 | tf_op jit(solution)/shard_map/reduce_scatter | solution.py:762
  392.7 12.1 %copy-start.1 = (bf16[768,768]{1,0:T(8,128)(2,1)S(1)}, bf16[768,768]{1,0:T(8,128)(2,1)}, u32[]{:S(2)}) copy-start(bf16[768,768]{1,0:T(8,128)(2,1)} %copy.54) | copy-start | bytes 3538948
  407.6 1.9 copy-start.2
  410.8 73.5 %collective-permute-start.3 = (bf16[2,512,768]{2,1,0:T(8,128)(2,1)}, bf16[2,512,768]{2,1,0:T(8,128)(2,1)}, u32[]{:S(2)}, u32[]{:S(2)}) collective-permute-start(bf16[2,512,768]{2,1,0:T(8,128)(2,1)} %constant_dynamic-slice_fusion.1), channel_id=1, source_target_pairs={{0,1},{1,0},{2,3},{3,2},{4,5},{5,4},{6,7},{7,6},{8,9},{9,8},{10,11... | collective-permute-start | bytes 4718600 | tf_op jit(solution)/shard_map/ppermute | solution.py:686
  435.9 36.7 %copy-start.8 = (bf16[3,48,1536]{2,1,0:T(8,128)(2,1)S(1)}, bf16[3,48,1536]{2,1,0:T(8,128)(2,1)}, u32[]{:S(2)}) copy-start(bf16[3,48,1536]{2,1,0:T(8,128)(2,1)} %reduce-scatter.4.cloned.1.call-done) | copy-start | bytes 1327108
  435.9 46.2 %copy-start.9 = (bf16[3,48,1536]{2,1,0:T(8,128)(2,1)S(1)}, bf16[3,48,1536]{2,1,0:T(8,128)(2,1)}, u32[]{:S(2)}) copy-start(bf16[3,48,1536]{2,1,0:T(8,128)(2,1)} %reduce-scatter.6.cloned.1.call-done) | copy-start | bytes 1327108
  459.2 4.4 copy-start.11
  459.2 13.3 %collective-permute-start.6 = (bf16[3,48,1536]{2,1,0:T(8,128)(2,1)}, bf16[3,48,1536]{2,1,0:T(8,128)(2,1)S(1)}, u32[]{:S(2)}, u32[]{:S(2)}) collective-permute-start(bf16[3,48,1536]{2,1,0:T(8,128)(2,1)} %reduce-scatter.4.cloned.1.call-done), channel_id=1, source_target_pairs={{0,1},{1,0},{2,3},{3,2},{4,5},{5,4},{6,7},{7,6},{8,9},{9,8},{10,11... | collective-permute-start | bytes 1327112 | tf_op jit(solution)/shard_map/ppermute | solution.py:686
  460.0 22.0 %collective-permute-start.7 = (bf16[3,48,1536]{2,1,0:T(8,128)(2,1)}, bf16[3,48,1536]{2,1,0:T(8,128)(2,1)S(1)}, u32[]{:S(2)}, u32[]{:S(2)}) collective-permute-start(bf16[3,48,1536]{2,1,0:T(8,128)(2,1)} %reduce-scatter.6.cloned.1.call-done), channel_id=1, source_target_pairs={{0,1},{1,0},{2,3},{3,2},{4,5},{5,4},{6,7},{7,6},{8,9},{9,8},{10,11... | collective-permute-start | bytes 1327112 | tf_op jit(solution)/shard_map/ppermute | solution.py:686
  462.9 50.6 %collective-permute-start.4 = (bf16[2,512,768]{2,1,0:T(8,128)(2,1)S(1)}, bf16[2,512,768]{2,1,0:T(8,128)(2,1)S(1)}, u32[]{:S(2)}, u32[]{:S(2)}) collective-permute-start(bf16[2,512,768]{2,1,0:T(8,128)(2,1)S(1)} %constant_dynamic-slice_fusion), channel_id=1, source_target_pairs={{0,1},{1,0},{2,3},{3,2},{4,5},{5,4},{6,7},{7,6},{8,9},{9,8},{10,11... | collective-permute-start | bytes 4718600 | tf_op jit(solution)/shard_map/ppermute | solution.py:686
  482.2 31.3 %copy-start.3 = (bf16[2048,768]{1,0:T(8,128)(2,1)S(1)}, bf16[2048,768]{1,0:T(8,128)(2,1)}, u32[]{:S(2)}) copy-start(bf16[2048,768]{1,0:T(8,128)(2,1)} %get-tuple-element.49) | copy-start | bytes 9437188
  482.2 31.3 %copy-start.4 = (bf16[2048,768]{1,0:T(8,128)(2,1)S(1)}, bf16[2048,768]{1,0:T(8,128)(2,1)}, u32[]{:S(2)}) copy-start(bf16[2048,768]{1,0:T(8,128)(2,1)} %get-tuple-element.65) | copy-start | bytes 9437188
  517.9 8.2 %collective-permute-start.5 = (bf16[48,3072]{1,0:T(8,128)(2,1)}, bf16[48,3072]{1,0:T(8,128)(2,1)S(1)}, u32[]{:S(2)}, u32[]{:S(2)}) collective-permute-start(bf16[48,3072]{1,0:T(8,128)(2,1)} %reduce-scatter.8.cloned.1.call-done), channel_id=1, source_target_pairs={{0,1},{1,0},{2,3},{3,2},{4,5},{5,4},{6,7},{7,6},{8,9},{9,8},{10,11... | collective-permute-start | bytes 884744 | tf_op jit(solution)/shard_map/ppermute | solution.py:686
  523.0 3.1 copy-start.10
Sparse Core Ops, SparseCore 0:
  204.7 91.3 reduce-scatter.3
  300.1 89.5 reduce-scatter.5
  407.8 76.2 reduce-scatter.7

commit v4 on v3

--- a/solution.py
+++ b/solution.py
@@ -150,12 +150,13 @@
 
 
 def mixer_forward_kernel(
-    split_ref, keep_ref, x_ref, norm_gain_ref, wq_ref, wk_ref, wv_ref, fq_ref, fv_ref, fk_ref, slope_ref, shift_ref,
+    first_row, earlier, split_ref, keep_ref, x_ref, norm_gain_ref, wq_ref, wk_ref, wv_ref, fq_ref, fv_ref, fk_ref, slope_ref, shift_ref,
     skip_ref, wo_ref, ffn_gain_ref, fwd_real_ref, fwd_ref, inv_real_ref, inv_ref,
-    first_ref, q_ref, k_ref, v_ref, mixed_ref, gated_ref, resid_ref, second_ref,
-    qs, ks, vs, xv, xc, y_s, spec_s, u_s, o_s, qc,
+    *refs,
 ):
-    r, j = pl.program_id(0), pl.program_id(1)
+    first_ref, q_ref, k_ref, v_ref, mixed_ref, gated_ref, resid_ref, second_ref = refs[earlier : earlier + 8]
+    qs, ks, vs, xv, xc, y_s, spec_s, u_s, o_s, qc = refs[earlier + 8 :]
+    r, j = first_row + pl.program_id(0), pl.program_id(1)
     length, width = q_ref.shape
     quarter = length // 4
     split, keep = split_ref[r], keep_ref[r]
@@ -241,10 +242,10 @@
     return pl.BlockSpec(shape, index, pipeline_mode=pl.Buffered(1))
 
 
-def mixer_specs(length, model, width):
+def mixer_specs(length, model, width, first_row):
     blocks = model // width
-    row = pl.BlockSpec((None, length, model), lambda r, j, *_: (r, 0, 0))
-    part = pl.BlockSpec((None, length, width), lambda r, j, *_: (r, 0, j))
+    row = pl.BlockSpec((None, length, model), lambda r, j, *_: (r + first_row, 0, 0))
+    part = pl.BlockSpec((None, length, width), lambda r, j, *_: (r + first_row, 0, j))
 
     def columns(rows, offset):
         return pl.BlockSpec((rows, width), lambda r, j, *_: (0, j + offset * blocks))
@@ -256,21 +257,23 @@
     return blocks, row, part, columns, out_rows, gain, tables + tables
 
 
-def mixer_forward(x, split, keep, norm_gain, proj_in, short_filter, cond_filter, slope, shift, skip, proj_out, ffn_gain, tables, width=256):
+def mixer_forward(x, split, keep, norm_gain, proj_in, short_filter, cond_filter, slope, shift, skip, proj_out, ffn_gain, tables, first_row, total_rows, earlier, width=256):
     rows, length, model = x.shape
-    blocks, row, part, columns, out_rows, gain, table_specs = mixer_specs(length, model, width)
+    blocks, row, part, columns, out_rows, gain, table_specs = mixer_specs(length, model, width, first_row)
+    x_row = pl.BlockSpec((None, length, model), lambda r, j, *_: (r, 0, 0))
     one = columns(1, 0)
     shape = jax.ShapeDtypeStruct
-    low, full = shape((rows, length, model), BF), shape((rows, length, model), F32)
+    low, full = shape((total_rows, length, model), BF), shape((total_rows, length, model), F32)
     pad = pltpu.VMEM((length + 8, width), F32)
     flops = rows * (2 * length * model * (3 * model + model) + 2 * 3 * model * (2 * length) * length // 2)
+    operands = (split, keep, x, norm_gain, proj_in, proj_in, proj_in, short_filter, short_filter, cond_filter, slope, shift, skip, proj_out, ffn_gain, *tables)
     return pl.pallas_call(
-        mixer_forward_kernel,
+        functools.partial(mixer_forward_kernel, first_row, len(earlier)),
         out_shape=[low, low, low, low, low, low, full, low],
         grid_spec=pltpu.PrefetchScalarGridSpec(
             num_scalar_prefetch=2,
             grid=(rows, blocks),
-            in_specs=[row, gain, columns(model, 0), columns(model, 1), columns(model, 2), columns(3, 0), columns(3, 1), columns(3, 0), one, one, one, out_rows, gain] + table_specs,
+            in_specs=[x_row, gain, columns(model, 0), columns(model, 1), columns(model, 2), columns(3, 0), columns(3, 1), columns(3, 0), one, one, one, out_rows, gain] + table_specs + [pl.BlockSpec(memory_space=pl.ANY)] * len(earlier),
             out_specs=[row, part, part, part, part, part, row, row],
             scratch_shapes=[pad, pad, pad] + [pltpu.VMEM((length, width), BF)] * 2 + [
                 pltpu.VMEM((2 * length, 2 * width), BF),
@@ -282,8 +285,9 @@
         ),
         compiler_params=pltpu.CompilerParams(dimension_semantics=("arbitrary", "arbitrary"), vmem_limit_bytes=LIMIT),
         cost_estimate=pl.CostEstimate(flops=flops, bytes_accessed=rows * length * model * 20, transcendentals=rows * length * model),
+        input_output_aliases={len(operands) + k: k for k in range(len(earlier))},
         name="mixer_forward",
-    )(split, keep, x, norm_gain, proj_in, proj_in, proj_in, short_filter, short_filter, cond_filter, slope, shift, skip, proj_out, ffn_gain, *tables)
+    )(*operands, *earlier)
 
 
 def normal_cdf_pdf(x):
@@ -296,11 +300,14 @@
 
 
 def ffn_kernel(
-    sa_ref, og_ref, sat_ref, ogt_ref, wg_ref, wu_ref, wo_ref, out_ref, back_ref, grads_ref, gs, us, ds, hid, gg, ug
+    sa_ref, og_ref, sat_ref, ogt_ref, wg_ref, wu_ref, wo_ref, out_ref, back_ref, grads_ref, *scratch
 ):
     j = pl.program_id(0)
     tokens, model = sa_ref.shape
-    tile = gs.shape[0]
+    streams = [scratch[6 * n : 6 * n + 6] for n in range(2)]
+    tile = streams[0][0].shape[0]
+    half = tokens // 2
+    steps = half // tile
     chunk = 32
 
     @pl.when(j == 0)
@@ -311,31 +318,58 @@
 
         loop(tokens // tile, body)
 
-    def body(i):
-        rows = rows_of(i, tile)
+    def place(n, i, size=tile, offset=0):
+        return pl.ds(pl.multiple_of(n * half + i * tile + offset, size), size)
+
+    def products(n, i):
+        gs, us, ds = streams[n][:3]
+        rows = place(n, i)
         sa = sa_ref[rows, :]
         gs[...] = mm(sa, wg_ref[...])
         us[...] = mm(sa, wu_ref[...])
         ds[...] = mm_t(og_ref[rows, :], wo_ref[...])
+
+    def elementwise(n, i):
+        gs, us, ds, hid, gg, ug = streams[n]
         for c in range(tile // chunk):
             part = slice(c * chunk, (c + 1) * chunk)
             gate, up, dh = gs[part, :], us[part, :], ds[part, :]
             cdf, xpdf = normal_cdf_pdf(gate)
             act = gate * cdf
-            target = pl.ds(pl.multiple_of(i * tile + c * chunk, chunk), chunk)
+            target = place(0, i, chunk, c * chunk)
             hid[target, :] = (act * up).astype(BF)
             gg[target, :] = (dh * up * (cdf + xpdf)).astype(BF)
             ug[target, :] = (dh * act).astype(BF)
-        out_ref[rows, :] += mm(hid[rows, :], wo_ref[...])
-        back_ref[rows, :] += mm_t(gg[rows, :], wg_ref[...]) + mm_t(ug[rows, :], wu_ref[...])
-
-    loop(tokens // tile, body)
-    grads_ref[0] = mm(sat_ref[...], gg[...]).astype(BF)
-    grads_ref[1] = mm(sat_ref[...], ug[...]).astype(BF)
-    grads_ref[2] = mm(ogt_ref[...], hid[...]).astype(BF)
-
-
-def ffn_both(second_act, out_grad, second_turned, grad_turned, ffn_in, ffn_out, piece, pieces, width=512, tile=256):
+
+    def sums(n, i):
+        hid, gg, ug = streams[n][3:]
+        rows, source = place(n, i), place(0, i)
+        out_ref[rows, :] += mm(hid[source, :], wo_ref[...])
+        back_ref[rows, :] += mm_t(gg[source, :], wg_ref[...]) + mm_t(ug[source, :], wu_ref[...])
+
+    products(0, 0)
+    products(1, 0)
+    elementwise(0, 0)
+
+    def body(i):
+        products(0, i + 1)
+        sums(0, i)
+        elementwise(1, i)
+        products(1, i + 1)
+        sums(1, i)
+        elementwise(0, i + 1)
+
+    loop(steps - 1, body)
+    last = steps - 1
+    sums(0, last)
+    elementwise(1, last)
+    sums(1, last)
+    (hid0, gg0, ug0), (hid1, gg1, ug1) = streams[0][3:], streams[1][3:]
+    for k, (ref, first, second) in enumerate(((sat_ref, gg0, gg1), (sat_ref, ug0, ug1), (ogt_ref, hid0, hid1))):
+        grads_ref[k] = (mm(ref[:, 0:half], first[...]) + mm(ref[:, half:tokens], second[...])).astype(BF)
+
+
+def ffn_both(second_act, out_grad, second_turned, grad_turned, ffn_in, ffn_out, piece, pieces, width=512, tile=512):
     tokens, model = second_act.shape
     total_blocks = ffn_out.shape[0] // width
     blocks = total_blocks // pieces
@@ -355,7 +389,7 @@
             pl.BlockSpec((width, model), lambda j: (j + first, 0)),
         ],
         out_specs=[whole, whole, pl.BlockSpec((3, model, width), lambda j: (0, 0, j))],
-        scratch_shapes=[pltpu.VMEM((tile, width), F32)] * 3 + [pltpu.VMEM((tokens, width), BF)] * 3,
+        scratch_shapes=([pltpu.VMEM((tile, width), F32)] * 3 + [pltpu.VMEM((tokens // 2, width), BF)] * 3) * 2,
         compiler_params=pltpu.CompilerParams(dimension_semantics=("arbitrary",), vmem_limit_bytes=LIMIT),
         cost_estimate=pl.CostEstimate(flops=18 * tokens * model * hidden, bytes_accessed=tokens * model * 24 + model * hidden * 12, transcendentals=tokens * hidden),
         name="ffn_both",
@@ -677,6 +711,7 @@
             pltpu.SemaphoreType.DMA((steps,)),
         ],
         compiler_params=pltpu.CompilerParams(collective_id=7, has_side_effects=True),
+        cost_estimate=pl.CostEstimate(flops=20_000_000_000, bytes_accessed=0, transcendentals=0),
         name="exchange_sum",
     )(value)
 
@@ -686,13 +721,15 @@
     return lax.ppermute(value, "seq", [(i, (i + 1) % count) for i in range(count)])
 
 
-def gather_rows(value):
+def gather_rows(value, first=0, count=None):
+    own = value.shape[0] // lax.axis_size("seq")
+    count = own if count is None else count
     if lax.axis_size("seq") != 2:
-        return lax.all_to_all(value, "seq", split_axis=0, concat_axis=1, tiled=True)
+        whole = lax.all_to_all(value, "seq", split_axis=0, concat_axis=1, tiled=True)
+        return whole[first : first + count]
     s = lax.axis_index("seq")
-    own = value.shape[0] // 2
-    mine = lax.dynamic_slice_in_dim(value, s * own, own)
-    other = swapped(lax.dynamic_slice_in_dim(value, (1 - s) * own, own))
+    mine = lax.dynamic_slice_in_dim(value, s * own + first, count)
+    other = swapped(lax.dynamic_slice_in_dim(value, (1 - s) * own + first, count))
     return jnp.concatenate([jnp.where(s == 0, mine, other), jnp.where(s == 0, other, mine)], axis=1)
 
 
@@ -725,18 +762,26 @@
     shaped = lambda a: a.reshape(own, length, model)
     lift = lambda a: a.reshape(1, -1)
 
-    x = gather_rows(inputs)
+    pieces = [(0, 1), (1, own - 1)] if own > 1 else [(0, own)]
+    xs = []
+    for start, size in pieces:
+        xs.append(gather_rows(after(inputs, xs) if xs else inputs, start, size))
     kept = jnp.sum(keep_mask, axis=1)
     kept = kept + swapped(kept) if count == 2 else lax.psum(kept, "seq")
     keep = lax.dynamic_slice_in_dim(kept, first_row, own)
     split = lax.dynamic_slice_in_dim(split_point, first_row, own)
-    whole_grad = flat(gather_rows(after(out_grad, x)))
     tables = spectral_tables(length, lax.axis_index("seq") * (2 * length))
     slope, shift, skip = lift(spec_slope), lift(spec_shift), lift(skip_gain)
 
-    first, q, k, v, mixed, gated, resid, second = mixer_forward(
-        x, split, keep, lift(norm_gain), proj_in, short_filter, cond_filter, slope, shift, skip, proj_out, lift(ffn_gain), tables
-    )
+    held = ()
+    for x, (start, size) in zip(xs, pieces):
+        held = mixer_forward(
+            x, split, keep, lift(norm_gain), proj_in, short_filter, cond_filter, slope, shift, skip, proj_out, lift(ffn_gain), tables, start, own, held
+        )
+        if start == 0:
+            whole_grad = flat(gather_rows(after(out_grad, (xs[-1], held[-1]))))
+    first, q, k, v, mixed, gated, resid, second = held
+    x = jnp.concatenate(xs, axis=0)
     second = flat(second)
     second_turned, grad_turned = second.T, whole_grad.T
     pieces = 2

time: 540 us -> 521 us (0.965)
  waiting for transfers between devices: 66 us -> 17 us
  Pallas kernels: 348 us -> 373 us
  starting transfers between devices: 18.3 us -> 10.8 us
  other arithmetic: 39.4 us -> 46.2 us
  local copies, waits for them, and re-layouts: 31 us -> 37.4 us
    ppermute x8 -> x9, waiting for transfers between devices: 59.4 us -> 0.02 us  [swapped(): lax.ppermute(value, 'seq', [(i, (i + 1) % count) for i in range(count)])]
    pallas_call x1, Pallas kernels: 21.5 us -> 59.9 us  [exchange_sum(): pl.pallas_call(functools.partial(exchange_sum_kernel, rows, seq), out_sha...]
    pallas_call x2, Pallas kernels: 131 us -> 110 us  [ffn_both(): pl.pallas_call(ffn_kernel, out_shape=[shape((tokens, model), F32), shape(...]
    reduce_scatter x1, waiting for transfers between devices: 6.54 us -> 16.9 us  [per_device_rows(): chain = lax.psum_scatter(grads[0], 'rows', scatter_dimension=1, tiled=True)]
    reduce_scatter x1, starting transfers between devices: 9.22 us -> 0.04 us  [per_device_rows(): lax.psum_scatter(mix_part, 'rows', scatter_dimension=0, tiled=True)]
    pallas_call x1 -> x2, Pallas kernels: 72.3 us -> 79.7 us  [mixer_forward(): pl.pallas_call(functools.partial(mixer_forward_kernel, first_row, len(ear...]
  transfers between devices with their start and end apart: 11 -> 12, of which waited for: 5 -> 1; matrix products, arithmetic and copies ran while one was open for 14% -> 15% of each run, Pallas kernels for 53% -> 62%
where the time goes in v4:
time: 521 us; the launch traced here: 517 us
  Pallas kernels  373 us (72%)
  other arithmetic  46.2 us (9%)
  local copies, waits for them, and re-layouts  37.4 us (7%)
  matrix products  17.7 us (3%)
  waiting for transfers between devices  17 us (3%)
  between operations  14.5 us (3%)
  starting transfers between devices  10.8 us (2%)
    pallas_call x2, Pallas kernels, ffn_both(): pl.pallas_call(ffn_kernel, out_shape=[shape((tokens, model), F32), shape(...  110 us
    pallas_call x1, Pallas kernels, mixer_backward(): pl.pallas_call(mixer_backward_kernel, out_shape=[shape((rows, length, 3 *...  80 us
    pallas_call x2, Pallas kernels, mixer_forward(): pl.pallas_call(functools.partial(mixer_forward_kernel, first_row, len(ear...  79.7 us
    pallas_call x1, Pallas kernels, exchange_sum(): pl.pallas_call(functools.partial(exchange_sum_kernel, rows, seq), out_sha...  59.9 us
    pallas_call x1, Pallas kernels, input_back(): pl.pallas_call(functools.partial(input_back_kernel, width), out_shape=[sh...  23.8 us
    pallas_call x1, Pallas kernels, norm_back(): pl.pallas_call(functools.partial(norm_back_kernel, pieces), out_shape=[sh...  19.4 us
    dot_general x2, matrix products, turn(): lax.dot_general(a, b, (((0,), (0,)), ((), ())), preferred_element_type=F32)  17.7 us
    reduce_scatter x1, waiting for transfers between devices, per_device_rows(): chain = lax.psum_scatter(grads[0], 'rows', scatter_dimension=1, tiled=True)  16.9 us
  transfers between devices with their start and end apart: 12, of which 1 were waited for; matrix products, arithmetic and copies ran while one was open for 15% of the time, Pallas kernels for 62%

profile of v4, /device:TPU:0, one launch (start us, length us, event | category | flops | bytes accessed | tf_op | source)
XLA Modules:
  0.0 516.6 jit_solution(3422992049483614562)
XLA Ops:
  8.0 3.1 collective-permute-start
  11.1 2.1 constant_dynamic-slice_fusion.4
  16.5 5.0 multiply_convert_fusion.1
  30.6 2.6 copy.57.fwd_ref
  40.6 2.0 collective-permute-start.2
  42.6 39.7 %mixer_forward.2 = (bf16[2,1024,768]{2,1,0:T(8,128)(2,1)}, bf16[2,1024,768]{2,1,0:T(8,128)(2,1)}, bf16[2,1024,768]{2,1,0:T(8,128)(2,1)}, bf16[2,1024,768]{2,1,0:...) custom-call(s32[2]{0:T(128)} %dynamic_slice.36.split_ref, ...), custom_call_target="tpu_custom_call" | custom-call | flops 9663676416 | bytes 15728640 | tf_op jit(solution)/shard_map/mixer_forward/pallas_call | solution.py:270
  82.3 1.6 broadcast_select_fusion.7
  86.6 40.1 %mixer_forward.3 = (bf16[2,1024,768]{2,1,0:T(8,128)(2,1)}, bf16[2,1024,768]{2,1,0:T(8,128)(2,1)}, bf16[2,1024,768]{2,1,0:T(8,128)(2,1)}, bf16[2,1024,768]{2,1,0:...) custom-call(s32[2]{0:T(128)} %dynamic_slice.36.split_ref, ...), custom_call_target="tpu_custom_call", output_to_operand_aliasing={{0}: (19, {}), {1}: (20, {}), {2}: (21, {}), {3}: (22, {}),... | custom-call | flops 9663676416 | bytes 15728640 | tf_op jit(solution)/shard_map/mixer_forward/pallas_call | solution.py:270
  126.7 4.9 copy.71
  131.6 1.6 broadcast_select_fusion.5
  133.5 3.5 copy.61.ogt_ref
  136.9 55.0 %ffn_both.2 = (f32[2048,768]{1,0:T(8,128)}, f32[2048,768]{1,0:T(8,128)}, bf16[3,768,1536]{2,1,0:T(8,128)(2,1)}) custom-call(bf16[2048,768]{1,0:T(8,128)(2,1)} %bitcast.47, bf16[2048,768]{1,0:T(8,128)(2,1)} %bitcast.42, bf16[768,2048]{1,0:T(8,128)(2,1)} %bitcast.54, bf16[768,2048]{1,0:T(8,128)(2,1)} %copy.61.ogt_ref, bf16[768,6144]{1,0:T(8,128)(2,1)} %wu_ref.3, ...), custom_call_target="tpu_custom_call" | custom-call | flops 43486543872 | bytes 51904512 | tf_op jit(solution)/shard_map/ffn_both/pallas_call | solution.py:381
  192.0 55.4 %ffn_both.3 = (f32[2048,768]{1,0:T(8,128)}, f32[2048,768]{1,0:T(8,128)}, bf16[3,768,1536]{2,1,0:T(8,128)(2,1)}) custom-call(bf16[2048,768]{1,0:T(8,128)(2,1)} %bitcast.48, bf16[2048,768]{1,0:T(8,128)(2,1)} %bitcast.43, bf16[768,2048]{1,0:T(8,128)(2,1)} %bitcast.55, bf16[768,2048]{1,0:T(8,128)(2,1)} %copy.61.ogt_ref, bf16[768,6144]{1,0:T(8,128)(2,1)} %wu_ref.3, ...), custom_call_target="tpu_custom_call" | custom-call | flops 43486543872 | bytes 51904512 | tf_op jit(solution)/shard_map/ffn_both/pallas_call | solution.py:381
  247.4 19.4 %norm_back.1 = (bf16[2048,768]{1,0:T(8,128)(2,1)}, f32[2048,768]{1,0:T(8,128)}, bf16[2048,768]{1,0:T(8,128)(2,1)}, f32[8,768]{1,0:T(8,128)}) custom-call(f32[2048,768]{1,0:T(8,128)} %bitcast.45, f32[2048,768]{1,0:T(8,128)} %get-tuple-element.63.refs_0_, f32[2048,768]{1,0:T(8,128)} %get-tuple-element.64.refs_1_, f32[2048,768]{1,0:T(8,128)} %get-tuple-element.65.refs_2_, ...), custom_call_target="tpu_custom_call" | custom-call | flops 31457280 | bytes 34603008 | tf_op jit(solution)/shard_map/norm_back/pallas_call | solution.py:432
  266.7 16.9 %reduce-scatter.4.cloned.1.call-done = bf16[3,48,1536]{2,1,0:T(8,128)(2,1)} async-done(((bf16[3,768,1536]{2,1,0:T(8,128)(2,1)}), bf16[3,48,1536]{2,1,0:T(8,128)(2,1)}) %reduce-scatter.4.cloned.1.call-update) | async-done | bytes 442384 | tf_op jit(solution)/shard_map/reduce_scatter | solution.py:794
  283.7 1.8 copy-done.10
  285.5 5.6 %convolution_convert_fusion = bf16[768,768]{0,1:T(8,128)(2,1)} fusion(bf16[2048,768]{1,0:T(8,128)(2,1)S(1)} %bitcast.49, bf16[2048,768]{1,0:T(8,128)(2,1)} %get-tuple-element.72), kind=kOutput, calls=%fused_computation.15 | convolution fusion | flops 2416508928 | bytes 7471104 | tf_op jit(solution)/shard_map/dot_general | solution.py:659
  291.1 2.4 copy.68
  293.4 80.0 %mixer_backward.1 = (bf16[2,1024,2304]{2,1,0:T(8,128)(2,1)}, f32[12,8,768]{2,1,0:T(8,128)}) custom-call(s32[2]{0:T(128)} %dynamic_slice.36.split_ref, s32[2]{0:T(128)} %dynamic_slice.37.keep_ref, bf16[2,1024,768]{2,1,0:T(8,128)(2,1)} %bitcast.60, bf16[2,1024,768]{2,1,0:T(8,128)(2,1)} %get-tuple-element.73.q_ref, ...), custom_call_target="tpu_custom_call" | custom-call | flops 18522046464 | bytes 31457280 | tf_op jit(solution)/shard_map/mixer_backward/pallas_call | solution.py:592
  373.4 12.1 %bitcast_convert_fusion = bf16[768,2304]{1,0:T(8,128)(2,1)S(1)} fusion(bf16[2,1024,768]{2,1,0:T(8,128)(2,1)} %get-tuple-element.79, bf16[2,1024,2304]{2,1,0:T(8,128)(2,1)} %get-tuple-element.77), kind=kOutput, calls=%fused_computation | convolution fusion | flops 7249526784 | bytes 16121856 | tf_op jit(solution)/shard_map/dot_general | solution.py:659
  385.6 2.8 pad_maximum_fusion
  390.3 1.8 maximum_maximum_fusion
  394.5 1.6 collective-permute-start.4
  396.6 1.6 collective-permute-start.8
  398.2 23.8 %input_back.1 = (bf16[2048,768]{1,0:T(8,128)(2,1)}, f32[8,768]{1,0:T(8,128)}) custom-call(bf16[2048,768]{1,0:T(8,128)(2,1)} %bitcast.56, f32[2048,768]{1,0:T(8,128)} %get-tuple-element.68.grad_ref, f32[1,768]{1,0:T(1,128)} %reshape.83.norm_gain_ref.gain_ref, bf16[768,2304]{1,0:T(8,128)(2,1)} %w_ref.1, bf16[2048,2304]{1,0:T(8,128)(2,1)} %bitcast.61), custom_call_target="tpu_custom_call" | custom-call | flops 7247757312 | bytes 22020096 | tf_op jit(solution)/shard_map/input_back/pallas_call | solution.py:645
  422.0 1.6 constant_dynamic-slice_fusion
  424.8 59.9 %exchange_sum.1 = f32[14,768]{1,0:T(8,128)} custom-call(f32[14,768]{1,0:T(8,128)} %maximum_reduce_fusion.x_ref), custom_call_target="tpu_custom_call" | custom-call | flops 20000000000 | tf_op jit(solution)/shard_map/exchange_sum/pallas_call | solution.py:702
  484.7 1.7 slice_reduce_fusion
  494.4 4.8 broadcast_select_fusion.1
  499.2 1.4 collective-permute-start.6
  500.7 3.8 pad_maximum_fusion.2
  504.5 3.1 maximum_convert_fusion
  (132 shorter events, 39.7 us)
Async XLA Ops:
  7.2 276.4 %reduce-scatter.4.cloned.1.call-start = ((), (), s32[]{:S(2)}) async-start(), calls=%async_computation.3 | async-start | bytes 7520256 | tf_op jit(solution)/shard_map/reduce_scatter | solution.py:794
  8.0 27.2 %collective-permute-start = (s32[4]{0:T(128)S(1)}, s32[4]{0:T(128)S(1)}, u32[]{:S(2)}, u32[]{:S(2)}) collective-permute-start(s32[4]{0:T(128)S(1)} %reduce_sum.18), channel_id=1, source_target_pairs={{0,1},{1,0},{2,3},{3,2},{4,5},{5,4},{6,7},{7,6},{8,9},{9,8},{10,11... | collective-permute-start | bytes 56 | tf_op jit(solution)/shard_map/ppermute | solution.py:721
  13.2 22.7 %collective-permute-start.1 = (bf16[1,512,768]{2,1,0:T(8,128)(2,1)}, bf16[1,512,768]{2,1,0:T(8,128)(2,1)}, u32[]{:S(2)}, u32[]{:S(2)}) collective-permute-start(bf16[1,512,768]{2,1,0:T(8,128)(2,1)} %constant_dynamic-slice_fusion.4), channel_id=1, source_target_pairs={{0,1},{1,0},{2,3},{3,2},{4,5},{5,4},{6,7},{7,6},{8,9},{9,8},{10,11... | collective-permute-start | bytes 2359304 | tf_op jit(solution)/shard_map/ppermute | solution.py:721
  16.5 8.8 %copy-start.21 = (f32[768]{0:T(1024)S(1)}, f32[768]{0:T(1024)}, u32[]{:S(2)}) copy-start(f32[768]{0:T(1024)} %param.18) | copy-start | bytes 9220
  16.5 9.3 %copy-start.22 = (f32[768]{0:T(1024)S(1)}, f32[768]{0:T(1024)}, u32[]{:S(2)}) copy-start(f32[768]{0:T(1024)} %param.22) | copy-start | bytes 9220
  16.5 9.9 %copy-start.23 = (f32[768]{0:T(1024)S(1)}, f32[768]{0:T(1024)}, u32[]{:S(2)}) copy-start(f32[768]{0:T(1024)} %param.23) | copy-start | bytes 9220
  16.5 10.5 %copy-start.24 = (f32[768]{0:T(1024)S(1)}, f32[768]{0:T(1024)}, u32[]{:S(2)}) copy-start(f32[768]{0:T(1024)} %param.24) | copy-start | bytes 9220
  16.5 11.0 %copy-start.25 = (f32[768]{0:T(1024)S(1)}, f32[768]{0:T(1024)}, u32[]{:S(2)}) copy-start(f32[768]{0:T(1024)} %param.26) | copy-start | bytes 9220
  23.8 9.4 %copy-start.26 = (s32[4]{0:T(128)S(1)}, s32[4]{0:T(128)}, u32[]{:S(2)}) copy-start(s32[4]{0:T(128)} %param.16) | copy-start | bytes 52
  33.8 2.5 copy-start.14
  37.5 2.2 copy-start.3
  40.6 41.7 %collective-permute-start.2 = (bf16[1,512,768]{2,1,0:T(8,128)(2,1)}, bf16[1,512,768]{2,1,0:T(8,128)(2,1)}, u32[]{:S(2)}, u32[]{:S(2)}) collective-permute-start(bf16[1,512,768]{2,1,0:T(8,128)(2,1)} %constant_dynamic-slice_fusion.3), channel_id=1, source_target_pairs={{0,1},{1,0},{2,3},{3,2},{4,5},{5,4},{6,7},{7,6},{8,9},{9,8},{10,11... | collective-permute-start | bytes 2359304 | tf_op jit(solution)/shard_map/ppermute | solution.py:721
  82.3 3.1 copy-start.15
  83.9 2.7 copy-start.5
  83.9 2.7 copy-start.7
  86.6 45.0 %collective-permute-start.3 = (bf16[2,512,768]{2,1,0:T(8,128)(2,1)}, bf16[2,512,768]{2,1,0:T(8,128)(2,1)}, u32[]{:S(2)}, u32[]{:S(2)}) collective-permute-start(bf16[2,512,768]{2,1,0:T(8,128)(2,1)} %constant_dynamic-slice_fusion.2), channel_id=1, source_target_pairs={{0,1},{1,0},{2,3},{3,2},{4,5},{5,4},{6,7},{7,6},{8,9},{9,8},{10,11... | collective-permute-start | bytes 4718600 | tf_op jit(solution)/shard_map/ppermute | solution.py:721
  126.7 4.9 copy-start.16
  133.5 3.5 copy-start
  191.9 196.5 %reduce-scatter.6.cloned.1.call-start = ((), (), s32[]{:S(2)}) async-start(), calls=%async_computation.4 | async-start | bytes 7520256 | tf_op jit(solution)/shard_map/reduce_scatter | solution.py:801
  283.7 215.6 %reduce-scatter.8.cloned.1.call-start = ((), (), s32[]{:S(2)}) async-start(), calls=%async_computation.5 | async-start | bytes 5013504 | tf_op jit(solution)/shard_map/reduce_scatter | solution.py:807
  373.4 12.1 %copy-start.9 = (bf16[768,768]{1,0:T(8,128)(2,1)S(1)}, bf16[768,768]{1,0:T(8,128)(2,1)}, u32[]{:S(2)}) copy-start(bf16[768,768]{1,0:T(8,128)(2,1)} %copy.68) | copy-start | bytes 3538948
  390.2 3.0 copy-start.11
  394.5 98.5 %collective-permute-start.4 = (bf16[2,512,768]{2,1,0:T(8,128)(2,1)}, bf16[2,512,768]{2,1,0:T(8,128)(2,1)}, u32[]{:S(2)}, u32[]{:S(2)}) collective-permute-start(bf16[2,512,768]{2,1,0:T(8,128)(2,1)} %constant_dynamic-slice_fusion.1), channel_id=1, source_target_pairs={{0,1},{1,0},{2,3},{3,2},{4,5},{5,4},{6,7},{7,6},{8,9},{9,8},{10,11... | collective-permute-start | bytes 4718600 | tf_op jit(solution)/shard_map/ppermute | solution.py:721
  396.1 92.3 %collective-permute-start.7 = (bf16[3,48,1536]{2,1,0:T(8,128)(2,1)}, bf16[3,48,1536]{2,1,0:T(8,128)(2,1)}, u32[]{:S(2)}, u32[]{:S(2)}) collective-permute-start(bf16[3,48,1536]{2,1,0:T(8,128)(2,1)} %reduce-scatter.4.cloned.1.call-done), channel_id=1, source_target_pairs={{0,1},{1,0},{2,3},{3,2},{4,5},{5,4},{6,7},{7,6},{8,9},{9,8},{10,11... | collective-permute-start | bytes 1327112 | tf_op jit(solution)/shard_map/ppermute | solution.py:721
  396.6 93.1 %collective-permute-start.8 = (bf16[3,48,1536]{2,1,0:T(8,128)(2,1)}, bf16[3,48,1536]{2,1,0:T(8,128)(2,1)}, u32[]{:S(2)}, u32[]{:S(2)}) collective-permute-start(bf16[3,48,1536]{2,1,0:T(8,128)(2,1)} %reduce-scatter.6.cloned.1.call-done), channel_id=1, source_target_pairs={{0,1},{1,0},{2,3},{3,2},{4,5},{5,4},{6,7},{7,6},{8,9},{9,8},{10,11... | collective-permute-start | bytes 1327112 | tf_op jit(solution)/shard_map/ppermute | solution.py:721
  422.0 2.1 copy-start.17
  422.0 2.1 copy-start.19
  423.6 69.5 %collective-permute-start.5 = (bf16[2,512,768]{2,1,0:T(8,128)(2,1)S(1)}, bf16[2,512,768]{2,1,0:T(8,128)(2,1)}, u32[]{:S(2)}, u32[]{:S(2)}) collective-permute-start(bf16[2,512,768]{2,1,0:T(8,128)(2,1)S(1)} %constant_dynamic-slice_fusion), channel_id=1, source_target_pairs={{0,1},{1,0},{2,3},{3,2},{4,5},{5,4},{6,7},{7,6},{8,9},{9,8},{10,11... | collective-permute-start | bytes 4718600 | tf_op jit(solution)/shard_map/ppermute | solution.py:721
  490.9 2.2 copy-start.12
  491.0 3.5 copy-start.13
  499.2 8.4 %collective-permute-start.6 = (bf16[48,3072]{1,0:T(8,128)(2,1)}, bf16[48,3072]{1,0:T(8,128)(2,1)S(1)}, u32[]{:S(2)}, u32[]{:S(2)}) collective-permute-start(bf16[48,3072]{1,0:T(8,128)(2,1)} %reduce-scatter.8.cloned.1.call-done), channel_id=1, source_target_pairs={{0,1},{1,0},{2,3},{3,2},{4,5},{5,4},{6,7},{7,6},{8,9},{9,8},{10,11... | collective-permute-start | bytes 884744 | tf_op jit(solution)/shard_map/ppermute | solution.py:721
  504.5 3.1 copy-start.18
  (7 other events, 10.8 us)
Sparse Core Ops, SparseCore 0:
  192.0 91.5 reduce-scatter.3
  287.6 89.5 reduce-scatter.5
  388.6 78.1 reduce-scatter.7

commit v5 on v4

--- a/solution.py
+++ b/solution.py
@@ -369,11 +369,11 @@
         grads_ref[k] = (mm(ref[:, 0:half], first[...]) + mm(ref[:, half:tokens], second[...])).astype(BF)
 
 
-def ffn_both(second_act, out_grad, second_turned, grad_turned, ffn_in, ffn_out, piece, pieces, width=512, tile=512):
+def ffn_both(second_act, out_grad, second_turned, grad_turned, ffn_in, ffn_out, share, width=512, tile=512):
     tokens, model = second_act.shape
     total_blocks = ffn_out.shape[0] // width
-    blocks = total_blocks // pieces
-    first = piece * blocks
+    first, last = (total_blocks * n // 3 for n in share)
+    blocks = last - first
     hidden = blocks * width
     shape = jax.ShapeDtypeStruct
     whole = once((tokens, model), lambda j: (0, 0))
@@ -663,7 +663,7 @@
     return lax.optimization_barrier((value, earlier))[0]
 
 
-def exchange_sum_kernel(rows, seq, x_ref, out_ref, slots, total, send_sem, recv_sem):
+def exchange_sum_kernel(rows, seq, x_ref, send_ref, out_ref, other_ref, slots, total, send_sem, recv_sem, far_send_sem, far_recv_sem):
     r, s = lax.axis_index("rows"), lax.axis_index("seq")
     partners = []
     bit = 1
@@ -678,6 +678,12 @@
     for partner in partners:
         pl.semaphore_signal(barrier, inc=1, device_id=partner, device_id_type=pl.DeviceIdType.MESH)
     pl.semaphore_wait(barrier, len(partners))
+    part = other_ref.shape[1]
+    far = pltpu.make_async_remote_copy(
+        src_ref=send_ref.at[:, pl.ds(pl.multiple_of((1 - s) * part, part), part)], dst_ref=other_ref,
+        send_sem=far_send_sem, recv_sem=far_recv_sem, device_id=(r, 1 - s), device_id_type=pl.DeviceIdType.MESH,
+    )
+    far.start()
     total[0] = x_ref[...]
     for step, partner in enumerate(partners):
         copy = pltpu.make_async_remote_copy(
@@ -688,32 +694,60 @@
         copy.wait()
         total[step + 1] = total[step] + slots[step]
     out_ref[...] = total[len(partners)]
+    far.wait()
 
 
 def power_of_two(n):
     return n & (n - 1) == 0
 
 
-def exchange_sum(value):
+def exchange_sum(value, whole_rows):
     rows, seq = lax.axis_size("rows"), lax.axis_size("seq")
-    if not (power_of_two(rows) and power_of_two(seq)):
-        return lax.psum(value, ("rows", "seq"))
-    steps = (rows.bit_length() - 1) + (seq.bit_length() - 1)
-    return pl.pallas_call(
+    if not (power_of_two(rows) and seq == 2):
+        return lax.psum(value, ("rows", "seq")), scatter_rows(whole_rows).astype(F32)
+    steps = rows.bit_length()
+    own, length, model = whole_rows.shape
+    part = length // 2
+    shape = jax.ShapeDtypeStruct
+    total, other = pl.pallas_call(
         functools.partial(exchange_sum_kernel, rows, seq),
-        out_shape=jax.ShapeDtypeStruct(value.shape, value.dtype),
-        in_specs=[pl.BlockSpec(memory_space=pltpu.VMEM)],
-        out_specs=pl.BlockSpec(memory_space=pltpu.VMEM),
+        out_shape=[shape(value.shape, value.dtype), shape((own, part, model), whole_rows.dtype)],
+        in_specs=[pl.BlockSpec(memory_space=pltpu.VMEM), pl.BlockSpec(memory_space=pl.ANY)],
+        out_specs=[pl.BlockSpec(memory_space=pltpu.VMEM), pl.BlockSpec(memory_space=pl.ANY)],
         scratch_shapes=[
             pltpu.VMEM((steps, *value.shape), value.dtype),
             pltpu.VMEM((steps + 1, *value.shape), value.dtype),
             pltpu.SemaphoreType.DMA((steps,)),
             pltpu.SemaphoreType.DMA((steps,)),
+            pltpu.SemaphoreType.DMA,
+            pltpu.SemaphoreType.DMA,
         ],
         compiler_params=pltpu.CompilerParams(collective_id=7, has_side_effects=True),
         cost_estimate=pl.CostEstimate(flops=20_000_000_000, bytes_accessed=0, transcendentals=0),
         name="exchange_sum",
-    )(value)
+    )(value, whole_rows)
+    return total, assemble(whole_rows, other)
+
+
+def assemble_kernel(own, s_ref, mine_ref, other_ref, out_ref):
+    out_ref[...] = jnp.where(pl.program_id(0) // own == s_ref[0], mine_ref[...], other_ref[...]).astype(F32)
+
+
+def assemble(whole_rows, other):
+    own, part, model = other.shape
+    block = (None, part, model)
+    return pl.pallas_call(
+        functools.partial(assemble_kernel, own),
+        out_shape=jax.ShapeDtypeStruct((2 * own, part, model), F32),
+        grid_spec=pltpu.PrefetchScalarGridSpec(
+            num_scalar_prefetch=1,
+            grid=(2 * own,),
+            in_specs=[pl.BlockSpec(block, lambda i, s: (i % own, s[0], 0)), pl.BlockSpec(block, lambda i, s: (i % own, 0, 0))],
+            out_specs=pl.BlockSpec(block, lambda i, s: (i, 0, 0)),
+        ),
+        compiler_params=pltpu.CompilerParams(dimension_semantics=("arbitrary",), vmem_limit_bytes=LIMIT),
+        name="assemble",
+    )(lax.axis_index("seq").astype(jnp.int32)[None], whole_rows, other)
 
 
 def swapped(value):
@@ -784,33 +818,28 @@
     x = jnp.concatenate(xs, axis=0)
     second = flat(second)
     second_turned, grad_turned = second.T, whole_grad.T
-    pieces = 2
     totals, backs, grads = [], [], []
-    for piece in range(pieces):
-        total, back, grad = ffn_both(second, whole_grad, second_turned, grad_turned, ffn_in, ffn_out, piece, pieces)
+    for share in ((0, 1), (1, 3)):
+        total, back, grad = ffn_both(second, whole_grad, second_turned, grad_turned, ffn_in, ffn_out, share)
         totals.append(total)
         backs.append(back)
         grads.append(grad)
-    chain = lax.psum_scatter(grads[0], "rows", scatter_dimension=1, tiled=True)
-    ffn_shares = [chain]
+    early_share = lax.psum_scatter(grads[0], "rows", scatter_dimension=1, tiled=True)
     output, resid_grad, branch_low, ffn_gain_part = norm_back(flat(resid), totals, backs, whole_grad, lift(ffn_gain))
     output = scatter_rows(shaped(output))
     out_part = turn(flat(gated), branch_low)
-    for grad in grads[1:]:
-        grad, chain, branch_low = lax.optimization_barrier((grad, chain, branch_low))
-        chain = lax.psum_scatter(grad, "rows", scatter_dimension=1, tiled=True)
-        ffn_shares.append(chain)
+    grad, branch_low, early_share = lax.optimization_barrier((grads[1], branch_low, early_share))
+    late_share = lax.psum_scatter(grad, "rows", scatter_dimension=1, tiled=True)
     proj_grad, chan = mixer_backward(shaped(branch_low), split, keep, q, k, v, mixed, proj_out, short_filter, cond_filter, slope, shift, skip, tables)
     proj_grad = flat_wide(proj_grad)
     mix_part = jnp.concatenate([out_part, turn(flat(first), proj_grad)], axis=1)
-    mix_part, *ffn_shares = lax.optimization_barrier((mix_part, *ffn_shares))
+    mix_part, late_share = lax.optimization_barrier((mix_part, late_share))
     mix_share = lax.psum_scatter(mix_part, "rows", scatter_dimension=0, tiled=True)
     proj_grad = after(proj_grad, mix_part)
     input_grad, norm_gain_part = input_back(flat(x), resid_grad, lift(norm_gain), proj_in, proj_grad, width)
-    input_grad = scatter_rows(shaped(input_grad)).astype(F32)
-    ffn_shares = [seq_sum(share) for share in ffn_shares]
+    ffn_shares = [seq_sum(early_share), seq_sum(late_share)]
     small = jnp.sum(jnp.concatenate([ffn_gain_part[None], norm_gain_part[None], chan], 0), axis=1)
-    small = exchange_sum(small)
+    small, input_grad = exchange_sum(small, shaped(input_grad))
     scale = 1.0 / length
     mix_share = seq_sum(mix_share)
     in_share = mix_share[:, model:].reshape(-1, model // width, 3, width).transpose(0, 2, 1, 3)

time: 521 us -> 490 us (0.940)
  Pallas kernels: 373 us -> 357 us
  other arithmetic: 46.2 us -> 39.3 us
  waiting for transfers between devices: 17 us -> 11.1 us
    pallas_call x1, Pallas kernels: 59.9 us -> 38.6 us  [exchange_sum(): pl.pallas_call(functools.partial(exchange_sum_kernel, rows, seq), out_sha...]
    reduce_scatter x2, waiting for transfers between devices: 16.9 us -> 3.27 us  [the longest x1 3.25 us: per_device_rows(): late_share = lax.psum_scatter(grad, 'rows', scatter_dimension=1, tiled=True)]
    ppermute x9 -> x8, waiting for transfers between devices: 0.02 us -> 7.81 us  [swapped(): lax.ppermute(value, 'seq', [(i, (i + 1) % count) for i in range(count)])]
    pallas_call x0 -> x1, Pallas kernels: none -> 5.91 us  [assemble(): pl.pallas_call(functools.partial(assemble_kernel, own), out_shape=jax.Sha...]
    ppermute x9 -> x8, starting transfers between devices: 10.6 us -> 11.4 us  [swapped(): lax.ppermute(value, 'seq', [(i, (i + 1) % count) for i in range(count)])]
  transfers between devices with their start and end apart: 12 -> 11, of which waited for: 1 -> 3; matrix products, arithmetic and copies ran while one was open for 15% -> 15% of each run, Pallas kernels for 62% -> 66%
where the time goes in v5:
time: 490 us; the launch traced here: 485 us
  Pallas kernels  357 us (73%)
  other arithmetic  39.3 us (8%)
  local copies, waits for them, and re-layouts  33.9 us (7%)
  matrix products  17.7 us (4%)
  between operations  14.5 us (3%)
  starting transfers between devices  11.6 us (2%)
  waiting for transfers between devices  11.1 us (2%)
    pallas_call x2, Pallas kernels, ffn_both(): pl.pallas_call(ffn_kernel, out_shape=[shape((tokens, model), F32), shape(...  111 us
    pallas_call x1, Pallas kernels, mixer_backward(): pl.pallas_call(mixer_backward_kernel, out_shape=[shape((rows, length, 3 *...  80.1 us
    pallas_call x2, Pallas kernels, mixer_forward(): pl.pallas_call(functools.partial(mixer_forward_kernel, first_row, len(ear...  79.7 us
    pallas_call x1, Pallas kernels, exchange_sum(): pl.pallas_call(functools.partial(exchange_sum_kernel, rows, seq), out_sha...  38.6 us
    pallas_call x1, Pallas kernels, input_back(): pl.pallas_call(functools.partial(input_back_kernel, width), out_shape=[sh...  23.5 us
    pallas_call x1, Pallas kernels, norm_back(): pl.pallas_call(functools.partial(norm_back_kernel, pieces), out_shape=[sh...  19.1 us
    dot_general x2, matrix products, turn(): lax.dot_general(a, b, (((0,), (0,)), ((), ())), preferred_element_type=F32)  17.7 us
    ppermute x8, starting transfers between devices, swapped(): lax.ppermute(value, 'seq', [(i, (i + 1) % count) for i in range(count)])  11.4 us
  transfers between devices with their start and end apart: 11, of which 3 were waited for; matrix products, arithmetic and copies ran while one was open for 15% of the time, Pallas kernels for 66%

profile of v5, /device:TPU:0, one launch (start us, length us, event | category | flops | bytes accessed | tf_op | source)
XLA Modules:
  0.0 485.4 jit_solution(2216377163064326982)
XLA Ops:
  8.0 3.1 collective-permute-start
  11.1 2.1 constant_dynamic-slice_fusion.3
  14.3 2.1 fusion.51
  19.4 5.0 %multiply_convert_fusion.1 = (bf16[256,256]{0,1:T(8,128)(2,1)S(1)}, bf16[256,256]{0,1:T(8,128)(2,1)S(1)}, bf16[256,256]{0,1:T(8,128)(2,1)S(1)}, bf16[256,256]{0,1:T(8,128)(2,1)S(1)}) fusion(f32[256]{0:T(256)S(1)} %fusion.54, s32[256]{0:T(256)S(1)} %iota_and_fusion, s32[256]{0:T(256)S(1)} %fusion.58, s32[]{:T(128)S(6)} %mul.128, ...), kind=kLoop, calls=%fused_computation.108 | loop fusion | flops 5505024 | bytes 528388 | tf_op jit(solution)/shard_map/convert.6
  30.5 2.6 copy.57.fwd_ref
  40.6 2.0 collective-permute-start.2
  42.6 39.6 %mixer_forward.2 = (bf16[2,1024,768]{2,1,0:T(8,128)(2,1)}, bf16[2,1024,768]{2,1,0:T(8,128)(2,1)}, bf16[2,1024,768]{2,1,0:T(8,128)(2,1)}, bf16[2,1024,768]{2,1,0:...) custom-call(s32[2]{0:T(128)} %dynamic_slice.30.split_ref, ...), custom_call_target="tpu_custom_call" | custom-call | flops 9663676416 | bytes 15728640 | tf_op jit(solution)/shard_map/mixer_forward/pallas_call | solution.py:270
  86.7 40.1 %mixer_forward.3 = (bf16[2,1024,768]{2,1,0:T(8,128)(2,1)}, bf16[2,1024,768]{2,1,0:T(8,128)(2,1)}, bf16[2,1024,768]{2,1,0:T(8,128)(2,1)}, bf16[2,1024,768]{2,1,0:...) custom-call(s32[2]{0:T(128)} %dynamic_slice.30.split_ref, ...), custom_call_target="tpu_custom_call", output_to_operand_aliasing={{0}: (19, {}), {1}: (20, {}), {2}: (21, {}), {3}: (22, {}),... | custom-call | flops 9663676416 | bytes 15728640 | tf_op jit(solution)/shard_map/mixer_forward/pallas_call | solution.py:270
  126.8 4.9 %copy.71 = bf16[2048,768]{0,1:T(8,128)(2,1)} copy(bf16[2048,768]{1,0:T(8,128)(2,1)} %bitcast.47) | data formatting | bytes 6291456 | tf_op jit(solution)/shard_map/reshape | solution.py:794
  133.5 3.3 copy.61.ogt_ref
  136.9 39.3 %ffn_both.2 = (f32[2048,768]{1,0:T(8,128)}, f32[2048,768]{1,0:T(8,128)}, bf16[3,768,1024]{2,1,0:T(8,128)(2,1)}) custom-call(bf16[2048,768]{1,0:T(8,128)(2,1)} %bitcast.48, bf16[2048,768]{1,0:T(8,128)(2,1)} %bitcast.43, bf16[768,2048]{1,0:T(8,128)(2,1)} %bitcast.52, bf16[768,2048]{1,0:T(8,128)(2,1)} %copy.61.ogt_ref, bf16[768,6144]{1,0:T(8,128)(2,1)} %wu_ref.3, ...), custom_call_target="tpu_custom_call" | custom-call | flops 28991029248 | bytes 47185920 | tf_op jit(solution)/shard_map/ffn_both/pallas_call | solution.py:381
  176.2 71.2 %ffn_both.3 = (f32[2048,768]{1,0:T(8,128)}, f32[2048,768]{1,0:T(8,128)}, bf16[3,768,2048]{2,1,0:T(8,128)(2,1)}) custom-call(bf16[2048,768]{1,0:T(8,128)(2,1)} %bitcast.49, bf16[2048,768]{1,0:T(8,128)(2,1)} %bitcast.44, bf16[768,2048]{1,0:T(8,128)(2,1)} %bitcast.53, bf16[768,2048]{1,0:T(8,128)(2,1)} %copy.61.ogt_ref, bf16[768,6144]{1,0:T(8,128)(2,1)} %wu_ref.3, ...), custom_call_target="tpu_custom_call" | custom-call | flops 57982058496 | bytes 56623104 | tf_op jit(solution)/shard_map/ffn_both/pallas_call | solution.py:381
  247.5 19.1 %norm_back.1 = (bf16[2048,768]{1,0:T(8,128)(2,1)}, f32[2048,768]{1,0:T(8,128)}, bf16[2048,768]{1,0:T(8,128)(2,1)}, f32[8,768]{1,0:T(8,128)}) custom-call(f32[2048,768]{1,0:T(8,128)} %bitcast.46, f32[2048,768]{1,0:T(8,128)} %get-tuple-element.65.refs_0_, f32[2048,768]{1,0:T(8,128)} %get-tuple-element.66.refs_1_, f32[2048,768]{1,0:T(8,128)} %get-tuple-element.67.refs_2_, ...), custom_call_target="tpu_custom_call" | custom-call | flops 31457280 | bytes 34603008 | tf_op jit(solution)/shard_map/norm_back/pallas_call | solution.py:432
  266.7 1.8 copy-done.10
  268.5 5.6 %convolution_convert_fusion = bf16[768,768]{0,1:T(8,128)(2,1)} fusion(bf16[2048,768]{1,0:T(8,128)(2,1)S(1)} %bitcast.50, bf16[2048,768]{1,0:T(8,128)(2,1)} %get-tuple-element.74), kind=kOutput, calls=%fused_computation.12 | convolution fusion | flops 2416508928 | bytes 7471104 | tf_op jit(solution)/shard_map/dot_general | solution.py:659
  274.0 2.4 copy.68
  276.4 2.8 constant_dynamic-slice_fusion
  279.2 2.0 collective-permute-start.4
  281.2 80.1 %mixer_backward.1 = (bf16[2,1024,2304]{2,1,0:T(8,128)(2,1)}, f32[12,8,768]{2,1,0:T(8,128)}) custom-call(s32[2]{0:T(128)} %dynamic_slice.30.split_ref, s32[2]{0:T(128)} %dynamic_slice.31.keep_ref, bf16[2,1024,768]{2,1,0:T(8,128)(2,1)} %bitcast.61, bf16[2,1024,768]{2,1,0:T(8,128)(2,1)} %get-tuple-element.75.q_ref, ...), custom_call_target="tpu_custom_call" | custom-call | flops 18522046464 | bytes 31457280 | tf_op jit(solution)/shard_map/mixer_backward/pallas_call | solution.py:592
  361.3 12.1 %bitcast_convert_fusion = bf16[768,2304]{1,0:T(8,128)(2,1)S(1)} fusion(bf16[2,1024,768]{2,1,0:T(8,128)(2,1)} %get-tuple-element.81, bf16[2,1024,2304]{2,1,0:T(8,128)(2,1)} %get-tuple-element.79), kind=kOutput, calls=%fused_computation | convolution fusion | flops 7249526784 | bytes 16121856 | tf_op jit(solution)/shard_map/dot_general | solution.py:659
  373.4 2.9 pad_maximum_fusion
  376.3 3.3 reduce-scatter.6.cloned.1.call-done
  379.6 1.8 maximum_maximum_fusion
  383.0 2.0 broadcast_select_fusion.1
  385.0 1.9 pad_maximum_fusion.2
  386.9 3.0 collective-permute-done.6
  392.4 23.5 %input_back.1 = (bf16[2048,768]{1,0:T(8,128)(2,1)}, f32[8,768]{1,0:T(8,128)}) custom-call(bf16[2048,768]{1,0:T(8,128)(2,1)} %bitcast.51, f32[2048,768]{1,0:T(8,128)} %get-tuple-element.70.grad_ref, f32[1,768]{1,0:T(1,128)} %reshape.83.norm_gain_ref.gain_ref, bf16[768,2304]{1,0:T(8,128)(2,1)} %w_ref.1, bf16[2048,2304]{1,0:T(8,128)(2,1)} %bitcast.62), custom_call_target="tpu_custom_call" | custom-call | flops 7247757312 | bytes 22020096 | tf_op jit(solution)/shard_map/input_back/pallas_call | solution.py:645
  415.9 1.7 maximum_reduce_fusion.x_ref
  417.6 38.6 %exchange_sum.1 = (f32[14,768]{1,0:T(8,128)}, bf16[2,512,768]{2,1,0:T(8,128)(2,1)}) custom-call(f32[14,768]{1,0:T(8,128)} %maximum_reduce_fusion.x_ref, bf16[2,1024,768]{2,1,0:T(8,128)(2,1)} %bitcast.54), custom_call_target="tpu_custom_call" | custom-call | flops 20000000000 | tf_op jit(solution)/shard_map/exchange_sum/pallas_call | solution.py:712
  456.2 5.9 %assemble.1 = f32[4,512,768]{2,1,0:T(8,128)} custom-call(s32[1]{0:T(128)} %bitcast.10.s_ref, bf16[2,1024,768]{2,1,0:T(8,128)(2,1)} %bitcast.55, bf16[2,512,768]{2,1,0:T(8,128)(2,1)} %get-tuple-element.89.other_ref), custom_call_target="tpu_custom_call" | custom-call | tf_op jit(solution)/shard_map/assemble/pallas_call | solution.py:739
  462.1 1.7 slice_reduce_fusion
  470.7 4.7 collective-permute-done.5
  (123 shorter events, 38.8 us)
Async XLA Ops:
  7.2 259.4 %reduce-scatter.4.cloned.1.call-start = ((), (), s32[]{:S(2)}) async-start(), calls=%async_computation.3 | async-start | bytes 5013504 | tf_op jit(solution)/shard_map/reduce_scatter | solution.py:827
  8.0 27.1 %collective-permute-start = (s32[4]{0:T(128)S(1)}, s32[4]{0:T(128)S(1)}, u32[]{:S(2)}, u32[]{:S(2)}) collective-permute-start(s32[4]{0:T(128)S(1)} %reduce_sum.18), channel_id=1, source_target_pairs={{0,1},{1,0},{2,3},{3,2},{4,5},{5,4},{6,7},{7,6},{8,9},{9,8},{10,11... | collective-permute-start | bytes 56 | tf_op jit(solution)/shard_map/ppermute | solution.py:755
  13.2 22.7 %collective-permute-start.1 = (bf16[1,512,768]{2,1,0:T(8,128)(2,1)}, bf16[1,512,768]{2,1,0:T(8,128)(2,1)}, u32[]{:S(2)}, u32[]{:S(2)}) collective-permute-start(bf16[1,512,768]{2,1,0:T(8,128)(2,1)} %constant_dynamic-slice_fusion.3), channel_id=1, source_target_pairs={{0,1},{1,0},{2,3},{3,2},{4,5},{5,4},{6,7},{7,6},{8,9},{9,8},{10,11... | collective-permute-start | bytes 2359304 | tf_op jit(solution)/shard_map/ppermute | solution.py:755
  16.4 8.7 %copy-start.19 = (f32[768]{0:T(1024)S(1)}, f32[768]{0:T(1024)}, u32[]{:S(2)}) copy-start(f32[768]{0:T(1024)} %param.18) | copy-start | bytes 9220
  16.4 9.3 %copy-start.20 = (f32[768]{0:T(1024)S(1)}, f32[768]{0:T(1024)}, u32[]{:S(2)}) copy-start(f32[768]{0:T(1024)} %param.22) | copy-start | bytes 9220
  16.5 9.9 %copy-start.21 = (f32[768]{0:T(1024)S(1)}, f32[768]{0:T(1024)}, u32[]{:S(2)}) copy-start(f32[768]{0:T(1024)} %param.23) | copy-start | bytes 9220
  16.5 10.4 %copy-start.22 = (f32[768]{0:T(1024)S(1)}, f32[768]{0:T(1024)}, u32[]{:S(2)}) copy-start(f32[768]{0:T(1024)} %param.24) | copy-start | bytes 9220
  16.5 11.0 %copy-start.23 = (f32[768]{0:T(1024)S(1)}, f32[768]{0:T(1024)}, u32[]{:S(2)}) copy-start(f32[768]{0:T(1024)} %param.26) | copy-start | bytes 9220
  24.4 8.7 %copy-start.24 = (s32[4]{0:T(128)S(1)}, s32[4]{0:T(128)}, u32[]{:S(2)}) copy-start(s32[4]{0:T(128)} %param.16) | copy-start | bytes 52
  33.8 2.5 copy-start.11
  40.6 41.6 %collective-permute-start.2 = (bf16[1,512,768]{2,1,0:T(8,128)(2,1)}, bf16[1,512,768]{2,1,0:T(8,128)(2,1)}, u32[]{:S(2)}, u32[]{:S(2)}) collective-permute-start(bf16[1,512,768]{2,1,0:T(8,128)(2,1)} %constant_dynamic-slice_fusion.2), channel_id=1, source_target_pairs={{0,1},{1,0},{2,3},{3,2},{4,5},{5,4},{6,7},{7,6},{8,9},{9,8},{10,11... | collective-permute-start | bytes 2359304 | tf_op jit(solution)/shard_map/ppermute | solution.py:755
  82.3 3.1 copy-start.12
  83.9 2.7 copy-start.5
  83.9 2.7 copy-start.7
  86.6 45.1 %collective-permute-start.3 = (bf16[2,512,768]{2,1,0:T(8,128)(2,1)}, bf16[2,512,768]{2,1,0:T(8,128)(2,1)}, u32[]{:S(2)}, u32[]{:S(2)}) collective-permute-start(bf16[2,512,768]{2,1,0:T(8,128)(2,1)} %constant_dynamic-slice_fusion.1), channel_id=1, source_target_pairs={{0,1},{1,0},{2,3},{3,2},{4,5},{5,4},{6,7},{7,6},{8,9},{9,8},{10,11... | collective-permute-start | bytes 4718600 | tf_op jit(solution)/shard_map/ppermute | solution.py:755
  126.7 4.9 %copy-start.13 = (bf16[4,512,768]{2,1,0:T(8,128)(2,1)S(1)}, bf16[4,512,768]{2,1,0:T(8,128)(2,1)}, u32[]{:S(2)}) copy-start(bf16[4,512,768]{2,1,0:T(8,128)(2,1)} %param.29) | copy-start | bytes 9437188
  133.5 3.4 copy-start
  176.2 203.4 %reduce-scatter.6.cloned.1.call-start = ((), (), s32[]{:S(2)}) async-start(), calls=%async_computation.4 | async-start | bytes 10027008 | tf_op jit(solution)/shard_map/reduce_scatter | solution.py:832
  266.6 201.8 %reduce-scatter.8.cloned.1.call-start = ((), (), s32[]{:S(2)}) async-start(), calls=%async_computation.5 | async-start | bytes 5013504 | tf_op jit(solution)/shard_map/reduce_scatter | solution.py:837
  279.2 103.8 %collective-permute-start.4 = (bf16[2,512,768]{2,1,0:T(8,128)(2,1)}, bf16[2,512,768]{2,1,0:T(8,128)(2,1)}, u32[]{:S(2)}, u32[]{:S(2)}) collective-permute-start(bf16[2,512,768]{2,1,0:T(8,128)(2,1)} %constant_dynamic-slice_fusion), channel_id=1, source_target_pairs={{0,1},{1,0},{2,3},{3,2},{4,5},{5,4},{6,7},{7,6},{8,9},{9,8},{10,11... | collective-permute-start | bytes 4718600 | tf_op jit(solution)/shard_map/ppermute | solution.py:755
  361.3 12.1 %copy-start.9 = (bf16[768,768]{1,0:T(8,128)(2,1)S(1)}, bf16[768,768]{1,0:T(8,128)(2,1)}, u32[]{:S(2)}) copy-start(bf16[768,768]{1,0:T(8,128)(2,1)} %copy.68) | copy-start | bytes 3538948
  376.3 3.3 copy-start.2
  376.3 3.3 copy-start.4
  376.3 3.3 copy-start.6
  376.3 3.3 copy-start.8
  379.6 3.3 copy-start.14
  381.5 8.5 %collective-permute-start.6 = (bf16[3,48,1024]{2,1,0:T(8,128)(2,1)S(1)}, bf16[3,48,1024]{2,1,0:T(8,128)(2,1)S(1)}, u32[]{:S(2)}, u32[]{:S(2)}) collective-permute-start(bf16[3,48,1024]{2,1,0:T(8,128)(2,1)S(1)} %copy-done.18), channel_id=1, source_target_pairs={{0,1},{1,0},{2,3},{3,2},{4,5},{5,4},{6,7},{7,6},{8,9},{9,8},{10,11... | collective-permute-start | bytes 884744 | tf_op jit(solution)/shard_map/ppermute | solution.py:755
  390.9 74.9 %collective-permute-start.7 = (bf16[3,48,2048]{2,1,0:T(8,128)(2,1)}, bf16[3,48,2048]{2,1,0:T(8,128)(2,1)}, u32[]{:S(2)}, u32[]{:S(2)}) collective-permute-start(bf16[3,48,2048]{2,1,0:T(8,128)(2,1)} %reduce-scatter.6.cloned.1.call-done), channel_id=1, source_target_pairs={{0,1},{1,0},{2,3},{3,2},{4,5},{5,4},{6,7},{7,6},{8,9},{9,8},{10,11... | collective-permute-start | bytes 1769480 | tf_op jit(solution)/shard_map/ppermute | solution.py:755
  462.1 5.2 %copy-start.16 = (f32[48,1024]{1,0:T(8,128)S(1)}, f32[48,1024]{1,0:T(8,128)}, u32[]{:S(2)}) copy-start(f32[48,1024]{1,0:T(8,128)} %get-tuple-element.110) | copy-start | bytes 589828
  462.1 5.2 %copy-start.17 = (f32[48,1024]{1,0:T(8,128)S(1)}, f32[48,1024]{1,0:T(8,128)}, u32[]{:S(2)}) copy-start(f32[48,1024]{1,0:T(8,128)} %get-tuple-element.111) | copy-start | bytes 589828
  465.8 4.1 copy-start.15
  468.4 7.0 %collective-permute-start.5 = (bf16[48,3072]{1,0:T(8,128)(2,1)}, bf16[48,3072]{1,0:T(8,128)(2,1)S(1)}, u32[]{:S(2)}, u32[]{:S(2)}) collective-permute-start(bf16[48,3072]{1,0:T(8,128)(2,1)} %reduce-scatter.8.cloned.1.call-done), channel_id=1, source_target_pairs={{0,1},{1,0},{2,3},{3,2},{4,5},{5,4},{6,7},{7,6},{8,9},{9,8},{10,11... | collective-permute-start | bytes 884744 | tf_op jit(solution)/shard_map/ppermute | solution.py:755
  (4 other events, 6.9 us)
Sparse Core Ops, SparseCore 0:
  176.3 77.2 reduce-scatter.3
  266.7 112.7 reduce-scatter.5
  383.4 77.4 reduce-scatter.7

commit v6 on v5

--- a/solution.py
+++ b/solution.py
@@ -56,8 +56,8 @@
     )
 
 
-def loop(count, body):
-    lax.fori_loop(0, count, lambda i, c: (body(i), c)[1], 0)
+def loop(count, body, unroll=1):
+    lax.fori_loop(0, count, lambda i, c: (body(i), c)[1], 0, unroll=unroll)
 
 
 def rows_of(i, size):
@@ -106,7 +106,7 @@
     blockwise(u_ref, out_ref, inv_real_ref, inv_ref, quarter)
 
 
-def each_bin(quarter, body, tile=16):
+def each_bin(quarter, body, tile=64):
     half = quarter // 2
     body(0, half, True)
 
@@ -160,7 +160,7 @@
     length, width = q_ref.shape
     quarter = length // 4
     split, keep = split_ref[r], keep_ref[r]
-    tile = 64
+    tile = 128
 
     @pl.when(j == 0)
     def _():
@@ -171,7 +171,7 @@
             first_ref[rows, :] = (n * norm_gain_ref[...]).astype(BF)
             resid_ref[rows, :] = v
 
-        loop(length // tile, body)
+        loop(length // tile, body, 2)
         for ref in (qs, ks, vs):
             ref[0:8, :] = jnp.zeros((8, width), F32)
 
@@ -194,7 +194,7 @@
     blockwise(y_s, spec_s, fwd_real_ref, fwd_ref, quarter)
 
     def bins(re, im, first):
-        n = 16
+        n = 64
         re, im = pl.ds(pl.multiple_of(re, n), n), pl.ds(pl.multiple_of(im, n), n)
         vr, vi = spec_s[re, 0:width], spec_s[im, 0:width]
         cr, ci = spec_s[re, width : 2 * width], spec_s[im, width : 2 * width]
@@ -235,7 +235,7 @@
             n, _ = norm_stats(resid_ref[rows, :])
             second_ref[rows, :] = (n * ffn_gain_ref[...]).astype(BF)
 
-        loop(length // tile, body)
+        loop(length // tile, body, 2)
 
 
 def once(shape, index):
@@ -300,7 +300,7 @@
 
 
 def ffn_kernel(
-    sa_ref, og_ref, sat_ref, ogt_ref, wg_ref, wu_ref, wo_ref, out_ref, back_ref, grads_ref, *scratch
+    sa_ref, og_ref, sat_ref, ogt_ref, wg_ref, wu_ref, wo_ref, out_low_ref, back_low_ref, grads_ref, out_ref, back_ref, *scratch
 ):
     j = pl.program_id(0)
     tokens, model = sa_ref.shape
@@ -368,6 +368,15 @@
     for k, (ref, first, second) in enumerate(((sat_ref, gg0, gg1), (sat_ref, ug0, ug1), (ogt_ref, hid0, hid1))):
         grads_ref[k] = (mm(ref[:, 0:half], first[...]) + mm(ref[:, half:tokens], second[...])).astype(BF)
 
+    @pl.when(j == pl.num_programs(0) - 1)
+    def _():
+        def leave(i):
+            rows = rows_of(i, 64)
+            out_low_ref[rows, :] = out_ref[rows, :].astype(BF)
+            back_low_ref[rows, :] = back_ref[rows, :].astype(BF)
+
+        loop(tokens // 64, leave)
+
 
 def ffn_both(second_act, out_grad, second_turned, grad_turned, ffn_in, ffn_out, share, width=512, tile=512):
     tokens, model = second_act.shape
@@ -380,7 +389,7 @@
     turned = once((model, tokens), lambda j: (0, 0))
     return pl.pallas_call(
         ffn_kernel,
-        out_shape=[shape((tokens, model), F32), shape((tokens, model), F32), shape((3, model, hidden), BF)],
+        out_shape=[shape((tokens, model), BF), shape((tokens, model), BF), shape((3, model, hidden), BF)],
         grid=(blocks,),
         in_specs=[
             whole, whole, turned, turned,
@@ -389,7 +398,7 @@
             pl.BlockSpec((width, model), lambda j: (j + first, 0)),
         ],
         out_specs=[whole, whole, pl.BlockSpec((3, model, width), lambda j: (0, 0, j))],
-        scratch_shapes=([pltpu.VMEM((tile, width), F32)] * 3 + [pltpu.VMEM((tokens // 2, width), BF)] * 3) * 2,
+        scratch_shapes=[pltpu.VMEM((tokens, model), F32)] * 2 + ([pltpu.VMEM((tile, width), F32)] * 3 + [pltpu.VMEM((tokens // 2, width), BF)] * 3) * 2,
         compiler_params=pltpu.CompilerParams(dimension_semantics=("arbitrary",), vmem_limit_bytes=LIMIT),
         cost_estimate=pl.CostEstimate(flops=18 * tokens * model * hidden, bytes_accessed=tokens * model * 24 + model * hidden * 12, transcendentals=tokens * hidden),
         name="ffn_both",
@@ -410,12 +419,12 @@
         rows = rows_of(i, tile)
         resid = resid_ref[rows, :]
         n, scale = norm_stats(resid)
-        u = sum(ref[rows, :] for ref in back_refs)
+        u = sum(ref[rows, :].astype(F32) for ref in back_refs)
         ug = u * gain_ref[...]
         un = u * n
         part = ug - jnp.mean(ug, axis=-1, keepdims=True) - n * jnp.mean(ug * n, axis=-1, keepdims=True)
         grad = og_ref[rows, :].astype(F32) + scale * part
-        out_ref[rows, :] = (resid + sum(ref[rows, :] for ref in sum_refs)).astype(BF)
+        out_ref[rows, :] = (resid + sum(ref[rows, :].astype(F32) for ref in sum_refs)).astype(BF)
         grad_ref[rows, :] = grad
         low_ref[rows, :] = grad.astype(BF)
         gain_grad_ref[...] += jnp.sum(un.reshape(tile // 8, 8, un.shape[1]), axis=0)
@@ -455,7 +464,7 @@
     length, width = q_ref.shape
     quarter = length // 4
     split, keep = split_ref[r], keep_ref[r]
-    tile = 64
+    tile = 128
 
     @pl.when(r == 0)
     def _():
@@ -496,7 +505,7 @@
     blockwise(y_s, spec_s, fwd_real_ref, fwd_ref, quarter)
 
     def bins(re, im, first):
-        n = 16
+        n = 64
         re, im = pl.ds(pl.multiple_of(re, n), n), pl.ds(pl.multiple_of(im, n), n)
         vr, vi = spec_s[re, 0:width], spec_s[im, 0:width]
         cr, ci = spec_s[re, width : 2 * width], spec_s[im, width : 2 * width]

time: 490 us -> 481 us (0.982)
  Pallas kernels: 357 us -> 344 us
    pallas_call x2, Pallas kernels: 79.7 us -> 67.2 us  [mixer_forward(): pl.pallas_call(functools.partial(mixer_forward_kernel, first_row, len(ear...]
    pallas_call x2, Pallas kernels: 111 us -> 116 us  [ffn_both(): pl.pallas_call(ffn_kernel, out_shape=[shape((tokens, model), BF), shape((...]
  transfers between devices with their start and end apart: 11 -> 11, of which waited for: 3 -> 3; matrix products, arithmetic and copies ran while one was open for 15% -> 15% of each run, Pallas kernels for 66% -> 63%
where the time goes in v6:
time: 481 us; the launch traced here: 476 us
  Pallas kernels  344 us (72%)
  other arithmetic  39.3 us (8%)
  local copies, waits for them, and re-layouts  34 us (7%)
  matrix products  17.6 us (4%)
  waiting for transfers between devices  15.3 us (3%)
  between operations  14.5 us (3%)
  starting transfers between devices  11.6 us (2%)
    pallas_call x2, Pallas kernels, ffn_both(): pl.pallas_call(ffn_kernel, out_shape=[shape((tokens, model), BF), shape((...  116 us
    pallas_call x1, Pallas kernels, mixer_backward(): pl.pallas_call(mixer_backward_kernel, out_shape=[shape((rows, length, 3 *...  75.9 us
    pallas_call x2, Pallas kernels, mixer_forward(): pl.pallas_call(functools.partial(mixer_forward_kernel, first_row, len(ear...  67.2 us
    pallas_call x1, Pallas kernels, exchange_sum(): pl.pallas_call(functools.partial(exchange_sum_kernel, rows, seq), out_sha...  38.6 us
    pallas_call x1, Pallas kernels, input_back(): pl.pallas_call(functools.partial(input_back_kernel, width), out_shape=[sh...  23.5 us
    dot_general x2, matrix products, turn(): lax.dot_general(a, b, (((0,), (0,)), ((), ())), preferred_element_type=F32)  17.6 us
    pallas_call x1, Pallas kernels, norm_back(): pl.pallas_call(functools.partial(norm_back_kernel, pieces), out_shape=[sh...  16.8 us
    ppermute x8, starting transfers between devices, swapped(): lax.ppermute(value, 'seq', [(i, (i + 1) % count) for i in range(count)])  11.5 us
  transfers between devices with their start and end apart: 11, of which 3 were waited for; matrix products, arithmetic and copies ran while one was open for 15% of the time, Pallas kernels for 63%

profile of v6, /device:TPU:0, one launch (start us, length us, event | category | flops | bytes accessed | tf_op | source)
XLA Modules:
  0.0 476.5 jit_solution(9468161932055425844)
XLA Ops:
  8.0 3.1 collective-permute-start
  11.1 2.1 constant_dynamic-slice_fusion.3
  14.3 2.1 fusion.51
  19.4 4.9 %multiply_convert_fusion.1 = (bf16[256,256]{0,1:T(8,128)(2,1)S(1)}, bf16[256,256]{0,1:T(8,128)(2,1)S(1)}, bf16[256,256]{0,1:T(8,128)(2,1)S(1)}, bf16[256,256]{0,1:T(8,128)(2,1)S(1)}) fusion(f32[256]{0:T(256)S(1)} %fusion.54, s32[256]{0:T(256)S(1)} %iota_and_fusion, s32[256]{0:T(256)S(1)} %fusion.58, s32[]{:T(128)S(6)} %mul.128, ...), kind=kLoop, calls=%fused_computation.108 | loop fusion | flops 5505024 | bytes 528388 | tf_op jit(solution)/shard_map/convert.6
  30.5 2.7 copy.57.fwd_ref
  40.7 2.0 collective-permute-start.2
  42.7 33.5 %mixer_forward.2 = (bf16[2,1024,768]{2,1,0:T(8,128)(2,1)}, bf16[2,1024,768]{2,1,0:T(8,128)(2,1)}, bf16[2,1024,768]{2,1,0:T(8,128)(2,1)}, bf16[2,1024,768]{2,1,0:...) custom-call(s32[2]{0:T(128)} %dynamic_slice.30.split_ref, ...), custom_call_target="tpu_custom_call" | custom-call | flops 9663676416 | bytes 15728640 | tf_op jit(solution)/shard_map/mixer_forward/pallas_call | solution.py:270
  80.5 33.7 %mixer_forward.3 = (bf16[2,1024,768]{2,1,0:T(8,128)(2,1)}, bf16[2,1024,768]{2,1,0:T(8,128)(2,1)}, bf16[2,1024,768]{2,1,0:T(8,128)(2,1)}, bf16[2,1024,768]{2,1,0:...) custom-call(s32[2]{0:T(128)} %dynamic_slice.30.split_ref, ...), custom_call_target="tpu_custom_call", output_to_operand_aliasing={{0}: (19, {}), {1}: (20, {}), {2}: (21, {}), {3}: (22, {}),... | custom-call | flops 9663676416 | bytes 15728640 | tf_op jit(solution)/shard_map/mixer_forward/pallas_call | solution.py:270
  114.2 4.9 %copy.71 = bf16[2048,768]{0,1:T(8,128)(2,1)} copy(bf16[2048,768]{1,0:T(8,128)(2,1)} %bitcast.47) | data formatting | bytes 6291456 | tf_op jit(solution)/shard_map/reshape | solution.py:803
  121.0 3.4 copy.61.ogt_ref
  124.3 42.4 %ffn_both.2 = (bf16[2048,768]{1,0:T(8,128)(2,1)}, bf16[2048,768]{1,0:T(8,128)(2,1)}, bf16[3,768,1024]{2,1,0:T(8,128)(2,1)}) custom-call(bf16[2048,768]{1,0:T(8,128)(2,1)} %bitcast.48, bf16[2048,768]{1,0:T(8,128)(2,1)} %bitcast.43, bf16[768,2048]{1,0:T(8,128)(2,1)} %bitcast.52, bf16[768,2048]{1,0:T(8,128)(2,1)} %copy.61.ogt_ref, bf16[768,6144]{1,0:T(8,128)(2,1)} %wu_ref.3, ...), custom_call_target="tpu_custom_call" | custom-call | flops 28991029248 | bytes 47185920 | tf_op jit(solution)/shard_map/ffn_both/pallas_call | solution.py:390
  166.8 73.9 %ffn_both.3 = (bf16[2048,768]{1,0:T(8,128)(2,1)}, bf16[2048,768]{1,0:T(8,128)(2,1)}, bf16[3,768,2048]{2,1,0:T(8,128)(2,1)}) custom-call(bf16[2048,768]{1,0:T(8,128)(2,1)} %bitcast.49, bf16[2048,768]{1,0:T(8,128)(2,1)} %bitcast.44, bf16[768,2048]{1,0:T(8,128)(2,1)} %bitcast.53, bf16[768,2048]{1,0:T(8,128)(2,1)} %copy.61.ogt_ref, bf16[768,6144]{1,0:T(8,128)(2,1)} %wu_ref.3, ...), custom_call_target="tpu_custom_call" | custom-call | flops 57982058496 | bytes 56623104 | tf_op jit(solution)/shard_map/ffn_both/pallas_call | solution.py:390
  240.8 16.8 %norm_back.1 = (bf16[2048,768]{1,0:T(8,128)(2,1)}, f32[2048,768]{1,0:T(8,128)}, bf16[2048,768]{1,0:T(8,128)(2,1)}, f32[8,768]{1,0:T(8,128)}) custom-call(f32[2048,768]{1,0:T(8,128)} %bitcast.46, bf16[2048,768]{1,0:T(8,128)(2,1)} %get-tuple-element.65.refs_0_, bf16[2048,768]{1,0:T(8,128)(2,1)} %get-tuple-element.66.refs_1_, ...), custom_call_target="tpu_custom_call" | custom-call | flops 31457280 | bytes 34603008 | tf_op jit(solution)/shard_map/norm_back/pallas_call | solution.py:441
  257.7 1.8 copy-done.10
  259.5 5.6 %convolution_convert_fusion = bf16[768,768]{0,1:T(8,128)(2,1)} fusion(bf16[2048,768]{1,0:T(8,128)(2,1)S(1)} %bitcast.50, bf16[2048,768]{1,0:T(8,128)(2,1)} %get-tuple-element.74), kind=kOutput, calls=%fused_computation.12 | convolution fusion | flops 2416508928 | bytes 7471104 | tf_op jit(solution)/shard_map/dot_general | solution.py:668
  265.0 2.4 copy.68
  267.4 2.8 constant_dynamic-slice_fusion
  270.2 2.0 collective-permute-start.4
  272.2 75.9 %mixer_backward.1 = (bf16[2,1024,2304]{2,1,0:T(8,128)(2,1)}, f32[12,8,768]{2,1,0:T(8,128)}) custom-call(s32[2]{0:T(128)} %dynamic_slice.30.split_ref, s32[2]{0:T(128)} %dynamic_slice.31.keep_ref, bf16[2,1024,768]{2,1,0:T(8,128)(2,1)} %bitcast.61, bf16[2,1024,768]{2,1,0:T(8,128)(2,1)} %get-tuple-element.75.q_ref, ...), custom_call_target="tpu_custom_call" | custom-call | flops 18522046464 | bytes 31457280 | tf_op jit(solution)/shard_map/mixer_backward/pallas_call | solution.py:601
  348.1 12.1 %bitcast_convert_fusion = bf16[768,2304]{1,0:T(8,128)(2,1)S(1)} fusion(bf16[2,1024,768]{2,1,0:T(8,128)(2,1)} %get-tuple-element.81, bf16[2,1024,2304]{2,1,0:T(8,128)(2,1)} %get-tuple-element.79), kind=kOutput, calls=%fused_computation | convolution fusion | flops 7249526784 | bytes 16121856 | tf_op jit(solution)/shard_map/dot_general | solution.py:668
  360.2 2.9 pad_maximum_fusion
  363.1 7.5 %reduce-scatter.6.cloned.1.call-done = bf16[3,48,2048]{2,1,0:T(8,128)(2,1)} async-done(((bf16[3,768,2048]{2,1,0:T(8,128)(2,1)}), bf16[3,48,2048]{2,1,0:T(8,128)(2,1)}) %reduce-scatter.6.cloned.1.call-update) | async-done | bytes 589840 | tf_op jit(solution)/shard_map/reduce_scatter | solution.py:841
  370.6 1.8 maximum_maximum_fusion
  374.0 2.0 broadcast_select_fusion.1
  376.0 1.9 pad_maximum_fusion.2
  377.9 3.0 collective-permute-done.6
  383.3 23.5 %input_back.1 = (bf16[2048,768]{1,0:T(8,128)(2,1)}, f32[8,768]{1,0:T(8,128)}) custom-call(bf16[2048,768]{1,0:T(8,128)(2,1)} %bitcast.51, f32[2048,768]{1,0:T(8,128)} %get-tuple-element.70.grad_ref, f32[1,768]{1,0:T(1,128)} %reshape.83.norm_gain_ref.gain_ref, bf16[768,2304]{1,0:T(8,128)(2,1)} %w_ref.1, bf16[2048,2304]{1,0:T(8,128)(2,1)} %bitcast.62), custom_call_target="tpu_custom_call" | custom-call | flops 7247757312 | bytes 22020096 | tf_op jit(solution)/shard_map/input_back/pallas_call | solution.py:654
  406.8 1.7 maximum_reduce_fusion.x_ref
  408.5 38.6 %exchange_sum.1 = (f32[14,768]{1,0:T(8,128)}, bf16[2,512,768]{2,1,0:T(8,128)(2,1)}) custom-call(f32[14,768]{1,0:T(8,128)} %maximum_reduce_fusion.x_ref, bf16[2,1024,768]{2,1,0:T(8,128)(2,1)} %bitcast.54), custom_call_target="tpu_custom_call" | custom-call | flops 20000000000 | tf_op jit(solution)/shard_map/exchange_sum/pallas_call | solution.py:721
  447.1 5.9 %assemble.1 = f32[4,512,768]{2,1,0:T(8,128)} custom-call(s32[1]{0:T(128)} %bitcast.10.s_ref, bf16[2,1024,768]{2,1,0:T(8,128)(2,1)} %bitcast.55, bf16[2,512,768]{2,1,0:T(8,128)(2,1)} %get-tuple-element.89.other_ref), custom_call_target="tpu_custom_call" | custom-call | tf_op jit(solution)/shard_map/assemble/pallas_call | solution.py:748
  453.1 1.7 slice_reduce_fusion
  461.8 4.7 collective-permute-done.5
  (123 shorter events, 38.7 us)
Async XLA Ops:
  7.2 250.4 %reduce-scatter.4.cloned.1.call-start = ((), (), s32[]{:S(2)}) async-start(), calls=%async_computation.3 | async-start | bytes 5013504 | tf_op jit(solution)/shard_map/reduce_scatter | solution.py:836
  8.0 27.2 %collective-permute-start = (s32[4]{0:T(128)S(1)}, s32[4]{0:T(128)S(1)}, u32[]{:S(2)}, u32[]{:S(2)}) collective-permute-start(s32[4]{0:T(128)S(1)} %reduce_sum.18), channel_id=1, source_target_pairs={{0,1},{1,0},{2,3},{3,2},{4,5},{5,4},{6,7},{7,6},{8,9},{9,8},{10,11... | collective-permute-start | bytes 56 | tf_op jit(solution)/shard_map/ppermute | solution.py:764
  13.2 22.7 %collective-permute-start.1 = (bf16[1,512,768]{2,1,0:T(8,128)(2,1)}, bf16[1,512,768]{2,1,0:T(8,128)(2,1)}, u32[]{:S(2)}, u32[]{:S(2)}) collective-permute-start(bf16[1,512,768]{2,1,0:T(8,128)(2,1)} %constant_dynamic-slice_fusion.3), channel_id=1, source_target_pairs={{0,1},{1,0},{2,3},{3,2},{4,5},{5,4},{6,7},{7,6},{8,9},{9,8},{10,11... | collective-permute-start | bytes 2359304 | tf_op jit(solution)/shard_map/ppermute | solution.py:764
  16.4 8.7 %copy-start.19 = (f32[768]{0:T(1024)S(1)}, f32[768]{0:T(1024)}, u32[]{:S(2)}) copy-start(f32[768]{0:T(1024)} %param.18) | copy-start | bytes 9220
  16.4 9.3 %copy-start.20 = (f32[768]{0:T(1024)S(1)}, f32[768]{0:T(1024)}, u32[]{:S(2)}) copy-start(f32[768]{0:T(1024)} %param.22) | copy-start | bytes 9220
  16.5 9.9 %copy-start.21 = (f32[768]{0:T(1024)S(1)}, f32[768]{0:T(1024)}, u32[]{:S(2)}) copy-start(f32[768]{0:T(1024)} %param.23) | copy-start | bytes 9220
  16.5 10.4 %copy-start.22 = (f32[768]{0:T(1024)S(1)}, f32[768]{0:T(1024)}, u32[]{:S(2)}) copy-start(f32[768]{0:T(1024)} %param.24) | copy-start | bytes 9220
  16.5 11.0 %copy-start.23 = (f32[768]{0:T(1024)S(1)}, f32[768]{0:T(1024)}, u32[]{:S(2)}) copy-start(f32[768]{0:T(1024)} %param.26) | copy-start | bytes 9220
  24.4 8.8 %copy-start.24 = (s32[4]{0:T(128)S(1)}, s32[4]{0:T(128)}, u32[]{:S(2)}) copy-start(s32[4]{0:T(128)} %param.16) | copy-start | bytes 52
  33.8 2.5 copy-start.11
  40.7 35.5 %collective-permute-start.2 = (bf16[1,512,768]{2,1,0:T(8,128)(2,1)}, bf16[1,512,768]{2,1,0:T(8,128)(2,1)}, u32[]{:S(2)}, u32[]{:S(2)}) collective-permute-start(bf16[1,512,768]{2,1,0:T(8,128)(2,1)} %constant_dynamic-slice_fusion.2), channel_id=1, source_target_pairs={{0,1},{1,0},{2,3},{3,2},{4,5},{5,4},{6,7},{7,6},{8,9},{9,8},{10,11... | collective-permute-start | bytes 2359304 | tf_op jit(solution)/shard_map/ppermute | solution.py:764
  76.2 3.1 copy-start.12
  77.8 2.7 copy-start.5
  77.8 2.7 copy-start.7
  80.5 38.6 %collective-permute-start.3 = (bf16[2,512,768]{2,1,0:T(8,128)(2,1)}, bf16[2,512,768]{2,1,0:T(8,128)(2,1)}, u32[]{:S(2)}, u32[]{:S(2)}) collective-permute-start(bf16[2,512,768]{2,1,0:T(8,128)(2,1)} %constant_dynamic-slice_fusion.1), channel_id=1, source_target_pairs={{0,1},{1,0},{2,3},{3,2},{4,5},{5,4},{6,7},{7,6},{8,9},{9,8},{10,11... | collective-permute-start | bytes 4718600 | tf_op jit(solution)/shard_map/ppermute | solution.py:764
  114.2 4.9 %copy-start.13 = (bf16[4,512,768]{2,1,0:T(8,128)(2,1)S(1)}, bf16[4,512,768]{2,1,0:T(8,128)(2,1)}, u32[]{:S(2)}) copy-start(bf16[4,512,768]{2,1,0:T(8,128)(2,1)} %param.29) | copy-start | bytes 9437188
  121.0 3.4 copy-start
  166.8 203.8 %reduce-scatter.6.cloned.1.call-start = ((), (), s32[]{:S(2)}) async-start(), calls=%async_computation.4 | async-start | bytes 10027008 | tf_op jit(solution)/shard_map/reduce_scatter | solution.py:841
  257.6 201.8 %reduce-scatter.8.cloned.1.call-start = ((), (), s32[]{:S(2)}) async-start(), calls=%async_computation.5 | async-start | bytes 5013504 | tf_op jit(solution)/shard_map/reduce_scatter | solution.py:846
  270.2 103.7 %collective-permute-start.4 = (bf16[2,512,768]{2,1,0:T(8,128)(2,1)}, bf16[2,512,768]{2,1,0:T(8,128)(2,1)}, u32[]{:S(2)}, u32[]{:S(2)}) collective-permute-start(bf16[2,512,768]{2,1,0:T(8,128)(2,1)} %constant_dynamic-slice_fusion), channel_id=1, source_target_pairs={{0,1},{1,0},{2,3},{3,2},{4,5},{5,4},{6,7},{7,6},{8,9},{9,8},{10,11... | collective-permute-start | bytes 4718600 | tf_op jit(solution)/shard_map/ppermute | solution.py:764
  348.1 12.1 %copy-start.9 = (bf16[768,768]{1,0:T(8,128)(2,1)S(1)}, bf16[768,768]{1,0:T(8,128)(2,1)}, u32[]{:S(2)}) copy-start(bf16[768,768]{1,0:T(8,128)(2,1)} %copy.68) | copy-start | bytes 3538948
  363.1 7.5 %copy-start.2 = (bf16[1,512,768]{2,1,0:T(8,128)(2,1)S(1)}, bf16[1,512,768]{2,1,0:T(8,128)(2,1)}, u32[]{:S(2)}) copy-start(bf16[1,512,768]{2,1,0:T(8,128)(2,1)} %copy-done.1) | copy-start | bytes 2359300
  363.1 7.5 %copy-start.4 = (bf16[1,512,768]{2,1,0:T(8,128)(2,1)S(1)}, bf16[1,512,768]{2,1,0:T(8,128)(2,1)}, u32[]{:S(2)}) copy-start(bf16[1,512,768]{2,1,0:T(8,128)(2,1)} %copy-done.3) | copy-start | bytes 2359300
  363.1 7.5 %copy-start.6 = (bf16[1,512,768]{2,1,0:T(8,128)(2,1)S(1)}, bf16[1,512,768]{2,1,0:T(8,128)(2,1)}, u32[]{:S(2)}) copy-start(bf16[1,512,768]{2,1,0:T(8,128)(2,1)} %copy-done.5) | copy-start | bytes 2359300
  363.1 7.5 %copy-start.8 = (bf16[1,512,768]{2,1,0:T(8,128)(2,1)S(1)}, bf16[1,512,768]{2,1,0:T(8,128)(2,1)}, u32[]{:S(2)}) copy-start(bf16[1,512,768]{2,1,0:T(8,128)(2,1)} %copy-done.7) | copy-start | bytes 2359300
  370.6 3.3 copy-start.14
  372.5 8.5 %collective-permute-start.6 = (bf16[3,48,1024]{2,1,0:T(8,128)(2,1)S(1)}, bf16[3,48,1024]{2,1,0:T(8,128)(2,1)S(1)}, u32[]{:S(2)}, u32[]{:S(2)}) collective-permute-start(bf16[3,48,1024]{2,1,0:T(8,128)(2,1)S(1)} %copy-done.18), channel_id=1, source_target_pairs={{0,1},{1,0},{2,3},{3,2},{4,5},{5,4},{6,7},{7,6},{8,9},{9,8},{10,11... | collective-permute-start | bytes 884744 | tf_op jit(solution)/shard_map/ppermute | solution.py:764
  381.8 75.0 %collective-permute-start.7 = (bf16[3,48,2048]{2,1,0:T(8,128)(2,1)}, bf16[3,48,2048]{2,1,0:T(8,128)(2,1)}, u32[]{:S(2)}, u32[]{:S(2)}) collective-permute-start(bf16[3,48,2048]{2,1,0:T(8,128)(2,1)} %reduce-scatter.6.cloned.1.call-done), channel_id=1, source_target_pairs={{0,1},{1,0},{2,3},{3,2},{4,5},{5,4},{6,7},{7,6},{8,9},{9,8},{10,11... | collective-permute-start | bytes 1769480 | tf_op jit(solution)/shard_map/ppermute | solution.py:764
  453.1 5.3 %copy-start.16 = (f32[48,1024]{1,0:T(8,128)S(1)}, f32[48,1024]{1,0:T(8,128)}, u32[]{:S(2)}) copy-start(f32[48,1024]{1,0:T(8,128)} %get-tuple-element.110) | copy-start | bytes 589828
  453.1 5.3 %copy-start.17 = (f32[48,1024]{1,0:T(8,128)S(1)}, f32[48,1024]{1,0:T(8,128)}, u32[]{:S(2)}) copy-start(f32[48,1024]{1,0:T(8,128)} %get-tuple-element.111) | copy-start | bytes 589828
  456.8 4.1 copy-start.15
  459.5 7.0 %collective-permute-start.5 = (bf16[48,3072]{1,0:T(8,128)(2,1)}, bf16[48,3072]{1,0:T(8,128)(2,1)S(1)}, u32[]{:S(2)}, u32[]{:S(2)}) collective-permute-start(bf16[48,3072]{1,0:T(8,128)(2,1)} %reduce-scatter.8.cloned.1.call-done), channel_id=1, source_target_pairs={{0,1},{1,0},{2,3},{3,2},{4,5},{5,4},{6,7},{7,6},{8,9},{9,8},{10,11... | collective-permute-start | bytes 884744 | tf_op jit(solution)/shard_map/ppermute | solution.py:764
  (4 other events, 6.9 us)
Sparse Core Ops, SparseCore 0:
  166.9 77.2 reduce-scatter.3
  257.7 112.7 reduce-scatter.5
  374.4 77.3 reduce-scatter.7

commit v7 on v6

--- a/solution.py
+++ b/solution.py
@@ -300,7 +300,7 @@
 
 
 def ffn_kernel(
-    sa_ref, og_ref, sat_ref, ogt_ref, wg_ref, wu_ref, wo_ref, out_low_ref, back_low_ref, grads_ref, out_ref, back_ref, *scratch
+    sa_ref, og_ref, sat_ref, ogt_ref, wg_ref, wu_ref, wo_ref, out_ref, back_ref, grads_ref, *scratch
 ):
     j = pl.program_id(0)
     tokens, model = sa_ref.shape
@@ -368,15 +368,6 @@
     for k, (ref, first, second) in enumerate(((sat_ref, gg0, gg1), (sat_ref, ug0, ug1), (ogt_ref, hid0, hid1))):
         grads_ref[k] = (mm(ref[:, 0:half], first[...]) + mm(ref[:, half:tokens], second[...])).astype(BF)
 
-    @pl.when(j == pl.num_programs(0) - 1)
-    def _():
-        def leave(i):
-            rows = rows_of(i, 64)
-            out_low_ref[rows, :] = out_ref[rows, :].astype(BF)
-            back_low_ref[rows, :] = back_ref[rows, :].astype(BF)
-
-        loop(tokens // 64, leave)
-
 
 def ffn_both(second_act, out_grad, second_turned, grad_turned, ffn_in, ffn_out, share, width=512, tile=512):
     tokens, model = second_act.shape
@@ -389,7 +380,7 @@
     turned = once((model, tokens), lambda j: (0, 0))
     return pl.pallas_call(
         ffn_kernel,
-        out_shape=[shape((tokens, model), BF), shape((tokens, model), BF), shape((3, model, hidden), BF)],
+        out_shape=[shape((tokens, model), F32), shape((tokens, model), F32), shape((3, model, hidden), BF)],
         grid=(blocks,),
         in_specs=[
             whole, whole, turned, turned,
@@ -398,7 +389,7 @@
             pl.BlockSpec((width, model), lambda j: (j + first, 0)),
         ],
         out_specs=[whole, whole, pl.BlockSpec((3, model, width), lambda j: (0, 0, j))],
-        scratch_shapes=[pltpu.VMEM((tokens, model), F32)] * 2 + ([pltpu.VMEM((tile, width), F32)] * 3 + [pltpu.VMEM((tokens // 2, width), BF)] * 3) * 2,
+        scratch_shapes=([pltpu.VMEM((tile, width), F32)] * 3 + [pltpu.VMEM((tokens // 2, width), BF)] * 3) * 2,
         compiler_params=pltpu.CompilerParams(dimension_semantics=("arbitrary",), vmem_limit_bytes=LIMIT),
         cost_estimate=pl.CostEstimate(flops=18 * tokens * model * hidden, bytes_accessed=tokens * model * 24 + model * hidden * 12, transcendentals=tokens * hidden),
         name="ffn_both",
@@ -419,12 +410,12 @@
         rows = rows_of(i, tile)
         resid = resid_ref[rows, :]
         n, scale = norm_stats(resid)
-        u = sum(ref[rows, :].astype(F32) for ref in back_refs)
+        u = sum(ref[rows, :] for ref in back_refs)
         ug = u * gain_ref[...]
         un = u * n
         part = ug - jnp.mean(ug, axis=-1, keepdims=True) - n * jnp.mean(ug * n, axis=-1, keepdims=True)
         grad = og_ref[rows, :].astype(F32) + scale * part
-        out_ref[rows, :] = (resid + sum(ref[rows, :].astype(F32) for ref in sum_refs)).astype(BF)
+        out_ref[rows, :] = (resid + sum(ref[rows, :] for ref in sum_refs)).astype(BF)
         grad_ref[rows, :] = grad
         low_ref[rows, :] = grad.astype(BF)
         gain_grad_ref[...] += jnp.sum(un.reshape(tile // 8, 8, un.shape[1]), axis=0)
@@ -644,7 +635,7 @@
         in_grad_ref[rows, :] = (grad_ref[rows, :] + scale * part).astype(in_grad_ref.dtype)
         gain_grad_ref[...] += eight_sum(u * n)
 
-    loop(x_ref.shape[0] // tile, body)
+    loop(x_ref.shape[0] // tile, body, 2)
 
 
 def input_back(x, resid_grad, gain, proj_in, proj_grad, width, tile=512):

time: 481 us -> 473 us (0.983)
  Pallas kernels: 344 us -> 337 us
    pallas_call x2, Pallas kernels: 116 us -> 111 us  [ffn_both(): pl.pallas_call(ffn_kernel, out_shape=[shape((tokens, model), F32), shape(...]
where the time goes in v7:
time: 473 us; the launch traced here: 469 us
  Pallas kernels  337 us (71%)
  other arithmetic  39.3 us (8%)
  local copies, waits for them, and re-layouts  33.9 us (7%)
  matrix products  17.6 us (4%)
  waiting for transfers between devices  15.5 us (3%)
  between operations  14.5 us (3%)
  starting transfers between devices  11.5 us (2%)
    pallas_call x2, Pallas kernels, ffn_both(): pl.pallas_call(ffn_kernel, out_shape=[shape((tokens, model), F32), shape(...  111 us
    pallas_call x1, Pallas kernels, mixer_backward(): pl.pallas_call(mixer_backward_kernel, out_shape=[shape((rows, length, 3 *...  75.8 us
    pallas_call x2, Pallas kernels, mixer_forward(): pl.pallas_call(functools.partial(mixer_forward_kernel, first_row, len(ear...  67.2 us
    pallas_call x1, Pallas kernels, exchange_sum(): pl.pallas_call(functools.partial(exchange_sum_kernel, rows, seq), out_sha...  38.6 us
    pallas_call x1, Pallas kernels, input_back(): pl.pallas_call(functools.partial(input_back_kernel, width), out_shape=[sh...  19.4 us
    pallas_call x1, Pallas kernels, norm_back(): pl.pallas_call(functools.partial(norm_back_kernel, pieces), out_shape=[sh...  19.1 us
    dot_general x2, matrix products, turn(): lax.dot_general(a, b, (((0,), (0,)), ((), ())), preferred_element_type=F32)  17.6 us
    ppermute x8, starting transfers between devices, swapped(): lax.ppermute(value, 'seq', [(i, (i + 1) % count) for i in range(count)])  11.4 us
  transfers between devices with their start and end apart: 11, of which 3 were waited for; matrix products, arithmetic and copies ran while one was open for 15% of the time, Pallas kernels for 63%

profile of v7, /device:TPU:0, one launch (start us, length us, event | category | flops | bytes accessed | tf_op | source)
XLA Modules:
  0.0 469.2 jit_solution(7251692645199985553)
XLA Ops:
  8.0 3.1 collective-permute-start
  11.1 2.1 constant_dynamic-slice_fusion.3
  14.3 2.1 fusion.51
  19.4 4.9 %multiply_convert_fusion.1 = (bf16[256,256]{0,1:T(8,128)(2,1)S(1)}, bf16[256,256]{0,1:T(8,128)(2,1)S(1)}, bf16[256,256]{0,1:T(8,128)(2,1)S(1)}, bf16[256,256]{0,1:T(8,128)(2,1)S(1)}) fusion(f32[256]{0:T(256)S(1)} %fusion.54, s32[256]{0:T(256)S(1)} %iota_and_fusion, s32[256]{0:T(256)S(1)} %fusion.58, s32[]{:T(128)S(6)} %mul.128, ...), kind=kLoop, calls=%fused_computation.108 | loop fusion | flops 5505024 | bytes 528388 | tf_op jit(solution)/shard_map/convert.6
  30.5 2.6 copy.57.fwd_ref
  40.6 2.0 collective-permute-start.2
  42.6 33.4 %mixer_forward.2 = (bf16[2,1024,768]{2,1,0:T(8,128)(2,1)}, bf16[2,1024,768]{2,1,0:T(8,128)(2,1)}, bf16[2,1024,768]{2,1,0:T(8,128)(2,1)}, bf16[2,1024,768]{2,1,0:...) custom-call(s32[2]{0:T(128)} %dynamic_slice.30.split_ref, ...), custom_call_target="tpu_custom_call" | custom-call | flops 9663676416 | bytes 15728640 | tf_op jit(solution)/shard_map/mixer_forward/pallas_call | solution.py:270
  80.5 33.7 %mixer_forward.3 = (bf16[2,1024,768]{2,1,0:T(8,128)(2,1)}, bf16[2,1024,768]{2,1,0:T(8,128)(2,1)}, bf16[2,1024,768]{2,1,0:T(8,128)(2,1)}, bf16[2,1024,768]{2,1,0:...) custom-call(s32[2]{0:T(128)} %dynamic_slice.30.split_ref, ...), custom_call_target="tpu_custom_call", output_to_operand_aliasing={{0}: (19, {}), {1}: (20, {}), {2}: (21, {}), {3}: (22, {}),... | custom-call | flops 9663676416 | bytes 15728640 | tf_op jit(solution)/shard_map/mixer_forward/pallas_call | solution.py:270
  114.2 4.9 %copy.71 = bf16[2048,768]{0,1:T(8,128)(2,1)} copy(bf16[2048,768]{1,0:T(8,128)(2,1)} %bitcast.47) | data formatting | bytes 6291456 | tf_op jit(solution)/shard_map/reshape | solution.py:794
  121.0 3.3 copy.61.ogt_ref
  124.3 39.7 %ffn_both.2 = (f32[2048,768]{1,0:T(8,128)}, f32[2048,768]{1,0:T(8,128)}, bf16[3,768,1024]{2,1,0:T(8,128)(2,1)}) custom-call(bf16[2048,768]{1,0:T(8,128)(2,1)} %bitcast.48, bf16[2048,768]{1,0:T(8,128)(2,1)} %bitcast.43, bf16[768,2048]{1,0:T(8,128)(2,1)} %bitcast.52, bf16[768,2048]{1,0:T(8,128)(2,1)} %copy.61.ogt_ref, bf16[768,6144]{1,0:T(8,128)(2,1)} %wu_ref.3, ...), custom_call_target="tpu_custom_call" | custom-call | flops 28991029248 | bytes 47185920 | tf_op jit(solution)/shard_map/ffn_both/pallas_call | solution.py:381
  164.1 71.2 %ffn_both.3 = (f32[2048,768]{1,0:T(8,128)}, f32[2048,768]{1,0:T(8,128)}, bf16[3,768,2048]{2,1,0:T(8,128)(2,1)}) custom-call(bf16[2048,768]{1,0:T(8,128)(2,1)} %bitcast.49, bf16[2048,768]{1,0:T(8,128)(2,1)} %bitcast.44, bf16[768,2048]{1,0:T(8,128)(2,1)} %bitcast.53, bf16[768,2048]{1,0:T(8,128)(2,1)} %copy.61.ogt_ref, bf16[768,6144]{1,0:T(8,128)(2,1)} %wu_ref.3, ...), custom_call_target="tpu_custom_call" | custom-call | flops 57982058496 | bytes 56623104 | tf_op jit(solution)/shard_map/ffn_both/pallas_call | solution.py:381
  235.3 19.1 %norm_back.1 = (bf16[2048,768]{1,0:T(8,128)(2,1)}, f32[2048,768]{1,0:T(8,128)}, bf16[2048,768]{1,0:T(8,128)(2,1)}, f32[8,768]{1,0:T(8,128)}) custom-call(f32[2048,768]{1,0:T(8,128)} %bitcast.46, f32[2048,768]{1,0:T(8,128)} %get-tuple-element.65.refs_0_, f32[2048,768]{1,0:T(8,128)} %get-tuple-element.66.refs_1_, f32[2048,768]{1,0:T(8,128)} %get-tuple-element.67.refs_2_, ...), custom_call_target="tpu_custom_call" | custom-call | flops 31457280 | bytes 34603008 | tf_op jit(solution)/shard_map/norm_back/pallas_call | solution.py:432
  254.5 1.8 copy-done.10
  256.3 5.6 %convolution_convert_fusion = bf16[768,768]{0,1:T(8,128)(2,1)} fusion(bf16[2048,768]{1,0:T(8,128)(2,1)S(1)} %bitcast.50, bf16[2048,768]{1,0:T(8,128)(2,1)} %get-tuple-element.74), kind=kOutput, calls=%fused_computation.12 | convolution fusion | flops 2416508928 | bytes 7471104 | tf_op jit(solution)/shard_map/dot_general | solution.py:659
  261.9 2.4 copy.68
  264.3 2.8 constant_dynamic-slice_fusion
  267.1 2.0 collective-permute-start.4
  269.1 75.8 %mixer_backward.1 = (bf16[2,1024,2304]{2,1,0:T(8,128)(2,1)}, f32[12,8,768]{2,1,0:T(8,128)}) custom-call(s32[2]{0:T(128)} %dynamic_slice.30.split_ref, s32[2]{0:T(128)} %dynamic_slice.31.keep_ref, bf16[2,1024,768]{2,1,0:T(8,128)(2,1)} %bitcast.61, bf16[2,1024,768]{2,1,0:T(8,128)(2,1)} %get-tuple-element.75.q_ref, ...), custom_call_target="tpu_custom_call" | custom-call | flops 18522046464 | bytes 31457280 | tf_op jit(solution)/shard_map/mixer_backward/pallas_call | solution.py:592
  344.9 12.1 %bitcast_convert_fusion = bf16[768,2304]{1,0:T(8,128)(2,1)S(1)} fusion(bf16[2,1024,768]{2,1,0:T(8,128)(2,1)} %get-tuple-element.81, bf16[2,1024,2304]{2,1,0:T(8,128)(2,1)} %get-tuple-element.79), kind=kOutput, calls=%fused_computation | convolution fusion | flops 7249526784 | bytes 16121856 | tf_op jit(solution)/shard_map/dot_general | solution.py:659
  357.0 2.9 pad_maximum_fusion
  359.9 7.6 %reduce-scatter.6.cloned.1.call-done = bf16[3,48,2048]{2,1,0:T(8,128)(2,1)} async-done(((bf16[3,768,2048]{2,1,0:T(8,128)(2,1)}), bf16[3,48,2048]{2,1,0:T(8,128)(2,1)}) %reduce-scatter.6.cloned.1.call-update) | async-done | bytes 589840 | tf_op jit(solution)/shard_map/reduce_scatter | solution.py:832
  367.5 1.8 maximum_maximum_fusion
  370.9 2.0 broadcast_select_fusion.1
  372.9 1.9 pad_maximum_fusion.2
  374.8 3.1 collective-permute-done.6
  380.2 19.4 %input_back.1 = (bf16[2048,768]{1,0:T(8,128)(2,1)}, f32[8,768]{1,0:T(8,128)}) custom-call(bf16[2048,768]{1,0:T(8,128)(2,1)} %bitcast.51, f32[2048,768]{1,0:T(8,128)} %get-tuple-element.70.grad_ref, f32[1,768]{1,0:T(1,128)} %reshape.83.norm_gain_ref.gain_ref, bf16[768,2304]{1,0:T(8,128)(2,1)} %w_ref.1, bf16[2048,2304]{1,0:T(8,128)(2,1)} %bitcast.62), custom_call_target="tpu_custom_call" | custom-call | flops 7247757312 | bytes 22020096 | tf_op jit(solution)/shard_map/input_back/pallas_call | solution.py:645
  399.6 1.7 maximum_reduce_fusion.x_ref
  401.3 38.6 %exchange_sum.1 = (f32[14,768]{1,0:T(8,128)}, bf16[2,512,768]{2,1,0:T(8,128)(2,1)}) custom-call(f32[14,768]{1,0:T(8,128)} %maximum_reduce_fusion.x_ref, bf16[2,1024,768]{2,1,0:T(8,128)(2,1)} %bitcast.54), custom_call_target="tpu_custom_call" | custom-call | flops 20000000000 | tf_op jit(solution)/shard_map/exchange_sum/pallas_call | solution.py:712
  439.9 5.9 %assemble.1 = f32[4,512,768]{2,1,0:T(8,128)} custom-call(s32[1]{0:T(128)} %bitcast.10.s_ref, bf16[2,1024,768]{2,1,0:T(8,128)(2,1)} %bitcast.55, bf16[2,512,768]{2,1,0:T(8,128)(2,1)} %get-tuple-element.89.other_ref), custom_call_target="tpu_custom_call" | custom-call | tf_op jit(solution)/shard_map/assemble/pallas_call | solution.py:739
  445.8 1.7 slice_reduce_fusion
  454.4 4.8 %collective-permute-done.5 = bf16[48,3072]{1,0:T(8,128)(2,1)S(1)} collective-permute-done((bf16[48,3072]{1,0:T(8,128)(2,1)}, bf16[48,3072]{1,0:T(8,128)(2,1)S(1)}, u32[]{:S(2)}, u32[]{:S(2)}) %collective-permute-start.5) | collective-permute-done | bytes 294944 | tf_op jit(solution)/shard_map/ppermute | solution.py:755
  (123 shorter events, 38.8 us)
Async XLA Ops:
  7.2 247.3 %reduce-scatter.4.cloned.1.call-start = ((), (), s32[]{:S(2)}) async-start(), calls=%async_computation.3 | async-start | bytes 5013504 | tf_op jit(solution)/shard_map/reduce_scatter | solution.py:827
  8.0 27.1 %collective-permute-start = (s32[4]{0:T(128)S(1)}, s32[4]{0:T(128)S(1)}, u32[]{:S(2)}, u32[]{:S(2)}) collective-permute-start(s32[4]{0:T(128)S(1)} %reduce_sum.18), channel_id=1, source_target_pairs={{0,1},{1,0},{2,3},{3,2},{4,5},{5,4},{6,7},{7,6},{8,9},{9,8},{10,11... | collective-permute-start | bytes 56 | tf_op jit(solution)/shard_map/ppermute | solution.py:755
  13.2 22.7 %collective-permute-start.1 = (bf16[1,512,768]{2,1,0:T(8,128)(2,1)}, bf16[1,512,768]{2,1,0:T(8,128)(2,1)}, u32[]{:S(2)}, u32[]{:S(2)}) collective-permute-start(bf16[1,512,768]{2,1,0:T(8,128)(2,1)} %constant_dynamic-slice_fusion.3), channel_id=1, source_target_pairs={{0,1},{1,0},{2,3},{3,2},{4,5},{5,4},{6,7},{7,6},{8,9},{9,8},{10,11... | collective-permute-start | bytes 2359304 | tf_op jit(solution)/shard_map/ppermute | solution.py:755
  16.4 8.7 %copy-start.19 = (f32[768]{0:T(1024)S(1)}, f32[768]{0:T(1024)}, u32[]{:S(2)}) copy-start(f32[768]{0:T(1024)} %param.18) | copy-start | bytes 9220
  16.4 9.3 %copy-start.20 = (f32[768]{0:T(1024)S(1)}, f32[768]{0:T(1024)}, u32[]{:S(2)}) copy-start(f32[768]{0:T(1024)} %param.22) | copy-start | bytes 9220
  16.5 9.9 %copy-start.21 = (f32[768]{0:T(1024)S(1)}, f32[768]{0:T(1024)}, u32[]{:S(2)}) copy-start(f32[768]{0:T(1024)} %param.23) | copy-start | bytes 9220
  16.5 10.4 %copy-start.22 = (f32[768]{0:T(1024)S(1)}, f32[768]{0:T(1024)}, u32[]{:S(2)}) copy-start(f32[768]{0:T(1024)} %param.24) | copy-start | bytes 9220
  16.5 11.0 %copy-start.23 = (f32[768]{0:T(1024)S(1)}, f32[768]{0:T(1024)}, u32[]{:S(2)}) copy-start(f32[768]{0:T(1024)} %param.26) | copy-start | bytes 9220
  24.4 8.7 %copy-start.24 = (s32[4]{0:T(128)S(1)}, s32[4]{0:T(128)}, u32[]{:S(2)}) copy-start(s32[4]{0:T(128)} %param.16) | copy-start | bytes 52
  33.7 2.5 copy-start.11
  40.6 35.5 %collective-permute-start.2 = (bf16[1,512,768]{2,1,0:T(8,128)(2,1)}, bf16[1,512,768]{2,1,0:T(8,128)(2,1)}, u32[]{:S(2)}, u32[]{:S(2)}) collective-permute-start(bf16[1,512,768]{2,1,0:T(8,128)(2,1)} %constant_dynamic-slice_fusion.2), channel_id=1, source_target_pairs={{0,1},{1,0},{2,3},{3,2},{4,5},{5,4},{6,7},{7,6},{8,9},{9,8},{10,11... | collective-permute-start | bytes 2359304 | tf_op jit(solution)/shard_map/ppermute | solution.py:755
  76.1 3.1 copy-start.12
  77.7 2.7 copy-start.5
  77.8 2.7 copy-start.7
  80.5 38.7 %collective-permute-start.3 = (bf16[2,512,768]{2,1,0:T(8,128)(2,1)}, bf16[2,512,768]{2,1,0:T(8,128)(2,1)}, u32[]{:S(2)}, u32[]{:S(2)}) collective-permute-start(bf16[2,512,768]{2,1,0:T(8,128)(2,1)} %constant_dynamic-slice_fusion.1), channel_id=1, source_target_pairs={{0,1},{1,0},{2,3},{3,2},{4,5},{5,4},{6,7},{7,6},{8,9},{9,8},{10,11... | collective-permute-start | bytes 4718600 | tf_op jit(solution)/shard_map/ppermute | solution.py:755
  114.2 4.9 %copy-start.13 = (bf16[4,512,768]{2,1,0:T(8,128)(2,1)S(1)}, bf16[4,512,768]{2,1,0:T(8,128)(2,1)}, u32[]{:S(2)}) copy-start(bf16[4,512,768]{2,1,0:T(8,128)(2,1)} %param.29) | copy-start | bytes 9437188
  121.0 3.4 copy-start
  164.1 203.4 %reduce-scatter.6.cloned.1.call-start = ((), (), s32[]{:S(2)}) async-start(), calls=%async_computation.4 | async-start | bytes 10027008 | tf_op jit(solution)/shard_map/reduce_scatter | solution.py:832
  254.5 197.6 %reduce-scatter.8.cloned.1.call-start = ((), (), s32[]{:S(2)}) async-start(), calls=%async_computation.5 | async-start | bytes 5013504 | tf_op jit(solution)/shard_map/reduce_scatter | solution.py:837
  267.1 103.8 %collective-permute-start.4 = (bf16[2,512,768]{2,1,0:T(8,128)(2,1)}, bf16[2,512,768]{2,1,0:T(8,128)(2,1)}, u32[]{:S(2)}, u32[]{:S(2)}) collective-permute-start(bf16[2,512,768]{2,1,0:T(8,128)(2,1)} %constant_dynamic-slice_fusion), channel_id=1, source_target_pairs={{0,1},{1,0},{2,3},{3,2},{4,5},{5,4},{6,7},{7,6},{8,9},{9,8},{10,11... | collective-permute-start | bytes 4718600 | tf_op jit(solution)/shard_map/ppermute | solution.py:755
  344.9 12.1 %copy-start.9 = (bf16[768,768]{1,0:T(8,128)(2,1)S(1)}, bf16[768,768]{1,0:T(8,128)(2,1)}, u32[]{:S(2)}) copy-start(bf16[768,768]{1,0:T(8,128)(2,1)} %copy.68) | copy-start | bytes 3538948
  359.9 7.6 %copy-start.2 = (bf16[1,512,768]{2,1,0:T(8,128)(2,1)S(1)}, bf16[1,512,768]{2,1,0:T(8,128)(2,1)}, u32[]{:S(2)}) copy-start(bf16[1,512,768]{2,1,0:T(8,128)(2,1)} %copy-done.1) | copy-start | bytes 2359300
  359.9 7.6 %copy-start.4 = (bf16[1,512,768]{2,1,0:T(8,128)(2,1)S(1)}, bf16[1,512,768]{2,1,0:T(8,128)(2,1)}, u32[]{:S(2)}) copy-start(bf16[1,512,768]{2,1,0:T(8,128)(2,1)} %copy-done.3) | copy-start | bytes 2359300
  359.9 7.6 %copy-start.6 = (bf16[1,512,768]{2,1,0:T(8,128)(2,1)S(1)}, bf16[1,512,768]{2,1,0:T(8,128)(2,1)}, u32[]{:S(2)}) copy-start(bf16[1,512,768]{2,1,0:T(8,128)(2,1)} %copy-done.5) | copy-start | bytes 2359300
  359.9 7.6 %copy-start.8 = (bf16[1,512,768]{2,1,0:T(8,128)(2,1)S(1)}, bf16[1,512,768]{2,1,0:T(8,128)(2,1)}, u32[]{:S(2)}) copy-start(bf16[1,512,768]{2,1,0:T(8,128)(2,1)} %copy-done.7) | copy-start | bytes 2359300
  367.5 3.3 copy-start.14
  369.4 8.5 %collective-permute-start.6 = (bf16[3,48,1024]{2,1,0:T(8,128)(2,1)S(1)}, bf16[3,48,1024]{2,1,0:T(8,128)(2,1)S(1)}, u32[]{:S(2)}, u32[]{:S(2)}) collective-permute-start(bf16[3,48,1024]{2,1,0:T(8,128)(2,1)S(1)} %copy-done.18), channel_id=1, source_target_pairs={{0,1},{1,0},{2,3},{3,2},{4,5},{5,4},{6,7},{7,6},{8,9},{9,8},{10,11... | collective-permute-start | bytes 884744 | tf_op jit(solution)/shard_map/ppermute | solution.py:755
  378.8 70.7 %collective-permute-start.7 = (bf16[3,48,2048]{2,1,0:T(8,128)(2,1)}, bf16[3,48,2048]{2,1,0:T(8,128)(2,1)}, u32[]{:S(2)}, u32[]{:S(2)}) collective-permute-start(bf16[3,48,2048]{2,1,0:T(8,128)(2,1)} %reduce-scatter.6.cloned.1.call-done), channel_id=1, source_target_pairs={{0,1},{1,0},{2,3},{3,2},{4,5},{5,4},{6,7},{7,6},{8,9},{9,8},{10,11... | collective-permute-start | bytes 1769480 | tf_op jit(solution)/shard_map/ppermute | solution.py:755
  445.8 5.2 %copy-start.16 = (f32[48,1024]{1,0:T(8,128)S(1)}, f32[48,1024]{1,0:T(8,128)}, u32[]{:S(2)}) copy-start(f32[48,1024]{1,0:T(8,128)} %get-tuple-element.110) | copy-start | bytes 589828
  445.8 5.2 %copy-start.17 = (f32[48,1024]{1,0:T(8,128)S(1)}, f32[48,1024]{1,0:T(8,128)}, u32[]{:S(2)}) copy-start(f32[48,1024]{1,0:T(8,128)} %get-tuple-element.111) | copy-start | bytes 589828
  449.5 4.1 copy-start.15
  452.1 7.0 %collective-permute-start.5 = (bf16[48,3072]{1,0:T(8,128)(2,1)}, bf16[48,3072]{1,0:T(8,128)(2,1)S(1)}, u32[]{:S(2)}, u32[]{:S(2)}) collective-permute-start(bf16[48,3072]{1,0:T(8,128)(2,1)} %reduce-scatter.8.cloned.1.call-done), channel_id=1, source_target_pairs={{0,1},{1,0},{2,3},{3,2},{4,5},{5,4},{6,7},{7,6},{8,9},{9,8},{10,11... | collective-permute-start | bytes 884744 | tf_op jit(solution)/shard_map/ppermute | solution.py:755
  (4 other events, 6.9 us)
Sparse Core Ops, SparseCore 0:
  164.2 77.2 reduce-scatter.3
  254.6 112.7 reduce-scatter.5
  371.3 76.3 reduce-scatter.7
